TPU v7x, 512 devices: a whole 4x4x16 slice. The times are simulated.
512 devices in a mesh: gx: 32 (over z, core), gy: 8 (over x_lo, y), vert: 2 (over x_hi).
Axes of the slice: x: 4 (x_hi: 2, x_lo: 2; x = x_hi * 2 + x_lo), y: 4, z: 16, core: 2. Of those that a mesh axis runs over, the one named last changes fastest.
Arguments:
- vectors: float32 [16, 256, 64, 128], P('vert', 'gx', 'gy'), may hold values from -6 to 6
- conductivity: float32 [256, 64, 128], P('gx', 'gy'), may hold values from 0.3 to 3
- c_points: int32 [256, 64, 16], P('gx', 'gy'), may hold values from -1 to 127, as said below
Outputs:
- interp: float32 [256, 64, 16, 128], P('gx', 'gy')
- coarse: float32 [256, 64, 9, 256], P('gx', 'gy')
Inputs may be any that keep to these rules, and one draw needn't show every extreme that they name: `c_points`: in each tile column the used slots come first, hold distinct positions in increasing order, and number at least 8; some column uses all 16 slots.
All inputs are finite; a program needn't handle non-finite values.
Results may differ from a plain program's by a relative error of at most 0.0003.
Values sent between devices are 32-bit elements; how exact they have to be, the bound alone decides.
No kernel may reach another device: no remote copies, remote signals or barrier semaphores. Data moves between devices by JAX's collectives and lax.ppermute only.
A program may use at most 64 MiB of HBM per device.

v0:
```python
import jax
import jax.numpy as jnp
from jax import lax
from jax.sharding import PartitionSpec as P

SWEEPS = 3


ANISOTROPY = (1.0, 0.6, 0.15)
OMEGA = 0.6
SHIFT = 0.5
RIDGE = 0.1


def padded_2(block, sides, width):
    for axis, dim in sides:
        count = lax.axis_size(axis)
        forward = [(i, i + 1) for i in range(count - 1)]
        backward = [(target, source) for source, target in forward]
        low = lax.ppermute(
            lax.slice_in_dim(block, block.shape[dim] - width, None, axis=dim), axis, forward
        )
        high = lax.ppermute(lax.slice_in_dim(block, 0, width, axis=dim), axis, backward)
        block = jnp.concatenate([low, block, high], axis=dim)
    return block


def joined_along(tiles, dim):
    tiles = jnp.moveaxis(tiles, 0, dim)
    dims = tiles.shape
    return tiles.reshape(*dims[:dim], dims[dim] * dims[dim + 1], *dims[dim + 2 :])


def sent_to_all(value, axis):
    length = lax.axis_size(axis)
    return lax.all_to_all(
        jnp.broadcast_to(value[None], (length, *value.shape)), axis, 0, 0, tiled=True
    )


def gathered_copies(value, axis, dim):
    return joined_along(sent_to_all(value, axis), dim)


def stencil_offsets():
    result = []
    for move_x in (-1, 0, 1):
        for move_y in (-1, 0, 1):
            for move_z in (-1, 0, 1):
                if move_x != 0 or move_y != 0 or move_z != 0:
                    result.append((move_x, move_y, move_z))
    return result


def coupling(move):
    weight = 1.0
    for axis_no in range(3):
        if move[axis_no] != 0:
            weight = weight * ANISOTROPY[axis_no]
    return weight


def window_of(move, shape):
    return tuple(
        (slice(1 + move[axis_no], 1 + move[axis_no] + shape[axis_no]) for axis_no in range(3))
    )


def pad_depth(array):
    return jnp.pad(array, [(0, 0)] * (array.ndim - 1) + [(1, 1)])


def operator_apply(padded, kpad):
    shape = (kpad.shape[0] - 2, kpad.shape[1] - 2, kpad.shape[2] - 2)
    interior = kpad[1:-1, 1:-1, 1:-1]
    centre = padded[:, 1:-1, 1:-1, 1:-1]
    diagonal = SHIFT * interior * interior
    nearby = jnp.zeros_like(centre)
    for move in stencil_offsets():
        window = window_of(move, shape)
        couple = coupling(move) * interior * kpad[window]
        diagonal = diagonal + couple
        nearby = nearby + couple * padded[(slice(None),) + window]
    return (diagonal * centre - nearby, diagonal, centre)


def jacobi(padded, kpad):
    image, diagonal, centre = operator_apply(padded, kpad)
    alive = diagonal > 0.0
    guarded = jnp.where(alive, diagonal, 1.0)
    return jnp.where(alive, centre - OMEGA * image / guarded, 0.0)


def onehot_of(c_points, depth):
    return (c_points[..., None] == jnp.arange(depth, dtype=jnp.int32)).astype(jnp.float32)


def gram_terms(field, onehot):
    cvals = jnp.einsum("vxyz,xyjz->vxyj", field, onehot, precision=lax.Precision.HIGHEST)
    right = jnp.einsum("vxyz,vxyj->xyjz", field, cvals, precision=lax.Precision.HIGHEST)
    gram = jnp.einsum("vxyi,vxyj->xyij", cvals, cvals, precision=lax.Precision.HIGHEST)
    return (right, gram)


def batched_solve(system, right):
    slots = system.shape[0]
    lower = [[None] * slots for row in range(slots)]
    for col in range(slots):
        total = system[col, col]
        for inner in range(col):
            total = total - lower[col][inner] * lower[col][inner]
        pivot = jnp.sqrt(total)
        lower[col][col] = pivot
        for row in range(col + 1, slots):
            total = system[row, col]
            for inner in range(col):
                total = total - lower[row][inner] * lower[col][inner]
            lower[row][col] = total / pivot
    forward = []
    for row in range(slots):
        total = right[row]
        for inner in range(row):
            total = total - lower[row][inner][:, None] * forward[inner]
        forward.append(total / lower[row][row][:, None])
    backward = [None] * slots
    for row in range(slots - 1, -1, -1):
        total = forward[row]
        for inner in range(row + 1, slots):
            total = total - lower[inner][row][:, None] * backward[inner]
        backward[row] = total / lower[row][row][:, None]
    return jnp.stack(backward, axis=0)


def solve_interp(right, gram, onehot):
    cols_x, cols_y, slots, depth = right.shape
    ridge = RIDGE * jnp.trace(gram, axis1=2, axis2=3) / slots + 1e-06
    system = gram + ridge[:, :, None, None] * jnp.eye(slots, dtype=jnp.float32)
    system_last = jnp.transpose(system.reshape(cols_x * cols_y, slots, slots), (1, 2, 0))
    right_last = jnp.transpose(right.reshape(cols_x * cols_y, slots, depth), (1, 0, 2))
    solved = batched_solve(system_last, right_last)
    weights = jnp.transpose(solved, (1, 0, 2)).reshape(cols_x, cols_y, slots, depth)
    c_row = jnp.sum(onehot, axis=2)
    return weights * (1.0 - c_row[:, :, None, :]) + onehot


def galerkin(interp, ppad, kpad):
    shape = (kpad.shape[0] - 2, kpad.shape[1] - 2, kpad.shape[2] - 2)
    interior = kpad[1:-1, 1:-1, 1:-1]
    diagonal = SHIFT * interior * interior
    for move in stencil_offsets():
        diagonal = diagonal + coupling(move) * interior * kpad[window_of(move, shape)]
    blocks = []
    slots = interp.shape[2]
    for move_x in (-1, 0, 1):
        for move_y in (-1, 0, 1):
            if move_x == 0 and move_y == 0:
                image = diagonal[:, :, None, :] * interp
            else:
                image = jnp.zeros_like(interp)
            for move_z in (-1, 0, 1):
                if move_x == 0 and move_y == 0 and (move_z == 0):
                    continue
                move = (move_x, move_y, move_z)
                window = window_of(move, shape)
                couple = coupling(move) * interior * kpad[window]
                source = ppad[window[0], window[1], :, window[2]]
                image = image - couple[:, :, None, :] * source
            block = jnp.einsum("xyiz,xyjz->xyij", interp, image, precision=lax.Precision.HIGHEST)
            blocks.append(block.reshape(shape[0], shape[1], slots * slots))
    return jnp.stack(blocks, axis=2)


def body(vectors, conductivity, c_points):
    field = vectors
    kfull = padded_2(conductivity, (("gx", 0), ("gy", 1)), SWEEPS)
    extended = padded_2(field, (("gx", 1), ("gy", 2)), SWEEPS)
    for turn in range(SWEEPS):
        reach = SWEEPS - turn
        kslice = kfull[
            SWEEPS - reach : kfull.shape[0] - SWEEPS + reach,
            SWEEPS - reach : kfull.shape[1] - SWEEPS + reach,
        ]
        extended = jacobi(pad_depth(extended), pad_depth(kslice))
    field = extended
    kpad = pad_depth(
        kfull[SWEEPS - 1 : kfull.shape[0] - SWEEPS + 1, SWEEPS - 1 : kfull.shape[1] - SWEEPS + 1]
    )
    onehot = onehot_of(c_points, field.shape[-1])
    whole = gathered_copies(field, "vert", 0)
    right, gram = gram_terms(whole, onehot)
    interp = solve_interp(right, gram, onehot)
    prim = padded_2(interp, (("gx", 0), ("gy", 1)), 1)
    coarse = galerkin(interp, pad_depth(prim), kpad)
    return (interp, coarse)


def solution(mesh):
    placed = (P("vert", "gx", "gy", None), P("gx", "gy", None), P("gx", "gy", None))
    return jax.shard_map(
        body,
        mesh=mesh,
        in_specs=placed,
        out_specs=(P("gx", "gy", None, None), P("gx", "gy", None, None)),
        check_vma=False,
    )
```

profile of v0, /device:TPU:217, one launch (start us, length us, event | category | flops | bytes accessed | tf_op | source)
XLA Modules:
  0.0 118.0 jit_solution(355159118720755528)
XLA Ops:
  0.6 0.7 fusion.1040
  1.4 2.6 %collective-permute-start.1 = (f32[3,8,128]{2,1,0:T(8,128)S(1)}, f32[3,8,128]{2,1,0:T(8,128)S(1)}, u32[]{:S(2)}, u32[]{:S(2)}) collective-permute-start(f32[3,8,128]{2,1,0:T(8,128)S(1)} %get-tuple-element.470), channel_id=1, source_target_pairs={{16,0},{32,16},{48,32},{64,48},{80,64},{96,80},{112,96},{128,112},... | collective-permute-start | bytes 36872 | tf_op jit(solution)/shard_map/ppermute | solution.py:23
  3.9 3.4 %collective-permute-start = (f32[3,8,128]{2,1,0:T(8,128)S(1)}, f32[3,8,128]{2,1,0:T(8,128)S(1)}, u32[]{:S(2)}, u32[]{:S(2)}) collective-permute-start(f32[3,8,128]{2,1,0:T(8,128)S(1)} %get-tuple-element.471), channel_id=1, source_target_pairs={{0,16},{16,32},{32,48},{48,64},{64,80},{80,96},{96,112},{112,128},... | collective-permute-start | bytes 36872 | tf_op jit(solution)/shard_map/ppermute | solution.py:20
  7.4 1.0 fusion.1037
  8.4 1.9 %collective-permute-start.5 = (f32[8,3,8,128]{3,2,1,0:T(8,128)S(1)}, f32[8,3,8,128]{3,2,1,0:T(8,128)S(1)}, u32[]{:S(2)}, u32[]{:S(2)}) collective-permute-start(f32[8,3,8,128]{3,2,1,0:T(8,128)S(1)} %get-tuple-element.351), channel_id=1, source_target_pairs={{16,0},{32,16},{48,32},{64,48},{80,64},{96,80},{112,96},{128,112},... | collective-permute-start | bytes 294920 | tf_op jit(solution)/shard_map/ppermute | solution.py:23
  10.3 3.6 %collective-permute-start.4 = (f32[8,3,8,128]{3,2,1,0:T(8,128)S(1)}, f32[8,3,8,128]{3,2,1,0:T(8,128)S(1)}, u32[]{:S(2)}, u32[]{:S(2)}) collective-permute-start(f32[8,3,8,128]{3,2,1,0:T(8,128)S(1)} %get-tuple-element.352), channel_id=1, source_target_pairs={{0,16},{16,32},{32,48},{48,64},{64,80},{80,96},{96,112},{112,128},... | collective-permute-start | bytes 294920 | tf_op jit(solution)/shard_map/ppermute | solution.py:20
  13.9 1.0 convert_reduce_fusion
  15.0 0.9 fusion.405
  15.9 2.8 %collective-permute-start.2 = (f32[14,3,128]{2,1,0:T(4,128)S(1)}, f32[14,3,128]{2,1,0:T(4,128)S(1)}, u32[]{:S(2)}, u32[]{:S(2)}) collective-permute-start(f32[14,3,128]{2,1,0:T(4,128)S(1)} %get-tuple-element.465), channel_id=1, source_target_pairs={{0,2},{2,4},{4,6},{6,8},{8,10},{10,12},{12,14},{1,3},{3,5},{5,7},{... | collective-permute-start | bytes 64520 | tf_op jit(solution)/shard_map/ppermute | solution.py:20
  18.7 2.5 %collective-permute-start.3 = (f32[14,3,128]{2,1,0:T(4,128)S(1)}, f32[14,3,128]{2,1,0:T(4,128)S(1)}, u32[]{:S(2)}, u32[]{:S(2)}) collective-permute-start(f32[14,3,128]{2,1,0:T(4,128)S(1)} %get-tuple-element.466), channel_id=1, source_target_pairs={{2,0},{4,2},{6,4},{8,6},{10,8},{12,10},{14,12},{3,1},{5,3},{7,5},{... | collective-permute-start | bytes 64520 | tf_op jit(solution)/shard_map/ppermute | solution.py:23
  21.2 4.2 %collective-permute-done.3 = f32[14,3,128]{2,1,0:T(4,128)S(1)} collective-permute-done((f32[14,3,128]{2,1,0:T(4,128)S(1)}, f32[14,3,128]{2,1,0:T(4,128)S(1)}, u32[]{:S(2)}, u32[]{:S(2)}) %collective-permute-start.3) | collective-permute-done | bytes 21536 | tf_op jit(solution)/shard_map/ppermute | solution.py:23
  25.4 0.5 fusion.295
  27.4 0.5 fusion.349
  28.5 1.9 %collective-permute-start.6 = (f32[8,14,3,128]{3,2,1,0:T(4,128)S(1)}, f32[8,14,3,128]{3,2,1,0:T(4,128)S(1)}, u32[]{:S(2)}, u32[]{:S(2)}) collective-permute-start(f32[8,14,3,128]{3,2,1,0:T(4,128)S(1)} %get-tuple-element.347), channel_id=1, source_target_pairs={{0,2},{2,4},{4,6},{6,8},{8,10},{10,12},{12,14},{1,3},{3,5},{5,7},{... | collective-permute-start | bytes 516104 | tf_op jit(solution)/shard_map/ppermute | solution.py:20
  30.4 3.4 %collective-permute-start.7 = (f32[8,14,3,128]{3,2,1,0:T(4,128)S(1)}, f32[8,14,3,128]{3,2,1,0:T(4,128)S(1)}, u32[]{:S(2)}, u32[]{:S(2)}) collective-permute-start(f32[8,14,3,128]{3,2,1,0:T(4,128)S(1)} %get-tuple-element.348), channel_id=1, source_target_pairs={{2,0},{4,2},{6,4},{8,6},{10,8},{12,10},{14,12},{3,1},{5,3},{7,5},{... | collective-permute-start | bytes 516104 | tf_op jit(solution)/shard_map/ppermute | solution.py:23
  33.8 3.5 %collective-permute-done.6 = f32[8,14,3,128]{3,2,1,0:T(4,128)S(1)} collective-permute-done((f32[8,14,3,128]{3,2,1,0:T(4,128)S(1)}, f32[8,14,3,128]{3,2,1,0:T(4,128)S(1)}, u32[]{:S(2)}, u32[]{:S(2)}) %collective-permute-start.6) | collective-permute-done | bytes 172064 | tf_op jit(solution)/shard_map/ppermute | solution.py:20
  37.4 4.0 %collective-permute-done.7 = f32[8,14,3,128]{3,2,1,0:T(4,128)S(1)} collective-permute-done((f32[8,14,3,128]{3,2,1,0:T(4,128)S(1)}, f32[8,14,3,128]{3,2,1,0:T(4,128)S(1)}, u32[]{:S(2)}, u32[]{:S(2)}) %collective-permute-start.7) | collective-permute-done | bytes 172064 | tf_op jit(solution)/shard_map/ppermute | solution.py:23
  41.6 3.9 %fusion.48 = f32[8,12,12,128]{3,2,1,0:T(8,128)S(1)} fusion(f32[8,14,14,128]{3,2,1,0:T(8,128)S(1)} %pad_maximum_fusion, f32[12,12,128]{2,1,0:T(8,128)S(1)} %get-tuple-element.536, f32[12,12,128]{2,1,0:T(8,128)S(1)} %get-tuple-element.340, f32[12,12,128]{2,1,0:T(8,128)S(1)} %get-tuple-element.338, f32[12,12,128]{2,1,0:T(8,128)S(1)} %get-tuple-element.455, ...), kind=kLoop, calls=%fused_computation.154 | loop fusion | flops 8404992 | bytes 11362304 | tf_op jit(solution)/shard_map/jit(_where)/select_n | solution.py:91
  45.5 3.3 %fusion.96 = f32[8,10,10,128]{3,2,1,0:T(8,128)S(1)} fusion(f32[8,12,12,128]{3,2,1,0:T(8,128)S(1)} %fusion.48, f32[10,10,128]{2,1,0:T(8,128)S(1)} %get-tuple-element.354, f32[10,10,128]{2,1,0:T(8,128)S(1)} %get-tuple-element.336, f32[10,10,128]{2,1,0:T(8,128)S(1)} %get-tuple-element.329, f32[10,10,128]{2,1,0:T(8,128)S(1)} %get-tuple-element.365, ...), kind=kLoop, calls=%fused_computation.232 | loop fusion | flops 5836800 | bytes 9408512 | tf_op jit(solution)/shard_map/jit(_where)/select_n | solution.py:91
  48.9 1.3 %fusion.251 = f32[8,8,8,128]{3,2,1,0:T(8,128)S(1)} fusion(f32[8,10,10,128]{3,2,1,0:T(8,128)S(1)} %fusion.96, f32[8,8,128]{2,1,0:T(8,128)S(1)} %get-tuple-element.464, f32[8,8,128]{2,1,0:T(8,128)S(1)} %get-tuple-element.327, f32[8,8,128]{2,1,0:T(8,128)S(1)} %get-tuple-element.320, f32[8,8,128]{2,1,0:T(8,128)S(1)} %get-tuple-element.428, ...), kind=kLoop, calls=%fused_computation.400 | loop fusion | flops 3735552 | bytes 4202496 | tf_op jit(solution)/shard_map/jit(_where)/select_n | solution.py:91
  50.4 0.8 broadcast_in_dim.48
  51.3 3.7 %all-to-all-start = ((f32[2,8,8,8,128]{4,1,3,2,0:T(8,128)}), f32[2,8,8,8,128]{4,1,3,2,0:T(8,128)S(1)}, u32[]{:S(2)}, u32[]{:S(2)}) async-start(f32[2,8,8,8,128]{4,1,3,2,0:T(8,128)} %broadcast_in_dim.48), calls=%async_computation | async-start | bytes 1048576 | tf_op jit(solution)/shard_map/all_to_all | solution.py:36
  55.0 8.2 %all-to-all-done = f32[2,8,8,8,128]{4,1,3,2,0:T(8,128)S(1)} async-done(((f32[2,8,8,8,128]{4,1,3,2,0:T(8,128)}), f32[2,8,8,8,128]{4,1,3,2,0:T(8,128)S(1)}, u32[]{:S(2)}, u32[]{:S(2)}) %all-to-all-start) | async-done | bytes 524320 | tf_op jit(solution)/shard_map/all_to_all | solution.py:36
  63.2 0.6 convolution_bitcast_fusion
  63.8 1.1 select_reduce_fusion
  65.4 0.7 fusion.162
  68.1 2.4 %subtract_divide_fusion.26 = (f32[64,128]{1,0:T(8,128)S(1)}, f32[64,128]{1,0:T(8,128)S(1)}, f32[64,128]{1,0:T(8,128)S(1)}, f32[64,128]{1,0:T(8,128)S(1)}, f32[64...) fusion(f32[16,64,128]{2,1,0:T(8,128)S(1)} %bitcast.1924, ...), kind=kLoop, calls=%fused_computation.793 | loop fusion | flops 3932160 | bytes 886784 | tf_op jit(solution)/shard_map/div | solution.py:130
  70.6 1.4 %constant_dynamic-update-slice_fusion.21 = f32[16,64,128]{2,1,0:T(8,128)S(1)} fusion(f32[64,128]{1,0:T(8,128)S(1)} %get-tuple-element.21, f32[64,128]{1,0:T(8,128)S(1)} %get-tuple-element.20, f32[64,128]{1,0:T(8,128)S(1)} %get-tuple-element.19, f32[64,128]{1,0:T(8,128)S(1)} %get-tuple-element.18, f32[64,128]{1,0:T(8,128)S(1)} %get-tuple-element.25, ...), kind=kLoop, calls=%fused_computation.560 | loop fusion | flops 2473983 | bytes 652800
  72.0 2.4 %constant_dynamic-update-slice_fusion.18 = (f32[16,64,128]{2,1,0:T(8,128)S(1)}, f32[1,64,128]{2,1,0:T(8,128)S(1)}, f32[1,64,128]{2,1,0:T(8,128)S(1)}, f32[1,64,1...) fusion(f32[16,64,128]{2,1,0:T(8,128)S(1)} %constant_dynamic-upd, ...), kind=kLoop, calls=%fused_computation.557 | loop fusion | flops 3350528 | bytes 1015808
  75.0 0.4 convert_add_fusion
  75.4 7.9 %collective-permute-start.8 = (f32[1,8,16,128]{3,2,1,0:T(8,128)S(1)}, f32[1,8,16,128]{3,2,1,0:T(8,128)S(1)}, u32[]{:S(2)}, u32[]{:S(2)}) collective-permute-start(f32[1,8,16,128]{3,2,1,0:T(8,128)S(1)} %get-tuple-element.345), channel_id=1, source_target_pairs={{0,16},{16,32},{32,48},{48,64},{64,80},{80,96},{96,112},{112,128},... | collective-permute-start | bytes 196616 | tf_op jit(solution)/shard_map/ppermute | solution.py:20
  83.3 1.9 %collective-permute-start.9 = (f32[1,8,16,128]{3,2,1,0:T(8,128)S(1)}, f32[1,8,16,128]{3,2,1,0:T(8,128)S(1)}, u32[]{:S(2)}, u32[]{:S(2)}) collective-permute-start(f32[1,8,16,128]{3,2,1,0:T(8,128)S(1)} %get-tuple-element.346), channel_id=1, source_target_pairs={{16,0},{32,16},{48,32},{64,48},{80,64},{96,80},{112,96},{128,112},... | collective-permute-start | bytes 196616 | tf_op jit(solution)/shard_map/ppermute | solution.py:23
  85.3 3.6 %collective-permute-done.9 = f32[1,8,16,128]{3,2,1,0:T(8,128)S(1)} collective-permute-done((f32[1,8,16,128]{3,2,1,0:T(8,128)S(1)}, f32[1,8,16,128]{3,2,1,0:T(8,128)S(1)}, u32[]{:S(2)}, u32[]{:S(2)}) %collective-permute-start.9) | collective-permute-done | bytes 65568 | tf_op jit(solution)/shard_map/ppermute | solution.py:23
  88.9 1.9 %collective-permute-start.10 = (f32[10,1,16,128]{3,2,1,0:T(8,128)S(1)}, f32[10,1,16,128]{3,2,1,0:T(8,128)S(1)}, u32[]{:S(2)}, u32[]{:S(2)}) collective-permute-start(f32[10,1,16,128]{3,2,1,0:T(8,128)S(1)} %get-tuple-element.343), channel_id=1, source_target_pairs={{0,2},{2,4},{4,6},{6,8},{8,10},{10,12},{12,14},{1,3},{3,5},{5,7},{... | collective-permute-start | bytes 245768 | tf_op jit(solution)/shard_map/ppermute | solution.py:20
  90.8 3.6 %collective-permute-start.11 = (f32[10,1,16,128]{3,2,1,0:T(8,128)S(1)}, f32[10,1,16,128]{3,2,1,0:T(8,128)S(1)}, u32[]{:S(2)}, u32[]{:S(2)}) collective-permute-start(f32[10,1,16,128]{3,2,1,0:T(8,128)S(1)} %get-tuple-element.344), channel_id=1, source_target_pairs={{2,0},{4,2},{6,4},{8,6},{10,8},{12,10},{14,12},{3,1},{5,3},{7,5},{... | collective-permute-start | bytes 245768 | tf_op jit(solution)/shard_map/ppermute | solution.py:23
  94.4 3.7 %collective-permute-done.11 = f32[10,1,16,128]{3,2,1,0:T(8,128)S(1)} collective-permute-done((f32[10,1,16,128]{3,2,1,0:T(8,128)S(1)}, f32[10,1,16,128]{3,2,1,0:T(8,128)S(1)}, u32[]{:S(2)}, u32[]{:S(2)}) %collective-permute-start.11) | collective-permute-done | bytes 81952 | tf_op jit(solution)/shard_map/ppermute | solution.py:23
  98.3 0.5 select_maximum_fusion
  99.0 1.1 fusion.121
  100.1 1.9 %fusion.140 = f32[8,8,16,16]{3,2,1,0:T(8,128)} fusion(f32[8,8,16,128]{3,2,1,0:T(8,128)S(1)} %convert_add_fusion, f32[10,10,16,130]{3,2,1,0:T(8,128)S(1)} %select_maximum_fusion, f32[10,9,16,128]{3,2,1,0:T(8,128)S(1)} %get-tuple-element.341, f32[8,8,128]{2,1,0:T(8,128)S(1)} %get-tuple-element.433, f32[8,8,128]{2,1,0:T(8,128)S(1)} %get-tuple-element.323, ...), kind=kOutput, calls=%fused_computation.277 | convolution fusion | flops 25952256 | bytes 2260992 | tf_op jit(solution)/shard_map/xyiz,xyjz->xyij/dot_general | solution.py:168
  102.0 1.9 %fusion.98 = f32[8,8,16,16]{3,2,1,0:T(8,128)} fusion(f32[8,8,16,128]{3,2,1,0:T(8,128)S(1)} %convert_add_fusion, f32[10,10,16,130]{3,2,1,0:T(8,128)S(1)} %select_maximum_fusion, f32[10,9,16,128]{3,2,1,0:T(8,128)S(1)} %get-tuple-element.341, f32[8,8,128]{2,1,0:T(8,128)S(1)} %get-tuple-element.327, f32[8,8,128]{2,1,0:T(8,128)S(1)} %get-tuple-element.320, ...), kind=kOutput, calls=%fused_computation.235 | convolution fusion | flops 25952256 | bytes 2260992 | tf_op jit(solution)/shard_map/xyiz,xyjz->xyij/dot_general | solution.py:168
  103.9 1.9 %fusion.133 = f32[8,8,16,16]{3,2,1,0:T(8,128)} fusion(f32[8,8,16,128]{3,2,1,0:T(8,128)S(1)} %convert_add_fusion, f32[10,10,16,130]{3,2,1,0:T(8,128)S(1)} %select_maximum_fusion, f32[10,9,16,128]{3,2,1,0:T(8,128)S(1)} %get-tuple-element.342, f32[8,8,128]{2,1,0:T(8,128)S(1)} %get-tuple-element.429, f32[8,8,128]{2,1,0:T(8,128)S(1)} %get-tuple-element.324, ...), kind=kOutput, calls=%fused_computation.270 | convolution fusion | flops 25952256 | bytes 2260992 | tf_op jit(solution)/shard_map/xyiz,xyjz->xyij/dot_general | solution.py:168
  105.8 1.9 %fusion.114 = f32[8,8,16,16]{3,2,1,0:T(8,128)} fusion(f32[8,8,16,128]{3,2,1,0:T(8,128)S(1)} %convert_add_fusion, f32[10,10,16,130]{3,2,1,0:T(8,128)S(1)} %select_maximum_fusion, f32[10,9,16,128]{3,2,1,0:T(8,128)S(1)} %get-tuple-element.342, f32[8,8,128]{2,1,0:T(8,128)S(1)} %get-tuple-element.425, f32[8,8,128]{2,1,0:T(8,128)S(1)} %get-tuple-element.326, ...), kind=kOutput, calls=%fused_computation.251 | convolution fusion | flops 25952256 | bytes 2260992 | tf_op jit(solution)/shard_map/xyiz,xyjz->xyij/dot_general | solution.py:168
  107.6 1.9 %fusion.156 = f32[8,8,16,16]{3,2,1,0:T(8,128)} fusion(f32[8,8,16,128]{3,2,1,0:T(8,128)S(1)} %convert_add_fusion, f32[10,10,16,130]{3,2,1,0:T(8,128)S(1)} %select_maximum_fusion, f32[10,9,16,128]{3,2,1,0:T(8,128)S(1)} %get-tuple-element.342, f32[8,8,128]{2,1,0:T(8,128)S(1)} %get-tuple-element.435, f32[8,8,128]{2,1,0:T(8,128)S(1)} %get-tuple-element.322, ...), kind=kOutput, calls=%fused_computation.293 | convolution fusion | flops 25952256 | bytes 2260992 | tf_op jit(solution)/shard_map/xyiz,xyjz->xyij/dot_general | solution.py:168
  109.5 1.9 %fusion.128 = f32[8,8,16,16]{3,2,1,0:T(8,128)} fusion(f32[8,8,16,128]{3,2,1,0:T(8,128)S(1)} %convert_add_fusion, f32[10,10,16,130]{3,2,1,0:T(8,128)S(1)} %select_maximum_fusion, f32[8,8,128]{2,1,0:T(8,128)S(1)} %get-tuple-element.421, f32[8,8,128]{2,1,0:T(8,128)S(1)} %get-tuple-element.420, f32[8,8,128]{2,1,0:T(8,128)S(1)} %get-tuple-element.463), kind=kOutput, calls=%fused_computation.265 | convolution fusion | flops 25821184 | bytes 2260992 | tf_op jit(solution)/shard_map/xyiz,xyjz->xyij/dot_general | solution.py:168
  111.5 1.1 fusion.147
  112.8 1.1 fusion.105
  114.2 1.4 %stack_reshape.30 = f32[8,8,1,256]{3,1,0,2:T(8,128)S(1)} reshape(f32[8,8,16,16]{3,2,1,0:T(8,128)} %fusion.133) | data formatting | bytes 131072 | tf_op jit(solution)/shard_map/stack;reshape | solution.py:170
  117.2 0.8 copy-done.25
  (159 shorter events, 7.6 us)
Async XLA Ops:
  1.4 13.6 %collective-permute-start.1 = (f32[3,8,128]{2,1,0:T(8,128)S(1)}, f32[3,8,128]{2,1,0:T(8,128)S(1)}, u32[]{:S(2)}, u32[]{:S(2)}) collective-permute-start(f32[3,8,128]{2,1,0:T(8,128)S(1)} %get-tuple-element.470), channel_id=1, source_target_pairs={{16,0},{32,16},{48,32},{64,48},{80,64},{96,80},{112,96},{128,112},... | collective-permute-start | bytes 36872 | tf_op jit(solution)/shard_map/ppermute | solution.py:23
  3.9 11.0 %collective-permute-start = (f32[3,8,128]{2,1,0:T(8,128)S(1)}, f32[3,8,128]{2,1,0:T(8,128)S(1)}, u32[]{:S(2)}, u32[]{:S(2)}) collective-permute-start(f32[3,8,128]{2,1,0:T(8,128)S(1)} %get-tuple-element.471), channel_id=1, source_target_pairs={{0,16},{16,32},{32,48},{48,64},{64,80},{80,96},{96,112},{112,128},... | collective-permute-start | bytes 36872 | tf_op jit(solution)/shard_map/ppermute | solution.py:20
  8.4 20.1 %collective-permute-start.5 = (f32[8,3,8,128]{3,2,1,0:T(8,128)S(1)}, f32[8,3,8,128]{3,2,1,0:T(8,128)S(1)}, u32[]{:S(2)}, u32[]{:S(2)}) collective-permute-start(f32[8,3,8,128]{3,2,1,0:T(8,128)S(1)} %get-tuple-element.351), channel_id=1, source_target_pairs={{16,0},{32,16},{48,32},{64,48},{80,64},{96,80},{112,96},{128,112},... | collective-permute-start | bytes 294920 | tf_op jit(solution)/shard_map/ppermute | solution.py:23
  10.3 17.9 %collective-permute-start.4 = (f32[8,3,8,128]{3,2,1,0:T(8,128)S(1)}, f32[8,3,8,128]{3,2,1,0:T(8,128)S(1)}, u32[]{:S(2)}, u32[]{:S(2)}) collective-permute-start(f32[8,3,8,128]{3,2,1,0:T(8,128)S(1)} %get-tuple-element.352), channel_id=1, source_target_pairs={{0,16},{16,32},{32,48},{48,64},{64,80},{80,96},{96,112},{112,128},... | collective-permute-start | bytes 294920 | tf_op jit(solution)/shard_map/ppermute | solution.py:20
  15.8 33.0 %copy-start.12 = (f32[8,8,128]{2,1,0:T(8,128)}, f32[8,8,128]{2,1,0:T(8,128)S(1)}, u32[]{:S(2)}) copy-start(f32[8,8,128]{2,1,0:T(8,128)S(1)} %get-tuple-element.469) | copy-start | bytes 98308
  15.8 33.0 %copy-start.14 = (f32[8,8,128]{2,1,0:T(8,128)}, f32[8,8,128]{2,1,0:T(8,128)S(1)}, u32[]{:S(2)}) copy-start(f32[8,8,128]{2,1,0:T(8,128)S(1)} %get-tuple-element.467) | copy-start | bytes 98308
  15.9 5.3 %collective-permute-start.2 = (f32[14,3,128]{2,1,0:T(4,128)S(1)}, f32[14,3,128]{2,1,0:T(4,128)S(1)}, u32[]{:S(2)}, u32[]{:S(2)}) collective-permute-start(f32[14,3,128]{2,1,0:T(4,128)S(1)} %get-tuple-element.465), channel_id=1, source_target_pairs={{0,2},{2,4},{4,6},{6,8},{8,10},{10,12},{12,14},{1,3},{3,5},{5,7},{... | collective-permute-start | bytes 64520 | tf_op jit(solution)/shard_map/ppermute | solution.py:20
  18.7 6.7 %collective-permute-start.3 = (f32[14,3,128]{2,1,0:T(4,128)S(1)}, f32[14,3,128]{2,1,0:T(4,128)S(1)}, u32[]{:S(2)}, u32[]{:S(2)}) collective-permute-start(f32[14,3,128]{2,1,0:T(4,128)S(1)} %get-tuple-element.466), channel_id=1, source_target_pairs={{2,0},{4,2},{6,4},{8,6},{10,8},{12,10},{14,12},{3,1},{5,3},{7,5},{... | collective-permute-start | bytes 64520 | tf_op jit(solution)/shard_map/ppermute | solution.py:23
  26.2 0.8 copy-start.7
  27.3 21.6 %copy-start.8 = (f32[8,8,128]{2,1,0:T(8,128)}, f32[8,8,128]{2,1,0:T(8,128)S(1)}, u32[]{:S(2)}) copy-start(f32[8,8,128]{2,1,0:T(8,128)S(1)} %get-tuple-element.422) | copy-start | bytes 98308
  27.3 21.6 %copy-start.10 = (f32[8,8,128]{2,1,0:T(8,128)}, f32[8,8,128]{2,1,0:T(8,128)S(1)}, u32[]{:S(2)}) copy-start(f32[8,8,128]{2,1,0:T(8,128)S(1)} %get-tuple-element.423) | copy-start | bytes 98308
  27.3 21.6 %copy-start.16 = (f32[8,8,128]{2,1,0:T(8,128)}, f32[8,8,128]{2,1,0:T(8,128)S(1)}, u32[]{:S(2)}) copy-start(f32[8,8,128]{2,1,0:T(8,128)S(1)} %get-tuple-element.426) | copy-start | bytes 98308
  27.3 21.6 %copy-start.18 = (f32[8,8,128]{2,1,0:T(8,128)}, f32[8,8,128]{2,1,0:T(8,128)S(1)}, u32[]{:S(2)}) copy-start(f32[8,8,128]{2,1,0:T(8,128)S(1)} %get-tuple-element.427) | copy-start | bytes 98308
  27.3 21.6 %copy-start.20 = (f32[8,8,128]{2,1,0:T(8,128)}, f32[8,8,128]{2,1,0:T(8,128)S(1)}, u32[]{:S(2)}) copy-start(f32[8,8,128]{2,1,0:T(8,128)S(1)} %get-tuple-element.430) | copy-start | bytes 98308
  27.3 21.6 %copy-start.22 = (f32[8,8,128]{2,1,0:T(8,128)}, f32[8,8,128]{2,1,0:T(8,128)S(1)}, u32[]{:S(2)}) copy-start(f32[8,8,128]{2,1,0:T(8,128)S(1)} %get-tuple-element.431) | copy-start | bytes 98308
  27.4 1.0 copy-start.6
  28.5 8.8 %collective-permute-start.6 = (f32[8,14,3,128]{3,2,1,0:T(4,128)S(1)}, f32[8,14,3,128]{3,2,1,0:T(4,128)S(1)}, u32[]{:S(2)}, u32[]{:S(2)}) collective-permute-start(f32[8,14,3,128]{3,2,1,0:T(4,128)S(1)} %get-tuple-element.347), channel_id=1, source_target_pairs={{0,2},{2,4},{4,6},{6,8},{8,10},{10,12},{12,14},{1,3},{3,5},{5,7},{... | collective-permute-start | bytes 516104 | tf_op jit(solution)/shard_map/ppermute | solution.py:20
  30.4 11.0 %collective-permute-start.7 = (f32[8,14,3,128]{3,2,1,0:T(4,128)S(1)}, f32[8,14,3,128]{3,2,1,0:T(4,128)S(1)}, u32[]{:S(2)}, u32[]{:S(2)}) collective-permute-start(f32[8,14,3,128]{3,2,1,0:T(4,128)S(1)} %get-tuple-element.348), channel_id=1, source_target_pairs={{2,0},{4,2},{6,4},{8,6},{10,8},{12,10},{14,12},{3,1},{5,3},{7,5},{... | collective-permute-start | bytes 516104 | tf_op jit(solution)/shard_map/ppermute | solution.py:23
  50.3 13.0 %copy-start.24 = (s32[8,8,16]{2,1,0:T(8,128)S(1)}, s32[8,8,16]{2,1,0:T(8,128)}, u32[]{:S(2)}) copy-start(s32[8,8,16]{2,1,0:T(8,128)} %param.5) | copy-start | bytes 12292
  51.3 12.0 %all-to-all-start = ((f32[2,8,8,8,128]{4,1,3,2,0:T(8,128)}), f32[2,8,8,8,128]{4,1,3,2,0:T(8,128)S(1)}, u32[]{:S(2)}, u32[]{:S(2)}) async-start(f32[2,8,8,8,128]{4,1,3,2,0:T(8,128)} %broadcast_in_dim.48), calls=%async_computation | async-start | bytes 1048576 | tf_op jit(solution)/shard_map/all_to_all | solution.py:36
  75.4 37.4 %copy-start = (f32[8,8,16,128]{3,2,1,0:T(8,128)}, f32[8,8,16,128]{3,2,1,0:T(8,128)S(1)}, u32[]{:S(2)}) copy-start(f32[8,8,16,128]{3,2,1,0:T(8,128)S(1)} %convert_add_fusion) | copy-start | bytes 1572868
  75.4 9.8 %collective-permute-start.8 = (f32[1,8,16,128]{3,2,1,0:T(8,128)S(1)}, f32[1,8,16,128]{3,2,1,0:T(8,128)S(1)}, u32[]{:S(2)}, u32[]{:S(2)}) collective-permute-start(f32[1,8,16,128]{3,2,1,0:T(8,128)S(1)} %get-tuple-element.345), channel_id=1, source_target_pairs={{0,16},{16,32},{32,48},{48,64},{64,80},{80,96},{96,112},{112,128},... | collective-permute-start | bytes 196616 | tf_op jit(solution)/shard_map/ppermute | solution.py:20
  83.3 5.6 %collective-permute-start.9 = (f32[1,8,16,128]{3,2,1,0:T(8,128)S(1)}, f32[1,8,16,128]{3,2,1,0:T(8,128)S(1)}, u32[]{:S(2)}, u32[]{:S(2)}) collective-permute-start(f32[1,8,16,128]{3,2,1,0:T(8,128)S(1)} %get-tuple-element.346), channel_id=1, source_target_pairs={{16,0},{32,16},{48,32},{64,48},{80,64},{96,80},{112,96},{128,112},... | collective-permute-start | bytes 196616 | tf_op jit(solution)/shard_map/ppermute | solution.py:23
  88.9 5.5 %collective-permute-start.10 = (f32[10,1,16,128]{3,2,1,0:T(8,128)S(1)}, f32[10,1,16,128]{3,2,1,0:T(8,128)S(1)}, u32[]{:S(2)}, u32[]{:S(2)}) collective-permute-start(f32[10,1,16,128]{3,2,1,0:T(8,128)S(1)} %get-tuple-element.343), channel_id=1, source_target_pairs={{0,2},{2,4},{4,6},{6,8},{8,10},{10,12},{12,14},{1,3},{3,5},{5,7},{... | collective-permute-start | bytes 245768 | tf_op jit(solution)/shard_map/ppermute | solution.py:20
  90.8 7.3 %collective-permute-start.11 = (f32[10,1,16,128]{3,2,1,0:T(8,128)S(1)}, f32[10,1,16,128]{3,2,1,0:T(8,128)S(1)}, u32[]{:S(2)}, u32[]{:S(2)}) collective-permute-start(f32[10,1,16,128]{3,2,1,0:T(8,128)S(1)} %get-tuple-element.344), channel_id=1, source_target_pairs={{2,0},{4,2},{6,4},{8,6},{10,8},{12,10},{14,12},{3,1},{5,3},{7,5},{... | collective-permute-start | bytes 245768 | tf_op jit(solution)/shard_map/ppermute | solution.py:23
  98.3 0.8 copy-start.9
  98.3 0.8 copy-start.11
  109.5 1.9 %copy-start.15 = (f32[8,8,128]{2,1,0:T(8,128)S(1)}, f32[8,8,128]{2,1,0:T(8,128)}, u32[]{:S(2)}) copy-start(f32[8,8,128]{2,1,0:T(8,128)} %copy-done.14) | copy-start | bytes 98308
  109.5 1.9 %copy-start.21 = (f32[8,8,128]{2,1,0:T(8,128)S(1)}, f32[8,8,128]{2,1,0:T(8,128)}, u32[]{:S(2)}) copy-start(f32[8,8,128]{2,1,0:T(8,128)} %copy-done.20) | copy-start | bytes 98308
  109.5 1.9 %copy-start.23 = (f32[8,8,128]{2,1,0:T(8,128)S(1)}, f32[8,8,128]{2,1,0:T(8,128)}, u32[]{:S(2)}) copy-start(f32[8,8,128]{2,1,0:T(8,128)} %copy-done.22) | copy-start | bytes 98308
  111.4 1.4 %copy-start.13 = (f32[8,8,128]{2,1,0:T(8,128)S(1)}, f32[8,8,128]{2,1,0:T(8,128)}, u32[]{:S(2)}) copy-start(f32[8,8,128]{2,1,0:T(8,128)} %copy-done.12) | copy-start | bytes 98308
  111.4 1.4 %copy-start.17 = (f32[8,8,128]{2,1,0:T(8,128)S(1)}, f32[8,8,128]{2,1,0:T(8,128)}, u32[]{:S(2)}) copy-start(f32[8,8,128]{2,1,0:T(8,128)} %copy-done.16) | copy-start | bytes 98308
  111.4 1.4 %copy-start.19 = (f32[8,8,128]{2,1,0:T(8,128)S(1)}, f32[8,8,128]{2,1,0:T(8,128)}, u32[]{:S(2)}) copy-start(f32[8,8,128]{2,1,0:T(8,128)} %copy-done.18) | copy-start | bytes 98308
  113.9 1.9 %copy-start.1 = (f32[8,8,16,16]{3,2,1,0:T(8,128)S(1)}, f32[8,8,16,16]{3,2,1,0:T(8,128)}, u32[]{:S(2)}) copy-start(f32[8,8,16,16]{3,2,1,0:T(8,128)} %fusion.140) | copy-start | bytes 196612
  113.9 2.2 %copy-start.2 = (f32[8,8,16,16]{3,2,1,0:T(8,128)S(1)}, f32[8,8,16,16]{3,2,1,0:T(8,128)}, u32[]{:S(2)}) copy-start(f32[8,8,16,16]{3,2,1,0:T(8,128)} %fusion.98) | copy-start | bytes 196612
  113.9 2.4 %copy-start.3 = (f32[8,8,16,16]{3,2,1,0:T(8,128)S(1)}, f32[8,8,16,16]{3,2,1,0:T(8,128)}, u32[]{:S(2)}) copy-start(f32[8,8,16,16]{3,2,1,0:T(8,128)} %fusion.114) | copy-start | bytes 196612
  114.2 2.4 %copy-start.5 = (f32[8,8,16,16]{3,2,1,0:T(8,128)S(1)}, f32[8,8,16,16]{3,2,1,0:T(8,128)}, u32[]{:S(2)}) copy-start(f32[8,8,16,16]{3,2,1,0:T(8,128)} %fusion.128) | copy-start | bytes 196612
  114.2 2.6 %copy-start.4 = (f32[8,8,16,16]{3,2,1,0:T(8,128)S(1)}, f32[8,8,16,16]{3,2,1,0:T(8,128)}, u32[]{:S(2)}) copy-start(f32[8,8,16,16]{3,2,1,0:T(8,128)} %fusion.156) | copy-start | bytes 196612
  117.2 0.8 copy-start.25
where the time goes:
time: 119 us; the launch traced here: 118 us
  starting transfers between devices  41.2 us (35%)
  waiting for transfers between devices  27.3 us (23%)
  other arithmetic  22.8 us (19%)
  matrix products  16.9 us (14%)
  local copies, waits for them, and re-layouts  8.06 us (7%)
  between operations  1.75 us (1%)
    ppermute x6, starting transfers between devices, padded_2(): lax.ppermute(lax.slice_in_dim(block, block.shape[dim] - width, None, axis...  21.6 us
    ppermute x6, starting transfers between devices, padded_2(): lax.ppermute(lax.slice_in_dim(block, 0, width, axis=dim), axis, backward)  15.9 us
    ppermute x6, waiting for transfers between devices, padded_2(): lax.ppermute(lax.slice_in_dim(block, 0, width, axis=dim), axis, backward)  15.6 us
    dot_general x9, matrix products, galerkin(): jnp.einsum('xyiz,xyjz->xyij', interp, image, precision=lax.Precision.HIGH...  14.5 us
    select_n x3, other arithmetic, jacobi(): return jnp.where(alive, centre - OMEGA * image / guarded, 0.0)  8.58 us
    all_to_all x1, waiting for transfers between devices, sent_to_all(): lax.all_to_all(jnp.broadcast_to(value[None], (length, *value.shape)), axi...  8.22 us
    unnamed x5, other arithmetic  4.28 us
    all_to_all x1, starting transfers between devices, sent_to_all(): lax.all_to_all(jnp.broadcast_to(value[None], (length, *value.shape)), axi...  3.72 us
  transfers between devices with their start and end apart: 13, of which 6 were waited for; matrix products, arithmetic and copies ran while one was open for 5% of the time, Pallas kernels for 0%

commit v1 on v0

v1 whole, which is shorter than its diff:
```python
import jax
import jax.numpy as jnp
from jax import lax
from jax.experimental import pallas as pl
from jax.experimental.pallas import tpu as pltpu
from jax.sharding import PartitionSpec as P

WY = 0.6
WZ = 0.15
OMEGA = 0.6
SHIFT = 0.5
RIDGE = 0.1
F32 = jnp.float32
BF16 = jnp.bfloat16
VMEM = pltpu.VMEM
SLAB = (37, 8, 128)


def iota(shape, dim):
    return lax.broadcasted_iota(jnp.int32, shape, dim)


def along_z(t, low, high):
    return t + low * pltpu.roll(t, 1, 1) + high * pltpu.roll(t, 127, 1)


def z_weights(rows):
    lane = iota((rows, 128), 1)
    return jnp.where(lane == 0, 0.0, WZ), jnp.where(lane == 127, 0.0, WZ)


def pack_kernel(vec, cond, points, tiles, ylow, yhigh, xlow, xhigh, padded):
    for x in range(8):
        for y in range(8):
            t = vec[pl.ds(x * 8 + y, 8, stride=64), :]
            tiles[x * 8 + y] = t
            if y < 4:
                ylow[x * 4 + y] = t
            else:
                yhigh[x * 4 + y - 4] = t
            if x < 4:
                xlow[x * 8 + y] = t
            else:
                xhigh[(x - 4) * 8 + y] = t
    padded[...] = jnp.full((64, 128), -1.0, F32)
    padded[:, 0:16] = points[...].astype(F32)
    for t in range(4):
        for half in range(2):
            x = 2 * t + half
            ylow[32 + t, half * 4 : half * 4 + 4, :] = cond[x * 8 : x * 8 + 4, :]
            yhigh[32 + t, half * 4 : half * 4 + 4, :] = cond[x * 8 + 4 : x * 8 + 8, :]
        xlow[32 + t] = cond[t * 8 : t * 8 + 8, :]
        xhigh[32 + t] = cond[t * 8 + 32 : t * 8 + 40, :]
    ylow[36] = padded[pl.ds(0, 8, stride=8), :]
    yhigh[36] = padded[pl.ds(7, 8, stride=8), :]
    xlow[36] = padded[0:8, :]
    xhigh[36] = padded[56:64, :]


def corner_kernel(ylow, yhigh, low, high):
    for out, x in ((low, 0), (high, 1)):
        out[0:16] = ylow[16 * x : 16 * x + 16]
        out[16:32] = yhigh[16 * x : 16 * x + 16]
        out[32:34] = ylow[32 + 2 * x : 34 + 2 * x]
        out[34:36] = yhigh[32 + 2 * x : 34 + 2 * x]
        out[36] = jnp.zeros((8, 128), F32)
        out[36, 0:1, :] = ylow[36, 7 * x : 7 * x + 1, :]
        out[36, 1:2, :] = yhigh[36, 7 * x : 7 * x + 1, :]


def sweep_kernel(
    tiles, cond, padded, ylow, yhigh, xlow, xhigh, clow, chigh,
    field, k_out, e_out, c_out,
    u0, u1, kk, kz, hh, h4, rk, ee,
):
    for x in range(16):
        for part, y0, n in ((0, 0, 4), (1, 4, 8), (2, 12, 4)):
            if 4 <= x < 12:
                if part == 1:
                    rows = cond[(x - 4) * 8 : (x - 4) * 8 + 8, :]
                else:
                    src = ylow if part == 0 else yhigh
                    half = (x - 4) % 2 * 4
                    rows = src[32 + (x - 4) // 2, half : half + 4, :]
            else:
                xx = x if x < 4 else x - 12
                if part == 1:
                    rows = (xlow if x < 4 else xhigh)[32 + xx]
                else:
                    src = clow if x < 4 else chigh
                    half = xx % 2 * 4
                    rows = src[32 + part + xx // 2, half : half + 4, :]
            kk[x, y0 : y0 + n, :] = rows

    low16, high16 = z_weights(16)
    for x in range(16):
        kz[x] = along_z(kk[x], low16, high16)
    for x in range(1, 15):
        k = kk[x]
        s = kz[x - 1] + kz[x] + kz[x + 1]
        s = s + WY * (pltpu.roll(s, 1, 0) + pltpu.roll(s, 15, 0)) - k
        alive = k > 0.0
        h = jnp.where(alive, OMEGA * k / jnp.where(alive, SHIFT * k + s, 1.0), 0.0)
        hh[x] = h
        h4[x] = (1.0 - OMEGA) - h
        rk[x] = jnp.where(alive, 1.0 / jnp.where(alive, k, 1.0), 0.0)
        ee[x] = (SHIFT + 1.0) * k + s

    for x in range(16):
        for y in range(16):
            inner_x, inner_y = 4 <= x < 12, 4 <= y < 12
            if inner_x and inner_y:
                t = tiles[(x - 4) * 8 + y - 4]
            elif inner_x:
                t = (ylow if y < 4 else yhigh)[(x - 4) * 4 + (y if y < 4 else y - 12)]
            else:
                xx = x if x < 4 else x - 12
                if inner_y:
                    t = (xlow if x < 4 else xhigh)[xx * 8 + y - 4]
                else:
                    src = clow if x < 4 else chigh
                    t = src[xx * 4 + (y if y < 4 else 16 + y - 12)]
            u0[x, y] = t * jnp.broadcast_to(kk[x, y : y + 1, :], (8, 128))

    low8, high8 = z_weights(8)

    def sweep(src, first, count, write):
        def step(x, carry):
            hx, h4x = hh[x], h4[x]
            s = [
                src[x - 1, y] + src[x, y] + src[x + 1, y]
                for y in range(first - 1, first + count + 1)
            ]
            for j in range(count):
                y = first + j
                t = s[j + 1] + WY * (s[j] + s[j + 2])
                w = along_z(t, low8, high8)
                a = jnp.broadcast_to(h4x[y : y + 1, :], (8, 128))
                b = jnp.broadcast_to(hx[y : y + 1, :], (8, 128))
                write(x, y, a * src[x, y] + b * w)
            return carry

        lax.fori_loop(first, first + count, step, 0)

    def to_u1(x, y, value):
        u1[x, y] = value

    def to_u0(x, y, value):
        u0[x, y] = value

    sweep(u0, 1, 14, to_u1)
    sweep(u1, 2, 12, to_u0)

    def step(x, carry):
        hx, h4x, rx = hh[x], h4[x], rk[x]
        s = [u0[x - 1, y] + u0[x, y] + u0[x + 1, y] for y in range(2, 14)]
        for j in range(10):
            y = 3 + j
            t = s[j + 1] + WY * (s[j] + s[j + 2])
            w = along_z(t, low8, high8)
            a = jnp.broadcast_to(h4x[y : y + 1, :], (8, 128))
            b = jnp.broadcast_to(hx[y : y + 1, :], (8, 128))
            r = jnp.broadcast_to(rx[y : y + 1, :], (8, 128))
            field[(x - 3) * 10 + j] = (a * u0[x, y] + b * w) * r
        return carry

    lax.fori_loop(3, 13, step, 0)

    for x in range(10):
        k_out[x * 10 : x * 10 + 10, :] = kk[x + 3, 3:13, :]
        e_out[x * 10 : x * 10 + 10, :] = ee[x + 3, 3:13, :]
        row = x * 10
        if 1 <= x < 9:
            c_out[row : row + 1, :] = ylow[36, x - 1 : x, :]
            c_out[row + 1 : row + 9, :] = padded[(x - 1) * 8 : (x - 1) * 8 + 8, :]
            c_out[row + 9 : row + 10, :] = yhigh[36, x - 1 : x, :]
        else:
            side, corner = (xlow, clow) if x == 0 else (xhigh, chigh)
            c_out[row : row + 1, :] = corner[36, 0:1, :]
            c_out[row + 1 : row + 9, :] = side[36]
            c_out[row + 9 : row + 10, :] = corner[36, 1:2, :]
    k_out[100:104, :] = jnp.zeros((4, 128), F32)
    e_out[100:104, :] = jnp.zeros((4, 128), F32)
    c_out[100:104, :] = jnp.full((4, 128), -1.0, F32)


def halves(t):
    first = t.astype(BF16)
    return first, (t - first.astype(F32)).astype(BF16)


def product(a, b):
    return lax.dot_general(a, b, (((1,), (0,)), ((), ())), preferred_element_type=F32)


def product_t(a, b):
    return lax.dot_general(a, b, (((1,), (1,)), ((), ())), preferred_element_type=F32)


def gather_lanes(t, index):
    return jnp.take_along_axis(t, index, axis=1)


def galerkin_kernel(
    vert, own, other, k10, e10, onehot, index,
    interp, coarse,
    rights, lhs_rows, r1s, r2s, e1s, e2s,
):
    first = vert[0] == 0
    lane16 = iota((16, 128), 1)
    sub16 = iota((16, 128), 0)
    lane8 = iota((8, 128), 1)
    sub8 = iota((8, 128), 0)
    block16, block8 = lane16 // 16, lane8 // 16
    lane128, sub128 = iota((128, 128), 1), iota((128, 128), 0)
    own_block = (lane128 % 64) // 8 == sub128 // 16
    ones = jnp.where(lane128 // 16 == sub128 // 16, 1.0, 0.0).astype(BF16)
    block_ones = [jnp.where(block16 == bb, 1.0, 0.0).astype(BF16) for bb in range(8)]
    on_diag = lane16 % 16 == sub16
    low128, high128 = z_weights(128)
    systems = []
    for g in range(13):
        n = 8 if g < 12 else 4
        a = own[8 * g : 8 * g + n].reshape(n * 8, 128)
        b = other[8 * g : 8 * g + n].reshape(n * 8, 128)
        fa, fb = jnp.where(first, a, b), jnp.where(first, b, a)
        if n == 8:
            f = jnp.concatenate([fa, fb], axis=0)
        else:
            none = jnp.zeros((32, 128), F32)
            f = jnp.concatenate([fa, none, fb, none], axis=0)
        f1, f2 = halves(f)
        oh = onehot[128 * g : 128 * g + 128, :]
        c1 = jnp.where(own_block, product_t(oh, f1), 0.0).astype(BF16)
        c2 = jnp.where(own_block, product_t(oh, f2), 0.0).astype(BF16)
        right = product(
            jnp.concatenate([c1, c1, c2], axis=1), jnp.concatenate([f1, f2, f1], axis=0)
        )
        rights[128 * g : 128 * g + 128, :] = right
        spots = jnp.broadcast_to(index[g : g + 1, :], (16, 128))
        wanted = jnp.maximum(spots, 0)
        gram = jnp.zeros((16, 128), F32)
        for bb in range(8):
            part = gather_lanes(right[16 * bb : 16 * bb + 16, :], wanted)
            gram = jnp.where(block16 == bb, part, gram)
        gram = jnp.where(spots >= 0, gram, 0.0)
        d = jnp.where(on_diag, gram, 0.0)
        d = d[0:8, :] + d[8:16, :]
        for shift in (4, 2, 1):
            d = d + pltpu.roll(d, shift, 0)
        for bit in (1, 2, 4, 8):
            d = d + gather_lanes(d, lane8 ^ bit)
        ridge = (RIDGE / 16) * d + 1e-06
        ridge = jnp.concatenate([ridge, ridge], axis=0)
        system = gram + jnp.where(on_diag, ridge, 0.0)
        systems.append([system[0:8, :], system[8:16, :]])

    for k in range(16):
        half, row = k // 8, k % 8
        at_k = lane8 % 16 == k
        spot = block8 * 16 + k
        for s in systems:
            pivot_row = jnp.broadcast_to(s[half][row : row + 1, :], (8, 128))
            scale = 1.0 / gather_lanes(pivot_row, spot)
            r = jnp.where(at_k, 1.0, pivot_row) * scale
            for t in range(2):
                factor = gather_lanes(s[t], spot)
                new = jnp.where(at_k, 0.0, s[t]) - factor * r
                if t == half:
                    new = jnp.where(sub8 == row, r, new)
                s[t] = new

    for g in range(13):
        m1, m2 = halves(jnp.concatenate(systems[g], axis=0))
        m1 = jnp.concatenate([m1 * block_ones[bb] for bb in range(8)], axis=0)
        m2 = jnp.concatenate([m2 * block_ones[bb] for bb in range(8)], axis=0)
        r1, r2 = halves(rights[128 * g : 128 * g + 128, :])
        w = product(
            jnp.concatenate([m1, m1, m2], axis=1), jnp.concatenate([r1, r2, r1], axis=0)
        )
        oh = onehot[128 * g : 128 * g + 128, :]
        c_row = product(ones, oh)
        p = w * (1.0 - c_row) + oh.astype(F32)
        kb = jnp.concatenate(
            [jnp.broadcast_to(k10[8 * g + bb : 8 * g + bb + 1, :], (16, 128)) for bb in range(8)],
            axis=0,
        )
        eb = jnp.concatenate(
            [jnp.broadcast_to(e10[8 * g + bb : 8 * g + bb + 1, :], (16, 128)) for bb in range(8)],
            axis=0,
        )
        left = kb * p
        image = along_z(left, low128, high128)
        centre = eb * p - image
        r1s[128 * g : 128 * g + 128, :], r2s[128 * g : 128 * g + 128, :] = halves(image)
        e1s[128 * g : 128 * g + 128, :], e2s[128 * g : 128 * g + 128, :] = halves(centre)
        for bb in range(8):
            x, y = divmod(8 * g + bb, 10)
            if 1 <= x < 9 and 1 <= y < 9:
                interp[(x - 1) * 8 + y - 1] = p[16 * bb : 16 * bb + 16, :]
                lhs_rows[x - 1, pl.ds(y - 1, 16, stride=8), :] = left[16 * bb : 16 * bb + 16, :]

    picks = [16 * ((sub8 + o) % 8) + lane8 % 16 for o in range(3)]
    for x in range(1, 9):
        l1, l2 = halves(lhs_rows[x - 1])
        lhs = jnp.concatenate([l1, l1, l2], axis=1)
        for ox in range(-1, 2):
            base = (x + ox) * 160

            def turned(ref):
                return jnp.concatenate(
                    [
                        ref[base : base + 160, :],
                        ref[base + 32 : base + 128, :],
                    ],
                    axis=0,
                )

            q1, q2 = turned(r1s), turned(r2s)
            t = product_t(lhs, jnp.concatenate([q1, q2, q1], axis=1))
            t0, t1 = t[:, 0:128], t[:, 128:256]
            if ox == 0:
                s1 = e1s[base + 16 : base + 144, :]
                s2 = e2s[base + 16 : base + 144, :]
                mid = product_t(lhs, jnp.concatenate([s1, s2, s1], axis=1))
            out = [[jnp.zeros((8, 128), F32) for half in range(2)] for oy in range(3)]
            for i in range(16):
                rows = slice(8 * i, 8 * i + 8)
                if ox == 0:
                    centre = gather_lanes(mid[rows, :], picks[0])
                else:
                    centre = gather_lanes(
                        jnp.where(block8 == 0, t1[rows, :], t0[rows, :]), picks[1]
                    )
                found = (
                    gather_lanes(t0[rows, :], picks[0]),
                    centre,
                    gather_lanes(t1[rows, :], picks[2]),
                )
                for oy in range(3):
                    out[oy][i // 8] = jnp.where(block8 == i % 8, found[oy], out[oy][i // 8])
            for oy in range(3):
                o = 3 * (ox + 1) + oy
                scale = 1.0 if o == 4 else (-1.0 if oy == 1 else -WY)
                for half in range(2):
                    coarse[x - 1, o, :, half * 128 : half * 128 + 128] = scale * out[oy][half]


def call(kernel, outs, scratch=(), specs=None, args=(), flops=0):
    shapes = [jax.ShapeDtypeStruct(*o) for o in outs]
    moved = sum(a.size * 4 for a in args) + sum(4 * s.size for s in shapes)
    return pl.pallas_call(
        kernel,
        out_shape=shapes,
        in_specs=specs or [pl.BlockSpec(memory_space=VMEM)] * len(args),
        out_specs=[pl.BlockSpec(memory_space=VMEM)] * len(outs),
        scratch_shapes=list(scratch),
        compiler_params=pltpu.CompilerParams(vmem_limit_bytes=48 << 20),
        cost_estimate=pl.CostEstimate(flops=flops, bytes_accessed=moved, transcendentals=0),
    )(*args)


def shifted(value, axis, step):
    count = lax.axis_size(axis)
    pairs = [(i, i + step) for i in range(count) if 0 <= i + step < count]
    return lax.ppermute(value, axis, pairs)


def body(vectors, conductivity, c_points):
    cond = conductivity.reshape(64, 128)
    tiles, ylow, yhigh, xlow, xhigh, padded = call(
        pack_kernel,
        [((64, 8, 128), F32)] + [(SLAB, F32)] * 4 + [((64, 128), F32)],
        args=(vectors.reshape(512, 128), cond, c_points.reshape(64, 16)),
    )
    from_ylow = shifted(yhigh, "gy", 1)
    from_yhigh = shifted(ylow, "gy", -1)
    from_xlow = shifted(xhigh, "gx", 1)
    from_xhigh = shifted(xlow, "gx", -1)
    clow, chigh = call(corner_kernel, [(SLAB, F32)] * 2, args=(from_ylow, from_yhigh))
    from_clow = shifted(chigh, "gx", 1)
    from_chigh = shifted(clow, "gx", -1)
    rows = ((104, 128), F32)
    field, k10, e10, c10 = call(
        sweep_kernel,
        [((100, 8, 128), F32), rows, rows, rows],
        [VMEM((16, 16, 8, 128), F32)] * 2 + [VMEM((16, 16, 128), F32)] * 6,
        args=(tiles, cond, padded, from_ylow, from_yhigh, from_xlow, from_xhigh, from_clow, from_chigh),
    )
    other = lax.ppermute(field, "vert", [(0, 1), (1, 0)])
    points = c10[:, 0:16].astype(jnp.int32)
    onehot = (points.reshape(1664, 1) == jnp.arange(128, dtype=jnp.int32)).astype(BF16)
    index = jnp.pad(points.reshape(13, 128), ((0, 3), (0, 0)))
    vert = lax.axis_index("vert").astype(jnp.int32).reshape(1)
    interp, coarse = call(
        galerkin_kernel,
        [((64, 16, 128), F32), ((8, 9, 8, 256), F32)],
        [VMEM((1664, 128), F32), VMEM((8, 128, 128), F32)] + [VMEM((1664, 128), BF16)] * 4,
        specs=[pl.BlockSpec(memory_space=pltpu.SMEM)] + [pl.BlockSpec(memory_space=VMEM)] * 6,
        args=(vert, field, other, k10, e10, onehot, index),
    )
    return interp.reshape(8, 8, 16, 128), jnp.transpose(coarse, (0, 2, 1, 3))


def solution(mesh):
    placed = (P("vert", "gx", "gy", None), P("gx", "gy", None), P("gx", "gy", None))
    return jax.shard_map(
        body,
        mesh=mesh,
        in_specs=placed,
        out_specs=(P("gx", "gy", None, None), P("gx", "gy", None, None)),
        check_vma=False,
    )
```

time: 119 us -> 55 us (0.46)
  the two profiles are of different devices: /device:TPU:217 before, /device:TPU:130 now
where the time goes in v1:
time: 55 us; the launch traced here: 54.5 us
  starting transfers between devices  25.5 us (46%)
  waiting for transfers between devices  12.9 us (23%)
  Pallas kernels  12.4 us (23%)
  local copies, waits for them, and re-layouts  2.63 us (5%)
  between operations  0.78 us (1%)
    ppermute x6, starting transfers between devices, shifted(): return lax.ppermute(value, axis, pairs)  21.5 us
    pallas_call x4, Pallas kernels, call(): pl.pallas_call(kernel, out_shape=shapes, in_specs=specs or [pl.BlockSpec(...  12.4 us
    ppermute x1, waiting for transfers between devices, body(): other = lax.ppermute(field, 'vert', [(0, 1), (1, 0)])  10.2 us
    ppermute x1, starting transfers between devices, body(): other = lax.ppermute(field, 'vert', [(0, 1), (1, 0)])  4.03 us
    ppermute x6, waiting for transfers between devices, shifted(): return lax.ppermute(value, axis, pairs)  2.68 us
    unnamed x8, local copies, waits for them, and re-layouts  2.46 us
  transfers between devices with their start and end apart: 7, of which 3 were waited for; matrix products, arithmetic and copies ran while one was open for 1% of the time, Pallas kernels for 0%

profile of v1, /device:TPU:130, one launch (start us, length us, event | category | flops | bytes accessed | tf_op | source)
XLA Modules:
  0.0 54.5 jit_solution(7597904183040572824)
XLA Ops:
  0.6 0.0 copy-start
  0.6 0.9 %copy-done = f32[8,8,8,128]{3,2,1,0:T(8,128)S(1)} copy-done((f32[8,8,8,128]{3,2,1,0:T(8,128)S(1)}, f32[8,8,8,128]{3,2,1,0:T(8,128)}, u32[]{:S(2)}) %copy-start) | copy-done | bytes 262168
  1.6 0.0 copy-start.1
  1.6 0.8 %copy-done.1 = f32[8,8,128]{2,1,0:T(8,128)S(1)} copy-done((f32[8,8,128]{2,1,0:T(8,128)S(1)}, f32[8,8,128]{2,1,0:T(8,128)}, u32[]{:S(2)}) %copy-start.1) | copy-done | bytes 32792
  2.3 0.0 copy-start.3
  2.3 0.8 %copy-done.3 = s32[8,8,16]{2,1,0:T(8,128)S(1)} copy-done((s32[8,8,16]{2,1,0:T(8,128)S(1)}, s32[8,8,16]{2,1,0:T(8,128)}, u32[]{:S(2)}) %copy-start.3) | copy-done | bytes 4120
  3.1 0.2 shard_map.50
  3.3 3.5 %collective-permute-start = (f32[37,8,128]{2,1,0:T(8,128)S(1)}, f32[37,8,128]{2,1,0:T(8,128)S(1)}, u32[]{:S(2)}, u32[]{:S(2)}) collective-permute-start(f32[37,8,128]{2,1,0:T(8,128)S(1)} %get-tuple-element.18), channel_id=1, source_target_pairs={{0,2},{2,4},{4,6},{6,8},{8,10},{10,12},{12,14},{1,3},{3,5},{5,7},{... | collective-permute-start | bytes 454664 | tf_op jit(solution)/shard_map/ppermute | solution.py:366
  6.8 4.5 %collective-permute-start.1 = (f32[37,8,128]{2,1,0:T(8,128)S(1)}, f32[37,8,128]{2,1,0:T(8,128)S(1)}, u32[]{:S(2)}, u32[]{:S(2)}) collective-permute-start(f32[37,8,128]{2,1,0:T(8,128)S(1)} %get-tuple-element.19), channel_id=1, source_target_pairs={{2,0},{4,2},{6,4},{8,6},{10,8},{12,10},{14,12},{3,1},{5,3},{7,5},{... | collective-permute-start | bytes 454664 | tf_op jit(solution)/shard_map/ppermute | solution.py:366
  11.2 1.9 %collective-permute-start.2 = (f32[37,8,128]{2,1,0:T(8,128)S(1)}, f32[37,8,128]{2,1,0:T(8,128)S(1)}, u32[]{:S(2)}, u32[]{:S(2)}) collective-permute-start(f32[37,8,128]{2,1,0:T(8,128)S(1)} %get-tuple-element.20), channel_id=1, source_target_pairs={{0,16},{16,32},{32,48},{48,64},{64,80},{80,96},{96,112},{112,128},... | collective-permute-start | bytes 454664 | tf_op jit(solution)/shard_map/ppermute | solution.py:366
  13.2 4.9 %collective-permute-start.3 = (f32[37,8,128]{2,1,0:T(8,128)S(1)}, f32[37,8,128]{2,1,0:T(8,128)S(1)}, u32[]{:S(2)}, u32[]{:S(2)}) collective-permute-start(f32[37,8,128]{2,1,0:T(8,128)S(1)} %get-tuple-element.21), channel_id=1, source_target_pairs={{16,0},{32,16},{48,32},{64,48},{80,64},{96,80},{112,96},{128,112},... | collective-permute-start | bytes 454664 | tf_op jit(solution)/shard_map/ppermute | solution.py:366
  18.0 0.0 collective-permute-done.ylow
  18.0 0.0 collective-permute-done.1.yhigh
  18.1 0.0 copy-start.2
  18.1 1.9 %collective-permute-start.4 = (f32[37,8,128]{2,1,0:T(8,128)S(1)}, f32[37,8,128]{2,1,0:T(8,128)S(1)}, u32[]{:S(2)}, u32[]{:S(2)}) collective-permute-start(f32[37,8,128]{2,1,0:T(8,128)S(1)} %get-tuple-element.22), channel_id=1, source_target_pairs={{0,16},{16,32},{32,48},{48,64},{64,80},{80,96},{96,112},{112,128},... | collective-permute-start | bytes 454664 | tf_op jit(solution)/shard_map/ppermute | solution.py:366
  20.0 4.9 %collective-permute-start.5 = (f32[37,8,128]{2,1,0:T(8,128)S(1)}, f32[37,8,128]{2,1,0:T(8,128)S(1)}, u32[]{:S(2)}, u32[]{:S(2)}) collective-permute-start(f32[37,8,128]{2,1,0:T(8,128)S(1)} %get-tuple-element.23), channel_id=1, source_target_pairs={{16,0},{32,16},{48,32},{64,48},{80,64},{96,80},{112,96},{128,112},... | collective-permute-start | bytes 454664 | tf_op jit(solution)/shard_map/ppermute | solution.py:366
  24.9 0.0 collective-permute-done.2.xlow
  24.9 0.0 collective-permute-done.3.xhigh
  24.9 0.9 %collective-permute-done.4.clow = f32[37,8,128]{2,1,0:T(8,128)S(1)} collective-permute-done((f32[37,8,128]{2,1,0:T(8,128)S(1)}, f32[37,8,128]{2,1,0:T(8,128)S(1)}, u32[]{:S(2)}, u32[]{:S(2)}) %collective-permute-start.4) | collective-permute-done | bytes 151584 | tf_op jit(solution)/shard_map/ppermute | solution.py:366
  25.8 1.8 %collective-permute-done.5.chigh = f32[37,8,128]{2,1,0:T(8,128)S(1)} collective-permute-done((f32[37,8,128]{2,1,0:T(8,128)S(1)}, f32[37,8,128]{2,1,0:T(8,128)S(1)}, u32[]{:S(2)}, u32[]{:S(2)}) %collective-permute-start.5) | collective-permute-done | bytes 151584 | tf_op jit(solution)/shard_map/ppermute | solution.py:366
  27.6 0.0 copy-done.2
  27.6 4.1 %shard_map.52 = (f32[100,8,128]{2,1,0:T(8,128)S(1)}, f32[104,128]{1,0:T(8,128)S(1)}, f32[104,128]{1,0:T(8,128)S(1)}, f32[104,128]{1,0:T(8,128)S(1)}) custom-call(f32[64,8,128]{2,1,0:T(8,128)S(1)} %get-tuple-element.16.tiles, f32[64,128]{1,0:T(8,128)S(1)} %bitcast.8, f32[64,128]{1,0:T(8,128)S(1)} %get-tuple-element.17.padded, ...), custom_call_target="tpu_custom_call" | custom-call | bytes 1806336 | tf_op jit(solution)/shard_map/pallas_call | solution.py:352
  31.7 0.1 reshape.28
  31.8 0.1 eq.15
  31.8 4.0 %collective-permute-start.6 = (f32[100,8,128]{2,1,0:T(8,128)S(1)}, f32[100,8,128]{2,1,0:T(8,128)S(1)}, u32[]{:S(2)}, u32[]{:S(2)}) collective-permute-start(f32[100,8,128]{2,1,0:T(8,128)S(1)} %get-tuple-element.24.own), channel_id=1, source_target_pairs={{0,1},{1,0},{2,3},{3,2},{4,5},{5,4},{6,7},{7,6},{8,9},{9,8},{10,11... | collective-permute-start | bytes 1228808 | tf_op jit(solution)/shard_map/ppermute | solution.py:390
  35.9 0.3 fusion.onehot
  36.2 10.2 %collective-permute-done.6.other = f32[100,8,128]{2,1,0:T(8,128)S(1)} collective-permute-done((f32[100,8,128]{2,1,0:T(8,128)S(1)}, f32[100,8,128]{2,1,0:T(8,128)S(1)}, u32[]{:S(2)}, u32[]{:S(2)}) %collective-permute-start.6) | collective-permute-done | bytes 409632 | tf_op jit(solution)/shard_map/ppermute | solution.py:390
  46.4 8.1 %shard_map.53 = (f32[64,16,128]{2,1,0:T(8,128)}, f32[8,9,8,256]{3,2,1,0:T(8,128)}) custom-call(s32[1]{0:T(128)} %bitcast.vert, f32[100,8,128]{2,1,0:T(8,128)S(1)} %get-tuple-element.24.own, f32[100,8,128]{2,1,0:T(8,128)S(1)} %collective-permute-done.6.other, f32[104,128]{1,0:T(8,128)S(1)} %get-tuple-element.25.k10, f32[104,128]{1,0:T(8,128)S(1)} %get-tuple-element.26.e10, ...), custom_call_target="tpu_custom_call" | custom-call | bytes 2899972 | tf_op jit(solution)/shard_map/pallas_call | solution.py:352
  (3 shorter events, 0.0 us)
Async XLA Ops:
  0.6 1.0 %copy-start = (f32[8,8,8,128]{3,2,1,0:T(8,128)S(1)}, f32[8,8,8,128]{3,2,1,0:T(8,128)}, u32[]{:S(2)}) copy-start(f32[8,8,8,128]{3,2,1,0:T(8,128)} %param.3) | copy-start | bytes 786436
  1.6 0.8 %copy-start.1 = (f32[8,8,128]{2,1,0:T(8,128)S(1)}, f32[8,8,128]{2,1,0:T(8,128)}, u32[]{:S(2)}) copy-start(f32[8,8,128]{2,1,0:T(8,128)} %param.4) | copy-start | bytes 98308
  2.3 0.8 %copy-start.3 = (s32[8,8,16]{2,1,0:T(8,128)S(1)}, s32[8,8,16]{2,1,0:T(8,128)}, u32[]{:S(2)}) copy-start(s32[8,8,16]{2,1,0:T(8,128)} %param.5) | copy-start | bytes 12292
  3.3 14.8 %collective-permute-start = (f32[37,8,128]{2,1,0:T(8,128)S(1)}, f32[37,8,128]{2,1,0:T(8,128)S(1)}, u32[]{:S(2)}, u32[]{:S(2)}) collective-permute-start(f32[37,8,128]{2,1,0:T(8,128)S(1)} %get-tuple-element.18), channel_id=1, source_target_pairs={{0,2},{2,4},{4,6},{6,8},{8,10},{10,12},{12,14},{1,3},{3,5},{5,7},{... | collective-permute-start | bytes 454664 | tf_op jit(solution)/shard_map/ppermute | solution.py:366
  6.8 11.3 %collective-permute-start.1 = (f32[37,8,128]{2,1,0:T(8,128)S(1)}, f32[37,8,128]{2,1,0:T(8,128)S(1)}, u32[]{:S(2)}, u32[]{:S(2)}) collective-permute-start(f32[37,8,128]{2,1,0:T(8,128)S(1)} %get-tuple-element.19), channel_id=1, source_target_pairs={{2,0},{4,2},{6,4},{8,6},{10,8},{12,10},{14,12},{3,1},{5,3},{7,5},{... | collective-permute-start | bytes 454664 | tf_op jit(solution)/shard_map/ppermute | solution.py:366
  11.2 13.6 %collective-permute-start.2 = (f32[37,8,128]{2,1,0:T(8,128)S(1)}, f32[37,8,128]{2,1,0:T(8,128)S(1)}, u32[]{:S(2)}, u32[]{:S(2)}) collective-permute-start(f32[37,8,128]{2,1,0:T(8,128)S(1)} %get-tuple-element.20), channel_id=1, source_target_pairs={{0,16},{16,32},{32,48},{48,64},{64,80},{80,96},{96,112},{112,128},... | collective-permute-start | bytes 454664 | tf_op jit(solution)/shard_map/ppermute | solution.py:366
  13.2 11.7 %collective-permute-start.3 = (f32[37,8,128]{2,1,0:T(8,128)S(1)}, f32[37,8,128]{2,1,0:T(8,128)S(1)}, u32[]{:S(2)}, u32[]{:S(2)}) collective-permute-start(f32[37,8,128]{2,1,0:T(8,128)S(1)} %get-tuple-element.21), channel_id=1, source_target_pairs={{16,0},{32,16},{48,32},{64,48},{80,64},{96,80},{112,96},{128,112},... | collective-permute-start | bytes 454664 | tf_op jit(solution)/shard_map/ppermute | solution.py:366
  18.1 9.5 %copy-start.2 = (f32[8,8,128]{2,1,0:T(8,128)S(1)}, f32[8,8,128]{2,1,0:T(8,128)}, u32[]{:S(2)}) copy-start(f32[8,8,128]{2,1,0:T(8,128)} %param.4) | copy-start | bytes 98308
  18.1 7.7 %collective-permute-start.4 = (f32[37,8,128]{2,1,0:T(8,128)S(1)}, f32[37,8,128]{2,1,0:T(8,128)S(1)}, u32[]{:S(2)}, u32[]{:S(2)}) collective-permute-start(f32[37,8,128]{2,1,0:T(8,128)S(1)} %get-tuple-element.22), channel_id=1, source_target_pairs={{0,16},{16,32},{32,48},{48,64},{64,80},{80,96},{96,112},{112,128},... | collective-permute-start | bytes 454664 | tf_op jit(solution)/shard_map/ppermute | solution.py:366
  20.0 7.6 %collective-permute-start.5 = (f32[37,8,128]{2,1,0:T(8,128)S(1)}, f32[37,8,128]{2,1,0:T(8,128)S(1)}, u32[]{:S(2)}, u32[]{:S(2)}) collective-permute-start(f32[37,8,128]{2,1,0:T(8,128)S(1)} %get-tuple-element.23), channel_id=1, source_target_pairs={{16,0},{32,16},{48,32},{64,48},{80,64},{96,80},{112,96},{128,112},... | collective-permute-start | bytes 454664 | tf_op jit(solution)/shard_map/ppermute | solution.py:366
  31.8 14.5 %collective-permute-start.6 = (f32[100,8,128]{2,1,0:T(8,128)S(1)}, f32[100,8,128]{2,1,0:T(8,128)S(1)}, u32[]{:S(2)}, u32[]{:S(2)}) collective-permute-start(f32[100,8,128]{2,1,0:T(8,128)S(1)} %get-tuple-element.24.own), channel_id=1, source_target_pairs={{0,1},{1,0},{2,3},{3,2},{4,5},{5,4},{6,7},{7,6},{8,9},{9,8},{10,11... | collective-permute-start | bytes 1228808 | tf_op jit(solution)/shard_map/ppermute | solution.py:390

commit v2 on v1

v2 whole, which is shorter than its diff:
```python
import jax
import jax.numpy as jnp
from jax import lax
from jax.experimental import pallas as pl
from jax.experimental.pallas import tpu as pltpu
from jax.sharding import PartitionSpec as P


WY = 0.6
WZ = 0.15
OMEGA = 0.6
SHIFT = 0.5
RIDGE = 0.1
F32 = jnp.float32
BF16 = jnp.bfloat16
VMEM = pltpu.VMEM
SLAB = (37, 8, 128)
CROSS = (74, 8, 128)
SMEM = pl.BlockSpec(memory_space=pltpu.SMEM)
LOCAL = pl.BlockSpec(memory_space=VMEM)
BATCHES = ((0, 1, 2, 3), (4, 5, 6, 7), (8, 9, 10), (11, 12))
FAR = pl.BlockSpec(memory_space=pltpu.HBM)


def iota(shape, dim):
    return lax.broadcasted_iota(jnp.int32, shape, dim)


def along_z(t, low, high):
    return t + low * pltpu.roll(t, 1, 1) + high * pltpu.roll(t, 127, 1)


def z_weights(rows):
    lane = iota((rows, 128), 1)
    return jnp.where(lane == 0, 0.0, WZ), jnp.where(lane == 127, 0.0, WZ)


def pack_kernel(side, vec_in, cond_in, points_in, tiles, cond, padded, first, second, vec, points, sems):
    copies = [
        pltpu.make_async_copy(src, dst, sems.at[n])
        for n, (src, dst) in enumerate(
            ((vec_in, vec), (cond_in, cond), (points_in, points))
        )
    ]
    for copy in copies:
        copy.start()
    even = side[0]
    copies[2].wait()
    padded[...] = jnp.full((64, 128), -1.0, F32)
    padded[:, 0:16] = points[...].astype(F32)
    copies[1].wait()
    for out, up in ((first, even == 1), (second, even == 0)):
        for x in range(8):
            half = x % 2 * 4
            out[32 + x // 2, half : half + 4, :] = jnp.where(up, cond[x, 4:8, :], cond[x, 0:4, :])
        out[36] = jnp.where(up, padded[pl.ds(7, 8, stride=8), :], padded[pl.ds(0, 8, stride=8), :])
    copies[0].wait()
    for x in range(8):
        row = [vec[pl.ds(x * 8 + y, 8, stride=64), :] for y in range(8)]
        for y in range(8):
            tiles[x * 8 + y] = row[y]
        for y in range(4):
            first[x * 4 + y] = jnp.where(even == 1, row[y + 4], row[y])
            second[x * 4 + y] = jnp.where(even == 1, row[y], row[y + 4])


def cross_kernel(side, tiles, cond, padded, got1, got2, first, second):
    y_even, x_even = side[0] == 1, side[1]

    def low(*at):
        return jnp.where(y_even, got2[at], got1[at])

    def high(*at):
        return jnp.where(y_even, got1[at], got2[at])

    for out, up in ((first, x_even), (second, 1 - x_even)):
        for xx in range(4):
            x = xx + 4 * up
            for y in range(4):
                out[xx * 16 + y] = low(x * 4 + y)
                out[xx * 16 + 12 + y] = high(x * 4 + y)
            for y in range(8):
                out[xx * 16 + 4 + y] = tiles[x * 8 + y]
            rows = slice(xx % 2 * 4, xx % 2 * 4 + 4)
            k = cond[x]
            out[64 + 2 * xx, 0:4, :] = low(32 + xx // 2 + 2 * up, rows)
            out[64 + 2 * xx, 4:8, :] = k[0:4, :]
            out[65 + 2 * xx, 0:4, :] = k[4:8, :]
            out[65 + 2 * xx, 4:8, :] = high(32 + xx // 2 + 2 * up, rows)
        top = up == 1
        out[73] = jnp.zeros((8, 128), F32)
        out[72, 0:1, :] = jnp.where(top, low(36, slice(7, 8)), low(36, slice(0, 1)))
        out[72, 1:8, :] = jnp.where(top, padded[56:63, :], padded[0:7, :])
        out[73, 0:1, :] = jnp.where(top, padded[63:64, :], padded[7:8, :])
        out[73, 1:2, :] = jnp.where(top, high(36, slice(7, 8)), high(36, slice(0, 1)))


def sweep_kernel(
    side, tiles, cond, padded, got1, got2, cross1, cross2,
    field, k_out, e_out, c_out,
    u0, u1, kk, kz, hh, h4, rk, ee,
):
    y_even, x_even = side[0] == 1, side[1] == 1

    def ylow(*at):
        return jnp.where(y_even, got2[at], got1[at])

    def yhigh(*at):
        return jnp.where(y_even, got1[at], got2[at])

    def xlow(*at):
        return jnp.where(x_even, cross2[at], cross1[at])

    def xhigh(*at):
        return jnp.where(x_even, cross1[at], cross2[at])

    for x in range(16):
        if 4 <= x < 12:
            rows = slice(x % 2 * 4, x % 2 * 4 + 4)
            kk[x, 0:4, :] = ylow(32 + (x - 4) // 2, rows)
            kk[x, 4:12, :] = cond[x - 4]
            kk[x, 12:16, :] = yhigh(32 + (x - 4) // 2, rows)
        else:
            source, xx = (xlow, x) if x < 4 else (xhigh, x - 12)
            kk[x, 0:8, :] = source(64 + 2 * xx)
            kk[x, 8:16, :] = source(65 + 2 * xx)

    low16, high16 = z_weights(16)
    for x in range(16):
        kz[x] = along_z(kk[x], low16, high16)
    for x in range(1, 15):
        k = kk[x]
        s = kz[x - 1] + kz[x] + kz[x + 1]
        s = s + WY * (pltpu.roll(s, 1, 0) + pltpu.roll(s, 15, 0)) - k
        alive = k > 0.0
        h = jnp.where(alive, OMEGA * k / jnp.where(alive, SHIFT * k + s, 1.0), 0.0)
        hh[x] = h
        h4[x] = (1.0 - OMEGA) - h
        rk[x] = jnp.where(alive, 1.0 / jnp.where(alive, k, 1.0), 0.0)
        ee[x] = (SHIFT + 1.0) * k + s

    for x in range(16):
        for y in range(16):
            if x < 4:
                t = xlow(x * 16 + y)
            elif x >= 12:
                t = xhigh((x - 12) * 16 + y)
            elif y < 4:
                t = ylow((x - 4) * 4 + y)
            elif y >= 12:
                t = yhigh((x - 4) * 4 + y - 12)
            else:
                t = tiles[(x - 4) * 8 + y - 4]
            u0[x, y] = t * jnp.broadcast_to(kk[x, y : y + 1, :], (8, 128))

    low8, high8 = z_weights(8)

    def sweep(src, first, count, write):
        def step(x, carry):
            hx, h4x = hh[x], h4[x]
            s = [
                src[x - 1, y] + src[x, y] + src[x + 1, y]
                for y in range(first - 1, first + count + 1)
            ]
            for j in range(count):
                y = first + j
                t = s[j + 1] + WY * (s[j] + s[j + 2])
                w = along_z(t, low8, high8)
                a = jnp.broadcast_to(h4x[y : y + 1, :], (8, 128))
                b = jnp.broadcast_to(hx[y : y + 1, :], (8, 128))
                write(x, y, a * src[x, y] + b * w)
            return carry

        lax.fori_loop(first, first + count, step, 0, unroll=2)

    def to_u1(x, y, value):
        u1[x, y] = value

    def to_u0(x, y, value):
        u0[x, y] = value

    sweep(u0, 1, 14, to_u1)
    sweep(u1, 2, 12, to_u0)

    def step(x, carry):
        hx, h4x, rx = hh[x], h4[x], rk[x]
        s = [u0[x - 1, y] + u0[x, y] + u0[x + 1, y] for y in range(2, 14)]
        for j in range(10):
            y = 3 + j
            t = s[j + 1] + WY * (s[j] + s[j + 2])
            w = along_z(t, low8, high8)
            a = jnp.broadcast_to(h4x[y : y + 1, :], (8, 128))
            b = jnp.broadcast_to(hx[y : y + 1, :], (8, 128))
            r = jnp.broadcast_to(rx[y : y + 1, :], (8, 128))
            field[(x - 3) * 10 + j] = (a * u0[x, y] + b * w) * r
        return carry

    lax.fori_loop(3, 13, step, 0, unroll=2)

    for x in range(10):
        k_out[x * 10 : x * 10 + 10, :] = kk[x + 3, 3:13, :]
        e_out[x * 10 : x * 10 + 10, :] = ee[x + 3, 3:13, :]
        row = x * 10
        if 1 <= x < 9:
            c_out[row : row + 1, :] = ylow(36, slice(x - 1, x))
            c_out[row + 1 : row + 9, :] = padded[(x - 1) * 8 : (x - 1) * 8 + 8, :]
            c_out[row + 9 : row + 10, :] = yhigh(36, slice(x - 1, x))
        else:
            source = xlow if x == 0 else xhigh
            c_out[row : row + 8, :] = source(72)
            c_out[row + 8 : row + 10, :] = source(73, slice(0, 2))
    k_out[100:104, :] = jnp.zeros((4, 128), F32)
    e_out[100:104, :] = jnp.zeros((4, 128), F32)
    c_out[100:104, :] = jnp.full((4, 128), -1.0, F32)


def halves(t):
    first = t.astype(BF16)
    return first, (t - first.astype(F32)).astype(BF16)


def product(a, b):
    return lax.dot_general(a, b, (((1,), (0,)), ((), ())), preferred_element_type=F32)


def product_t(a, b):
    return lax.dot_general(a, b, (((1,), (1,)), ((), ())), preferred_element_type=F32)


def gather_lanes(t, index):
    return jnp.take_along_axis(t, index, axis=1)


def galerkin_kernel(
    vert, own, other, k10, e10, onehot, index,
    interp, coarse,
    rs, ps, l1s, l2s, r1s, r2s, e1s, e2s, ts, mids, cs, sems,
):
    first = vert[0] == 0
    lane16 = iota((16, 128), 1)
    sub16 = iota((16, 128), 0)
    lane8 = iota((8, 128), 1)
    sub8 = iota((8, 128), 0)
    block16, block8 = lane16 // 16, lane8 // 16
    lane128, sub128 = iota((128, 128), 1), iota((128, 128), 0)
    own_block = (lane128 % 64) // 8 == sub128 // 16
    ones = jnp.where(lane128 // 16 == sub128 // 16, 1.0, 0.0).astype(BF16)
    block_ones = [jnp.where(block16 == bb, 1.0, 0.0).astype(BF16) for bb in range(8)]
    on_diag = lane16 % 16 == sub16
    low128, high128 = z_weights(128)

    def rows_of(g):
        return slice(128 * g, 128 * g + 128)

    def fields(g):
        n = 8 if g < 12 else 4
        a = own[8 * g : 8 * g + n].reshape(n * 8, 128)
        b = other[8 * g : 8 * g + n].reshape(n * 8, 128)
        fa, fb = jnp.where(first, a, b), jnp.where(first, b, a)
        if n == 8:
            return halves(jnp.concatenate([fa, fb], axis=0))
        none = jnp.zeros((32, 128), F32)
        return halves(jnp.concatenate([fa, none, fb, none], axis=0))

    def values(g, pair):
        oh = onehot[rows_of(g), :]
        return [jnp.where(own_block, product_t(oh, f), 0.0).astype(BF16) for f in pair]

    def rights(pair, spots):
        f1, f2 = pair
        c1, c2 = spots
        return product(
            jnp.concatenate([c1, c1, c2], axis=1), jnp.concatenate([f1, f2, f1], axis=0)
        )

    def system_of(g, right):
        spots = jnp.broadcast_to(index[g : g + 1, :], (16, 128))
        wanted = jnp.maximum(spots, 0)
        gram = jnp.zeros((16, 128), F32)
        for bb in range(8):
            part = gather_lanes(right[16 * bb : 16 * bb + 16, :], wanted)
            gram = jnp.where(block16 == bb, part, gram)
        gram = jnp.where(spots >= 0, gram, 0.0)
        d = jnp.where(on_diag, gram, 0.0)
        d = d[0:8, :] + d[8:16, :]
        for shift in (4, 2, 1):
            d = d + pltpu.roll(d, shift, 0)
        for bit in (1, 2, 4, 8):
            d = d + gather_lanes(d, lane8 ^ bit)
        ridge = (RIDGE / 16) * d + 1e-06
        ridge = jnp.concatenate([ridge, ridge], axis=0)
        system = gram + jnp.where(on_diag, ridge, 0.0)
        return [system[0:8, :], system[8:16, :]]

    systems = []
    for batch in BATCHES:
        pairs = [fields(g) for g in batch]
        spots = [values(g, pair) for g, pair in zip(batch, pairs)]
        found = [rights(pair, spot) for pair, spot in zip(pairs, spots)]
        for g, right in zip(batch, found):
            rs[rows_of(g), :] = right
        systems += [system_of(g, right) for g, right in zip(batch, found)]

    for k in range(16):
        half, row = k // 8, k % 8
        at_k = lane8 % 16 == k
        spot = block8 * 16 + k
        for s in systems:
            pivot_row = jnp.broadcast_to(s[half][row : row + 1, :], (8, 128))
            scale = 1.0 / gather_lanes(pivot_row, spot)
            r = jnp.where(at_k, 1.0, pivot_row) * scale
            for t in range(2):
                factor = gather_lanes(s[t], spot)
                new = jnp.where(at_k, 0.0, s[t]) - factor * r
                if t == half:
                    new = jnp.where(sub8 == row, r, new)
                s[t] = new

    def weights(g):
        m1, m2 = halves(jnp.concatenate(systems[g], axis=0))
        m1 = jnp.concatenate([m1 * block_ones[bb] for bb in range(8)], axis=0)
        m2 = jnp.concatenate([m2 * block_ones[bb] for bb in range(8)], axis=0)
        r1, r2 = halves(rs[rows_of(g), :])
        w = product(
            jnp.concatenate([m1, m1, m2], axis=1), jnp.concatenate([r1, r2, r1], axis=0)
        )
        return w, product(ones, onehot[rows_of(g), :])

    def spread(ref, g):
        return jnp.concatenate(
            [jnp.broadcast_to(ref[8 * g + bb : 8 * g + bb + 1, :], (16, 128)) for bb in range(8)],
            axis=0,
        )

    def finish(g, w, c_row):
        p = w * (1.0 - c_row) + onehot[rows_of(g), :].astype(F32)
        ps[rows_of(g), :] = p
        left = spread(k10, g) * p
        padded = slice(128 * g + 160, 128 * g + 288)
        l1s[padded, :], l2s[padded, :] = halves(left)
        image = along_z(left, low128, high128)
        r1s[rows_of(g), :], r2s[rows_of(g), :] = halves(image)
        e1s[rows_of(g), :], e2s[rows_of(g), :] = halves(spread(e10, g) * p - image)

    for batch in BATCHES:
        found = [weights(g) for g in batch]
        for g, pair in zip(batch, found):
            finish(g, *pair)

    interp_copies = [
        pltpu.make_async_copy(
            ps.at[pl.ds((x * 10 + 1) * 16, 128), :], interp.at[pl.ds((x - 1) * 128, 128), :],
            sems.at[x - 1],
        )
        for x in range(1, 9)
    ]
    for copy in interp_copies:
        copy.start()

    def multiply(x, slot):
        base = x * 160
        low, high = max(x - 1, 1), min(x + 1, 8)

        def lefts(ref):
            return [ref[160 * n + 176 : 160 * n + 304, :] for n in range(low, high + 1)]

        def stacked(ref, order):
            return jnp.concatenate(
                [ref[base + 16 * y : base + 16 * y + 16, :] for y in order], axis=0
            )

        lhs = jnp.concatenate(
            [jnp.concatenate([a, a, b], axis=1) for a, b in zip(lefts(l1s), lefts(l2s))], axis=0
        )
        order = (0, 7, 6, 5, 4, 3, 2, 1, 8, 7, 6, 5, 4, 3, 2, 9)
        q1, q2 = stacked(r1s, order), stacked(r2s, order)
        at = 128 * (low - x + 1)
        ts[slot, at : at + 128 * (high - low + 1), :] = product_t(
            lhs, jnp.concatenate([q1, q2, q1], axis=1)
        )
        if 1 <= x <= 8:
            order = (8, 7, 6, 5, 4, 3, 2, 1)
            q1, q2 = stacked(e1s, order), stacked(e2s, order)
            at = 128 * (x - low)
            mids[slot] = product_t(lhs[at : at + 128, :], jnp.concatenate([q1, q2, q1], axis=1))

    def arrange(x, slot):
        for side in range(3):
            ox = 1 - side
            if not 1 <= x - ox <= 8:
                continue
            for o in range(3):
                first_turn, last_turn = min(o, 1), max(o - 1, 0)
                amount = (first_turn - o - block8) % 8
                scale = 1.0 if ox == 0 and o == 1 else (-1.0 if o == 1 else -WY)
                for half in range(2):
                    merged = jnp.zeros((8, 128), F32)
                    for y in range(8):
                        rows = slice(16 * y + 8 * half, 16 * y + 8 * half + 8)
                        if ox == 0 and o == 1:
                            part = mids[slot, rows, :]
                        else:
                            rows = slice(128 * side + rows.start, 128 * side + rows.stop)
                            if o == 2 or (o == 1 and y == 7):
                                part = ts[slot, rows, 128:256]
                            else:
                                part = ts[slot, rows, 0:128]
                        merged = jnp.where(block8 == (-y - o) % 8, part, merged)
                    merged = pltpu.roll(merged, 16 * first_turn, 1, stride=16, stride_axis=0)
                    for bit in (1, 2, 4):
                        merged = jnp.where(amount & bit != 0, pltpu.roll(merged, bit, 0), merged)
                    merged = pltpu.roll(merged, 16 * last_turn, 1, stride=16, stride_axis=0)
                    cs[x - ox - 1, 3 * (ox + 1) + o, :, half * 128 : half * 128 + 128] = scale * merged

    coarse_copies = [
        pltpu.make_async_copy(cs.at[x], coarse.at[x], sems.at[8 + x]) for x in range(8)
    ]
    multiply(0, 0)
    for x in range(1, 11):
        if x < 10:
            multiply(x, x % 2)
        arrange(x - 1, (x - 1) % 2)
        if x > 2:
            coarse_copies[x - 3].start()
    for copy in interp_copies:
        copy.wait()
    for copy in coarse_copies:
        copy.wait()


def call(kernel, outs, scratch=(), specs=None, args=(), flops=0, outs_at=LOCAL):
    shapes = [jax.ShapeDtypeStruct(*o) for o in outs]
    moved = sum(a.size * 4 for a in args) + sum(4 * s.size for s in shapes)
    return pl.pallas_call(
        kernel,
        out_shape=shapes,
        in_specs=specs,
        out_specs=[outs_at] * len(outs),
        scratch_shapes=list(scratch),
        compiler_params=pltpu.CompilerParams(vmem_limit_bytes=48 << 20),
        cost_estimate=pl.CostEstimate(flops=flops, bytes_accessed=moved, transcendentals=0),
    )(*args)


def swapped(value, axis, first):
    count = lax.axis_size(axis)
    low = [(i, i + 1) for i in range(first, count - 1, 2)]
    return lax.ppermute(value, axis, low + [(j, i) for i, j in low])


def body(vectors, conductivity, c_points):
    side = jnp.stack([1 - lax.axis_index("gy") % 2, 1 - lax.axis_index("gx") % 2]).astype(jnp.int32)
    tiles, cond, padded, send1, send2 = call(
        pack_kernel,
        [((64, 8, 128), F32), ((8, 8, 128), F32), ((64, 128), F32), (SLAB, F32), (SLAB, F32)],
        [VMEM((512, 128), F32), VMEM((64, 16), jnp.int32), pltpu.SemaphoreType.DMA((3,))],
        specs=[SMEM] + [FAR] * 3,
        args=(side, vectors.reshape(512, 128), conductivity, c_points.reshape(64, 16)),
    )
    got2 = swapped(send2, "gy", 1)
    got1 = swapped(send1, "gy", 0)
    send1, send2 = call(
        cross_kernel,
        [(CROSS, F32)] * 2,
        specs=[SMEM] + [LOCAL] * 5,
        args=(side, tiles, cond, padded, got1, got2),
    )
    cross2 = swapped(send2, "gx", 1)
    cross1 = swapped(send1, "gx", 0)
    rows = ((104, 128), F32)
    field, k10, e10, c10 = call(
        sweep_kernel,
        [((100, 8, 128), F32), rows, rows, rows],
        [VMEM((16, 16, 8, 128), F32)] * 2 + [VMEM((16, 16, 128), F32)] * 6,
        specs=[SMEM] + [LOCAL] * 7,
        args=(side, tiles, cond, padded, got1, got2, cross1, cross2),
    )
    other = lax.ppermute(field, "vert", [(0, 1), (1, 0)])
    points = c10[:, 0:16].astype(jnp.int32)
    onehot = (points.reshape(1664, 1) == jnp.arange(128, dtype=jnp.int32)).astype(BF16)
    index = jnp.pad(points.reshape(13, 128), ((0, 3), (0, 0)))
    vert = lax.axis_index("vert").astype(jnp.int32).reshape(1)
    strips = [VMEM((1664, 128), F32)] * 2 + [VMEM((1920, 128), BF16)] * 2 + [VMEM((1664, 128), BF16)] * 4
    interp, coarse = call(
        galerkin_kernel,
        [((1024, 128), F32), ((8, 9, 8, 256), F32)],
        strips
        + [VMEM((2, 384, 256), F32), VMEM((2, 128, 128), F32), VMEM((8, 9, 8, 256), F32)]
        + [pltpu.SemaphoreType.DMA((16,))],
        specs=[SMEM] + [LOCAL] * 6,
        outs_at=FAR,
        args=(vert, field, other, k10, e10, onehot, index),
    )
    return interp.reshape(8, 8, 16, 128), jnp.transpose(coarse, (0, 2, 1, 3))


def solution(mesh):
    placed = (P("vert", "gx", "gy", None), P("gx", "gy", None), P("gx", "gy", None))
    return jax.shard_map(
        body,
        mesh=mesh,
        in_specs=placed,
        out_specs=(P("gx", "gy", None, None), P("gx", "gy", None, None)),
        check_vma=False,
    )
```

time: 55 us -> 52.5 us (0.955)
  the two profiles are of different devices: /device:TPU:130 before, /device:TPU:227 now
where the time goes in v2:
time: 52.5 us; the launch traced here: 52.2 us
  waiting for transfers between devices  19.2 us (37%)
  starting transfers between devices  19.1 us (36%)
  Pallas kernels  10.9 us (21%)
  local copies, waits for them, and re-layouts  1.78 us (3%)
  between operations  0.77 us (1%)
    ppermute x4, starting transfers between devices, swapped(): return lax.ppermute(value, axis, low + [(j, i) for i, j in low])  15.4 us
    pallas_call x4, Pallas kernels, call(): pl.pallas_call(kernel, out_shape=shapes, in_specs=specs, out_specs=[outs_...  10.9 us
    ppermute x1, waiting for transfers between devices, body(): other = lax.ppermute(field, 'vert', [(0, 1), (1, 0)])  9.8 us
    ppermute x4, waiting for transfers between devices, swapped(): return lax.ppermute(value, axis, low + [(j, i) for i, j in low])  9.42 us
    ppermute x1, starting transfers between devices, body(): other = lax.ppermute(field, 'vert', [(0, 1), (1, 0)])  3.75 us
    unnamed x6, local copies, waits for them, and re-layouts  1.62 us
  transfers between devices with their start and end apart: 5, of which 3 were waited for; matrix products, arithmetic and copies ran while one was open for 1% of the time, Pallas kernels for 0%

profile of v2, /device:TPU:227, one launch (start us, length us, event | category | flops | bytes accessed | tf_op | source)
XLA Modules:
  0.0 52.2 jit_solution(12906925164546768278)
XLA Ops:
  0.6 0.0 copy-start.2
  0.6 0.0 copy-start.1
  0.7 0.1 pad_add_fusion.side
  0.7 0.6 %copy-done.2 = s32[8,8,16]{2,1,0:T(8,128)S(1)} copy-done((s32[8,8,16]{2,1,0:T(8,128)S(1)}, s32[8,8,16]{2,1,0:T(8,128)}, u32[]{:S(2)}) %copy-start.2) | copy-done | bytes 4120
  1.4 0.0 copy-done.1
  1.4 0.0 copy-start
  1.4 0.9 %copy-done = f32[8,8,8,128]{3,2,1,0:T(8,128)S(1)} copy-done((f32[8,8,8,128]{3,2,1,0:T(8,128)S(1)}, f32[8,8,8,128]{3,2,1,0:T(8,128)}, u32[]{:S(2)}) %copy-start) | copy-done | bytes 262168
  2.4 0.9 %shard_map.50 = (f32[64,8,128]{2,1,0:T(8,128)S(1)}, f32[8,8,128]{2,1,0:T(8,128)S(1)}, f32[64,128]{1,0:T(8,128)S(1)}, f32[37,8,128]{2,1,0:T(8,128)S(1)}, f32[37,8,128]{2,1,0:T(8,128)S(1)}) custom-call(s32[2]{0:T(128)S(1)} %pad_add_fusion.side, f32[512,128]{1,0:T(8,128)S(1)} %bitcast.7, f32[8,8,128]{2,1,0:T(8,128)S(1)} %copy-done.1, s32[64,16]{1,0:T(8,128)S(1)} %bitcast.8), custom_call_target="tpu_custom_call" | custom-call | bytes 929800 | tf_op jit(solution)/shard_map/pallas_call | solution.py:434
  3.2 3.2 %collective-permute-start = (f32[37,8,128]{2,1,0:T(8,128)S(1)}, f32[37,8,128]{2,1,0:T(8,128)S(1)}, u32[]{:S(2)}, u32[]{:S(2)}) collective-permute-start(f32[37,8,128]{2,1,0:T(8,128)S(1)} %get-tuple-element.18), channel_id=1, source_target_pairs={{0,2},{4,6},{8,10},{12,14},{2,0},{6,4},{10,8},{14,12},{1,3},{5,7},... | collective-permute-start | bytes 454664 | tf_op jit(solution)/shard_map/ppermute | solution.py:448
  6.4 3.8 %collective-permute-start.1 = (f32[37,8,128]{2,1,0:T(8,128)S(1)}, f32[37,8,128]{2,1,0:T(8,128)S(1)}, u32[]{:S(2)}, u32[]{:S(2)}) collective-permute-start(f32[37,8,128]{2,1,0:T(8,128)S(1)} %get-tuple-element.19), channel_id=1, source_target_pairs={{2,4},{6,8},{10,12},{4,2},{8,6},{12,10},{3,5},{7,9},{11,13},{5,3},... | collective-permute-start | bytes 454664 | tf_op jit(solution)/shard_map/ppermute | solution.py:448
  10.2 0.0 collective-permute-done.got1
  10.2 4.7 %collective-permute-done.1.got2 = f32[37,8,128]{2,1,0:T(8,128)S(1)} collective-permute-done((f32[37,8,128]{2,1,0:T(8,128)S(1)}, f32[37,8,128]{2,1,0:T(8,128)S(1)}, u32[]{:S(2)}, u32[]{:S(2)}) %collective-permute-start.1) | collective-permute-done | bytes 151584 | tf_op jit(solution)/shard_map/ppermute | solution.py:448
  15.0 0.6 %shard_map.51 = (f32[74,8,128]{2,1,0:T(8,128)S(1)}, f32[74,8,128]{2,1,0:T(8,128)S(1)}) custom-call(s32[2]{0:T(128)S(1)} %pad_add_fusion.side, f32[64,8,128]{2,1,0:T(8,128)S(1)} %get-tuple-element.15.tiles, f32[8,8,128]{2,1,0:T(8,128)S(1)} %get-tuple-element.16.cond, f32[64,128]{1,0:T(8,128)S(1)} %get-tuple-element.17.padded, ...), custom_call_target="tpu_custom_call" | custom-call | bytes 1237000 | tf_op jit(solution)/shard_map/pallas_call | solution.py:434
  15.6 3.7 %collective-permute-start.2 = (f32[74,8,128]{2,1,0:T(8,128)S(1)}, f32[74,8,128]{2,1,0:T(8,128)S(1)}, u32[]{:S(2)}, u32[]{:S(2)}) collective-permute-start(f32[74,8,128]{2,1,0:T(8,128)S(1)} %get-tuple-element.20), channel_id=1, source_target_pairs={{0,16},{32,48},{64,80},{96,112},{128,144},{160,176},{192,208},{224... | collective-permute-start | bytes 909320 | tf_op jit(solution)/shard_map/ppermute | solution.py:448
  19.3 4.7 %collective-permute-start.3 = (f32[74,8,128]{2,1,0:T(8,128)S(1)}, f32[74,8,128]{2,1,0:T(8,128)S(1)}, u32[]{:S(2)}, u32[]{:S(2)}) collective-permute-start(f32[74,8,128]{2,1,0:T(8,128)S(1)} %get-tuple-element.21), channel_id=1, source_target_pairs={{16,32},{48,64},{80,96},{112,128},{144,160},{176,192},{208,224},{2... | collective-permute-start | bytes 909320 | tf_op jit(solution)/shard_map/ppermute | solution.py:448
  24.0 0.0 collective-permute-done.2.cross1
  24.0 4.7 %collective-permute-done.3.cross2 = f32[74,8,128]{2,1,0:T(8,128)S(1)} collective-permute-done((f32[74,8,128]{2,1,0:T(8,128)S(1)}, f32[74,8,128]{2,1,0:T(8,128)S(1)}, u32[]{:S(2)}, u32[]{:S(2)}) %collective-permute-start.3) | collective-permute-done | bytes 303136 | tf_op jit(solution)/shard_map/ppermute | solution.py:448
  28.6 3.2 %shard_map.52 = (f32[100,8,128]{2,1,0:T(8,128)S(1)}, f32[104,128]{1,0:T(8,128)S(1)}, f32[104,128]{1,0:T(8,128)S(1)}, f32[104,128]{1,0:T(8,128)S(1)}) custom-call(s32[2]{0:T(128)S(1)} %pad_add_fusion.side, f32[64,8,128]{2,1,0:T(8,128)S(1)} %get-tuple-element.15.tiles, f32[8,8,128]{2,1,0:T(8,128)S(1)} %get-tuple-element.16.cond, ...), custom_call_target="tpu_custom_call" | custom-call | bytes 1806344 | tf_op jit(solution)/shard_map/pallas_call | solution.py:434
  31.9 0.1 reshape.24
  32.0 0.1 eq.18
  32.1 3.8 %collective-permute-start.4 = (f32[100,8,128]{2,1,0:T(8,128)S(1)}, f32[100,8,128]{2,1,0:T(8,128)S(1)}, u32[]{:S(2)}, u32[]{:S(2)}) collective-permute-start(f32[100,8,128]{2,1,0:T(8,128)S(1)} %get-tuple-element.22.own), channel_id=1, source_target_pairs={{0,1},{1,0},{2,3},{3,2},{4,5},{5,4},{6,7},{7,6},{8,9},{9,8},{10,11... | collective-permute-start | bytes 1228808 | tf_op jit(solution)/shard_map/ppermute | solution.py:478
  35.8 0.3 fusion.onehot
  36.1 9.8 %collective-permute-done.4.other = f32[100,8,128]{2,1,0:T(8,128)S(1)} collective-permute-done((f32[100,8,128]{2,1,0:T(8,128)S(1)}, f32[100,8,128]{2,1,0:T(8,128)S(1)}, u32[]{:S(2)}, u32[]{:S(2)}) %collective-permute-start.4) | collective-permute-done | bytes 409632 | tf_op jit(solution)/shard_map/ppermute | solution.py:478
  45.9 6.3 %shard_map.53 = (f32[1024,128]{1,0:T(8,128)}, f32[8,9,8,256]{3,2,1,0:T(8,128)}) custom-call(s32[1]{0:T(128)} %bitcast.vert, f32[100,8,128]{2,1,0:T(8,128)S(1)} %get-tuple-element.22.own, f32[100,8,128]{2,1,0:T(8,128)S(1)} %collective-permute-done.4.other, f32[104,128]{1,0:T(8,128)S(1)} %get-tuple-element.23.k10, f32[104,128]{1,0:T(8,128)S(1)} %get-tuple-element.24.e10, ...), custom_call_target="tpu_custom_call" | custom-call | bytes 2899972 | tf_op jit(solution)/shard_map/pallas_call | solution.py:434
  (2 shorter events, 0.0 us)
Async XLA Ops:
  0.6 0.8 %copy-start.2 = (s32[8,8,16]{2,1,0:T(8,128)S(1)}, s32[8,8,16]{2,1,0:T(8,128)}, u32[]{:S(2)}) copy-start(s32[8,8,16]{2,1,0:T(8,128)} %param.5) | copy-start | bytes 12292
  0.6 0.8 %copy-start.1 = (f32[8,8,128]{2,1,0:T(8,128)S(1)}, f32[8,8,128]{2,1,0:T(8,128)}, u32[]{:S(2)}) copy-start(f32[8,8,128]{2,1,0:T(8,128)} %cond_in.1) | copy-start | bytes 98308
  1.4 0.9 %copy-start = (f32[8,8,8,128]{3,2,1,0:T(8,128)S(1)}, f32[8,8,8,128]{3,2,1,0:T(8,128)}, u32[]{:S(2)}) copy-start(f32[8,8,8,128]{3,2,1,0:T(8,128)} %param.3) | copy-start | bytes 786436
  3.2 7.0 %collective-permute-start = (f32[37,8,128]{2,1,0:T(8,128)S(1)}, f32[37,8,128]{2,1,0:T(8,128)S(1)}, u32[]{:S(2)}, u32[]{:S(2)}) collective-permute-start(f32[37,8,128]{2,1,0:T(8,128)S(1)} %get-tuple-element.18), channel_id=1, source_target_pairs={{0,2},{4,6},{8,10},{12,14},{2,0},{6,4},{10,8},{14,12},{1,3},{5,7},... | collective-permute-start | bytes 454664 | tf_op jit(solution)/shard_map/ppermute | solution.py:448
  6.4 8.5 %collective-permute-start.1 = (f32[37,8,128]{2,1,0:T(8,128)S(1)}, f32[37,8,128]{2,1,0:T(8,128)S(1)}, u32[]{:S(2)}, u32[]{:S(2)}) collective-permute-start(f32[37,8,128]{2,1,0:T(8,128)S(1)} %get-tuple-element.19), channel_id=1, source_target_pairs={{2,4},{6,8},{10,12},{4,2},{8,6},{12,10},{3,5},{7,9},{11,13},{5,3},... | collective-permute-start | bytes 454664 | tf_op jit(solution)/shard_map/ppermute | solution.py:448
  15.6 8.4 %collective-permute-start.2 = (f32[74,8,128]{2,1,0:T(8,128)S(1)}, f32[74,8,128]{2,1,0:T(8,128)S(1)}, u32[]{:S(2)}, u32[]{:S(2)}) collective-permute-start(f32[74,8,128]{2,1,0:T(8,128)S(1)} %get-tuple-element.20), channel_id=1, source_target_pairs={{0,16},{32,48},{64,80},{96,112},{128,144},{160,176},{192,208},{224... | collective-permute-start | bytes 909320 | tf_op jit(solution)/shard_map/ppermute | solution.py:448
  19.3 9.3 %collective-permute-start.3 = (f32[74,8,128]{2,1,0:T(8,128)S(1)}, f32[74,8,128]{2,1,0:T(8,128)S(1)}, u32[]{:S(2)}, u32[]{:S(2)}) collective-permute-start(f32[74,8,128]{2,1,0:T(8,128)S(1)} %get-tuple-element.21), channel_id=1, source_target_pairs={{16,32},{48,64},{80,96},{112,128},{144,160},{176,192},{208,224},{2... | collective-permute-start | bytes 909320 | tf_op jit(solution)/shard_map/ppermute | solution.py:448
  32.1 13.9 %collective-permute-start.4 = (f32[100,8,128]{2,1,0:T(8,128)S(1)}, f32[100,8,128]{2,1,0:T(8,128)S(1)}, u32[]{:S(2)}, u32[]{:S(2)}) collective-permute-start(f32[100,8,128]{2,1,0:T(8,128)S(1)} %get-tuple-element.22.own), channel_id=1, source_target_pairs={{0,1},{1,0},{2,3},{3,2},{4,5},{5,4},{6,7},{7,6},{8,9},{9,8},{10,11... | collective-permute-start | bytes 1228808 | tf_op jit(solution)/shard_map/ppermute | solution.py:478

commit v3 on v2

--- a/solution.py
+++ b/solution.py
@@ -16,9 +16,8 @@
 VMEM = pltpu.VMEM
 SLAB = (37, 8, 128)
 CROSS = (74, 8, 128)
-SMEM = pl.BlockSpec(memory_space=pltpu.SMEM)
 LOCAL = pl.BlockSpec(memory_space=VMEM)
-BATCHES = ((0, 1, 2, 3), (4, 5, 6, 7), (8, 9, 10), (11, 12))
+BATCHES = (((0, 1, 2, 3), (4, 5, 6, 7)), ((8, 9, 10), (11, 12)))
 FAR = pl.BlockSpec(memory_space=pltpu.HBM)
 
 
@@ -35,37 +34,22 @@
     return jnp.where(lane == 0, 0.0, WZ), jnp.where(lane == 127, 0.0, WZ)
 
 
-def pack_kernel(side, vec_in, cond_in, points_in, tiles, cond, padded, first, second, vec, points, sems):
-    copies = [
-        pltpu.make_async_copy(src, dst, sems.at[n])
-        for n, (src, dst) in enumerate(
-            ((vec_in, vec), (cond_in, cond), (points_in, points))
-        )
-    ]
-    for copy in copies:
-        copy.start()
-    even = side[0]
-    copies[2].wait()
+def pack_kernel(tiles, cond, points, padded, first, second):
+    even = 1 - lax.axis_index("gy") % 2
     padded[...] = jnp.full((64, 128), -1.0, F32)
     padded[:, 0:16] = points[...].astype(F32)
-    copies[1].wait()
-    for out, up in ((first, even == 1), (second, even == 0)):
+    for out, up in ((first, even), (second, 1 - even)):
         for x in range(8):
             half = x % 2 * 4
-            out[32 + x // 2, half : half + 4, :] = jnp.where(up, cond[x, 4:8, :], cond[x, 0:4, :])
-        out[36] = jnp.where(up, padded[pl.ds(7, 8, stride=8), :], padded[pl.ds(0, 8, stride=8), :])
-    copies[0].wait()
-    for x in range(8):
-        row = [vec[pl.ds(x * 8 + y, 8, stride=64), :] for y in range(8)]
-        for y in range(8):
-            tiles[x * 8 + y] = row[y]
-        for y in range(4):
-            first[x * 4 + y] = jnp.where(even == 1, row[y + 4], row[y])
-            second[x * 4 + y] = jnp.where(even == 1, row[y], row[y + 4])
-
-
-def cross_kernel(side, tiles, cond, padded, got1, got2, first, second):
-    y_even, x_even = side[0] == 1, side[1]
+            out[32 + x // 2, half : half + 4, :] = jnp.where(up == 1, cond[x, 4:8, :], cond[x, 0:4, :])
+            for y in range(4):
+                out[x * 4 + y] = tiles[x * 8 + y + 4 * up]
+        ends = padded[pl.ds(0, 8, stride=8), :], padded[pl.ds(7, 8, stride=8), :]
+        out[36] = jnp.where(up == 1, ends[1], ends[0])
+
+
+def cross_kernel(tiles, cond, padded, got1, got2, first, second):
+    y_even, x_even = lax.axis_index("gy") % 2 == 0, 1 - lax.axis_index("gx") % 2
 
     def low(*at):
         return jnp.where(y_even, got2[at], got1[at])
@@ -96,11 +80,11 @@
 
 
 def sweep_kernel(
-    side, tiles, cond, padded, got1, got2, cross1, cross2,
-    field, k_out, e_out, c_out,
+    tiles, cond, padded, got1, got2, cross1, cross2,
+    field_a, field_b, k_out, e_out, c_out,
     u0, u1, kk, kz, hh, h4, rk, ee,
 ):
-    y_even, x_even = side[0] == 1, side[1] == 1
+    y_even, x_even = lax.axis_index("gy") % 2 == 0, lax.axis_index("gx") % 2 == 0
 
     def ylow(*at):
         return jnp.where(y_even, got2[at], got1[at])
@@ -171,7 +155,7 @@
                 write(x, y, a * src[x, y] + b * w)
             return carry
 
-        lax.fori_loop(first, first + count, step, 0, unroll=2)
+        lax.fori_loop(first, first + count, step, 0, unroll=count)
 
     def to_u1(x, y, value):
         u1[x, y] = value
@@ -182,7 +166,7 @@
     sweep(u0, 1, 14, to_u1)
     sweep(u1, 2, 12, to_u0)
 
-    def step(x, carry):
+    def last(x, write):
         hx, h4x, rx = hh[x], h4[x], rk[x]
         s = [u0[x - 1, y] + u0[x, y] + u0[x + 1, y] for y in range(2, 14)]
         for j in range(10):
@@ -192,10 +176,31 @@
             a = jnp.broadcast_to(h4x[y : y + 1, :], (8, 128))
             b = jnp.broadcast_to(hx[y : y + 1, :], (8, 128))
             r = jnp.broadcast_to(rx[y : y + 1, :], (8, 128))
-            field[(x - 3) * 10 + j] = (a * u0[x, y] + b * w) * r
+            write(j, (a * u0[x, y] + b * w) * r)
+
+    def low_rows(x, carry):
+        def write(j, value):
+            field_a[(x - 3) * 10 + j] = value
+
+        last(x, write)
         return carry
 
-    lax.fori_loop(3, 13, step, 0, unroll=2)
+    def high_rows(x, carry):
+        def write(j, value):
+            field_b[(x - 3) * 10 + j - 64] = value
+
+        last(x, write)
+        return carry
+
+    def middle(j, value):
+        if j < 4:
+            field_a[60 + j] = value
+        else:
+            field_b[j - 4] = value
+
+    lax.fori_loop(3, 9, low_rows, 0, unroll=6)
+    last(9, middle)
+    lax.fori_loop(10, 13, high_rows, 0, unroll=3)
 
     for x in range(10):
         k_out[x * 10 : x * 10 + 10, :] = kk[x + 3, 3:13, :]
@@ -231,12 +236,45 @@
     return jnp.take_along_axis(t, index, axis=1)
 
 
-def galerkin_kernel(
-    vert, own, other, k10, e10, onehot, index,
-    interp, coarse,
-    rs, ps, l1s, l2s, r1s, r2s, e1s, e2s, ts, mids, cs, sems,
-):
-    first = vert[0] == 0
+KEPT = slice(800, 1024)
+
+
+def early_kernel(*refs):
+    galerkin(0, refs[:6], (), refs[6:8], refs[8:14], refs[14:])
+
+
+def late_kernel(*refs):
+    galerkin(1, refs[:6], refs[6:14], refs[14:16], (), refs[16:])
+
+
+def galerkin(part, sources, given, outputs, kept, scratch):
+    own, other, k10, e10, onehot, index = sources
+    if part == 0:
+        ps, cs = outputs
+        rs, l1s, l2s, r1s, r2s, e1s, e2s, ts, mids = scratch
+    else:
+        interp, coarse = outputs
+        rs, l1s, l2s, r1s, r2s, e1s, e2s, ts, mids, ps, cs, sems = scratch
+        early_ps, early_cs = given[0], given[1]
+
+    def interp_copy(x, source):
+        return pltpu.make_async_copy(
+            source.at[pl.ds((x * 10 + 1) * 16, 128), :],
+            interp.at[pl.ds((x - 1) * 128, 128), :],
+            sems.at[x - 1],
+        )
+
+    def coarse_copy(x, source):
+        return pltpu.make_async_copy(source.at[x - 1], coarse.at[x - 1], sems.at[7 + x])
+
+    copies = []
+    if part == 1:
+        copies += [interp_copy(x, early_ps) for x in range(1, 6)]
+        copies += [coarse_copy(x, early_cs) for x in range(1, 5)]
+        for copy in copies:
+            copy.start()
+    groups = range(8) if part == 0 else range(8, 13)
+    first = lax.axis_index("vert") == 0
     lane16 = iota((16, 128), 1)
     sub16 = iota((16, 128), 0)
     lane8 = iota((8, 128), 1)
@@ -254,8 +292,9 @@
 
     def fields(g):
         n = 8 if g < 12 else 4
-        a = own[8 * g : 8 * g + n].reshape(n * 8, 128)
-        b = other[8 * g : 8 * g + n].reshape(n * 8, 128)
+        at = slice(8 * (g - groups[0]), 8 * (g - groups[0]) + n)
+        a = own[at].reshape(n * 8, 128)
+        b = other[at].reshape(n * 8, 128)
         fa, fb = jnp.where(first, a, b), jnp.where(first, b, a)
         if n == 8:
             return halves(jnp.concatenate([fa, fb], axis=0))
@@ -292,28 +331,36 @@
         system = gram + jnp.where(on_diag, ridge, 0.0)
         return [system[0:8, :], system[8:16, :]]
 
-    systems = []
-    for batch in BATCHES:
+    systems = {}
+    for batch in BATCHES[part]:
         pairs = [fields(g) for g in batch]
         spots = [values(g, pair) for g, pair in zip(batch, pairs)]
         found = [rights(pair, spot) for pair, spot in zip(pairs, spots)]
         for g, right in zip(batch, found):
             rs[rows_of(g), :] = right
-        systems += [system_of(g, right) for g, right in zip(batch, found)]
-
-    for k in range(16):
+        systems.update({g: system_of(g, right) for g, right in zip(batch, found)})
+
+    for k in range(0, 16, 2):
         half, row = k // 8, k % 8
-        at_k = lane8 % 16 == k
+        at_0, at_1 = lane8 % 16 == k, lane8 % 16 == k + 1
         spot = block8 * 16 + k
-        for s in systems:
-            pivot_row = jnp.broadcast_to(s[half][row : row + 1, :], (8, 128))
-            scale = 1.0 / gather_lanes(pivot_row, spot)
-            r = jnp.where(at_k, 1.0, pivot_row) * scale
+
+        def row_of(t, row):
+            return jnp.broadcast_to(t[row : row + 1, :], (8, 128))
+
+        for s in systems.values():
+            f0 = [gather_lanes(t, spot) for t in s]
+            f1 = [gather_lanes(t, spot + 1) for t in s]
+            a, b, c = row_of(f0[half], row), row_of(f1[half], row), row_of(f1[half], row + 1)
+            inverse = 1.0 / (a * c - b * b)
+            p0, p1 = row_of(s[half], row), row_of(s[half], row + 1)
+            p0 = jnp.where(at_0, 1.0, jnp.where(at_1, 0.0, p0))
+            p1 = jnp.where(at_1, 1.0, jnp.where(at_0, 0.0, p1))
+            r0, r1 = (c * p0 - b * p1) * inverse, (a * p1 - b * p0) * inverse
             for t in range(2):
-                factor = gather_lanes(s[t], spot)
-                new = jnp.where(at_k, 0.0, s[t]) - factor * r
+                new = jnp.where(at_0 | at_1, 0.0, s[t]) - f0[t] * r0 - f1[t] * r1
                 if t == half:
-                    new = jnp.where(sub8 == row, r, new)
+                    new = jnp.where(sub8 == row, r0, jnp.where(sub8 == row + 1, r1, new))
                 s[t] = new
 
     def weights(g):
@@ -342,24 +389,33 @@
         r1s[rows_of(g), :], r2s[rows_of(g), :] = halves(image)
         e1s[rows_of(g), :], e2s[rows_of(g), :] = halves(spread(e10, g) * p - image)
 
-    for batch in BATCHES:
+    for batch in BATCHES[part]:
         found = [weights(g) for g in batch]
         for g, pair in zip(batch, found):
             finish(g, *pair)
 
-    interp_copies = [
-        pltpu.make_async_copy(
-            ps.at[pl.ds((x * 10 + 1) * 16, 128), :], interp.at[pl.ds((x - 1) * 128, 128), :],
-            sems.at[x - 1],
-        )
-        for x in range(1, 9)
-    ]
-    for copy in interp_copies:
-        copy.start()
+    moved = slice(KEPT.start + 160, KEPT.stop + 160)
+    pieces = ((l1s, moved), (l2s, moved), (r1s, KEPT), (r2s, KEPT), (e1s, KEPT), (e2s, KEPT))
+    if part == 0:
+        for to, (ref, at) in zip(kept, pieces):
+            to[...] = ref[at, :]
+    else:
+        for source, (ref, at) in zip(given[2:], pieces):
+            ref[at, :] = source[...]
+        ps[KEPT, :] = early_ps[KEPT, :]
+        cs[4, 0:6] = early_cs[4, 0:6]
+        late_copies = [interp_copy(x, ps) for x in range(6, 9)]
+        for copy in late_copies:
+            copy.start()
+        copies += late_copies
+
+    def wanted(x, source):
+        return 1 <= x <= 8 and (max(x, source) <= 5) == (part == 0)
 
     def multiply(x, slot):
         base = x * 160
-        low, high = max(x - 1, 1), min(x + 1, 8)
+        used = [n for n in range(x - 1, x + 2) if wanted(n, x)]
+        low, high = used[0], used[-1]
 
         def lefts(ref):
             return [ref[160 * n + 176 : 160 * n + 304, :] for n in range(low, high + 1)]
@@ -378,7 +434,7 @@
         ts[slot, at : at + 128 * (high - low + 1), :] = product_t(
             lhs, jnp.concatenate([q1, q2, q1], axis=1)
         )
-        if 1 <= x <= 8:
+        if wanted(x, x):
             order = (8, 7, 6, 5, 4, 3, 2, 1)
             q1, q2 = stacked(e1s, order), stacked(e2s, order)
             at = 128 * (x - low)
@@ -387,7 +443,7 @@
     def arrange(x, slot):
         for side in range(3):
             ox = 1 - side
-            if not 1 <= x - ox <= 8:
+            if not wanted(x - ox, x):
                 continue
             for o in range(3):
                 first_turn, last_turn = min(o, 1), max(o - 1, 0)
@@ -412,30 +468,27 @@
                     merged = pltpu.roll(merged, 16 * last_turn, 1, stride=16, stride_axis=0)
                     cs[x - ox - 1, 3 * (ox + 1) + o, :, half * 128 : half * 128 + 128] = scale * merged
 
-    coarse_copies = [
-        pltpu.make_async_copy(cs.at[x], coarse.at[x], sems.at[8 + x]) for x in range(8)
-    ]
-    multiply(0, 0)
-    for x in range(1, 11):
-        if x < 10:
-            multiply(x, x % 2)
-        arrange(x - 1, (x - 1) % 2)
-        if x > 2:
-            coarse_copies[x - 3].start()
-    for copy in interp_copies:
+    order = range(6) if part == 0 else range(5, 10)
+    multiply(order[0], 0)
+    for n, x in enumerate(order):
+        if n + 1 < len(order):
+            multiply(x + 1, (n + 1) % 2)
+        arrange(x, n % 2)
+        if part == 1 and x > 5:
+            copies.append(coarse_copy(x - 1, cs))
+            copies[-1].start()
+    for copy in copies:
         copy.wait()
-    for copy in coarse_copies:
-        copy.wait()
-
-
-def call(kernel, outs, scratch=(), specs=None, args=(), flops=0, outs_at=LOCAL):
+
+
+def call(kernel, outs, scratch=(), specs=None, args=(), flops=0, outs_at=None):
     shapes = [jax.ShapeDtypeStruct(*o) for o in outs]
     moved = sum(a.size * 4 for a in args) + sum(4 * s.size for s in shapes)
     return pl.pallas_call(
         kernel,
         out_shape=shapes,
-        in_specs=specs,
-        out_specs=[outs_at] * len(outs),
+        in_specs=specs or [LOCAL] * len(args),
+        out_specs=outs_at or [LOCAL] * len(outs),
         scratch_shapes=list(scratch),
         compiler_params=pltpu.CompilerParams(vmem_limit_bytes=48 << 20),
         cost_estimate=pl.CostEstimate(flops=flops, bytes_accessed=moved, transcendentals=0),
@@ -449,47 +502,52 @@
 
 
 def body(vectors, conductivity, c_points):
-    side = jnp.stack([1 - lax.axis_index("gy") % 2, 1 - lax.axis_index("gx") % 2]).astype(jnp.int32)
-    tiles, cond, padded, send1, send2 = call(
+    tiles = jnp.transpose(vectors, (1, 2, 0, 3)).reshape(64, 8, 128)
+    padded, send1, send2 = call(
         pack_kernel,
-        [((64, 8, 128), F32), ((8, 8, 128), F32), ((64, 128), F32), (SLAB, F32), (SLAB, F32)],
-        [VMEM((512, 128), F32), VMEM((64, 16), jnp.int32), pltpu.SemaphoreType.DMA((3,))],
-        specs=[SMEM] + [FAR] * 3,
-        args=(side, vectors.reshape(512, 128), conductivity, c_points.reshape(64, 16)),
-    )
+        [((64, 128), F32), (SLAB, F32), (SLAB, F32)],
+        args=(tiles, conductivity, c_points.reshape(64, 16)),
+    )
+    cond = conductivity
     got2 = swapped(send2, "gy", 1)
     got1 = swapped(send1, "gy", 0)
     send1, send2 = call(
         cross_kernel,
         [(CROSS, F32)] * 2,
-        specs=[SMEM] + [LOCAL] * 5,
-        args=(side, tiles, cond, padded, got1, got2),
+        args=(tiles, cond, padded, got1, got2),
     )
     cross2 = swapped(send2, "gx", 1)
     cross1 = swapped(send1, "gx", 0)
     rows = ((104, 128), F32)
-    field, k10, e10, c10 = call(
+    field_a, field_b, k10, e10, c10 = call(
         sweep_kernel,
-        [((100, 8, 128), F32), rows, rows, rows],
+        [((64, 8, 128), F32), ((36, 8, 128), F32), rows, rows, rows],
         [VMEM((16, 16, 8, 128), F32)] * 2 + [VMEM((16, 16, 128), F32)] * 6,
-        specs=[SMEM] + [LOCAL] * 7,
-        args=(side, tiles, cond, padded, got1, got2, cross1, cross2),
-    )
-    other = lax.ppermute(field, "vert", [(0, 1), (1, 0)])
+        args=(tiles, cond, padded, got1, got2, cross1, cross2),
+    )
+    pair = [(0, 1), (1, 0)]
+    other_a = lax.ppermute(field_a, "vert", pair)
+    other_b = lax.ppermute(field_b, "vert", pair)
     points = c10[:, 0:16].astype(jnp.int32)
     onehot = (points.reshape(1664, 1) == jnp.arange(128, dtype=jnp.int32)).astype(BF16)
     index = jnp.pad(points.reshape(13, 128), ((0, 3), (0, 0)))
-    vert = lax.axis_index("vert").astype(jnp.int32).reshape(1)
-    strips = [VMEM((1664, 128), F32)] * 2 + [VMEM((1920, 128), BF16)] * 2 + [VMEM((1664, 128), BF16)] * 4
+    scratch = (
+        [VMEM((1664, 128), F32)] + [VMEM((1920, 128), BF16)] * 2 + [VMEM((1664, 128), BF16)] * 4
+        + [VMEM((2, 384, 256), F32), VMEM((2, 128, 128), F32)]
+    )
+    late_scratch = [
+        VMEM((1664, 128), F32), VMEM((8, 9, 8, 256), F32), pltpu.SemaphoreType.DMA((16,)),
+    ]
+    kept = [((1024, 128), F32), ((5, 9, 8, 256), F32)] + [((224, 128), BF16)] * 6
+    kept = call(
+        early_kernel, kept, scratch, args=(field_a, other_a, k10, e10, onehot, index)
+    )
     interp, coarse = call(
-        galerkin_kernel,
+        late_kernel,
         [((1024, 128), F32), ((8, 9, 8, 256), F32)],
-        strips
-        + [VMEM((2, 384, 256), F32), VMEM((2, 128, 128), F32), VMEM((8, 9, 8, 256), F32)]
-        + [pltpu.SemaphoreType.DMA((16,))],
-        specs=[SMEM] + [LOCAL] * 6,
-        outs_at=FAR,
-        args=(vert, field, other, k10, e10, onehot, index),
+        scratch + late_scratch,
+        outs_at=[FAR] * 2,
+        args=(field_b, other_b, k10, e10, onehot, index, *kept),
     )
     return interp.reshape(8, 8, 16, 128), jnp.transpose(coarse, (0, 2, 1, 3))
 

time: 52.5 us -> 49.8 us (0.949)
  the two profiles are of different devices: /device:TPU:227 before, /device:TPU:377 now
where the time goes in v3:
time: 49.8 us; the launch traced here: 49.6 us
  waiting for transfers between devices  20.2 us (41%)
  starting transfers between devices  19 us (38%)
  Pallas kernels  8.04 us (16%)
  local copies, waits for them, and re-layouts  1.3 us (3%)
  between operations  0.76 us (2%)
    ppermute x4, starting transfers between devices, swapped(): return lax.ppermute(value, axis, low + [(j, i) for i, j in low])  12.2 us
    ppermute x4, waiting for transfers between devices, swapped(): return lax.ppermute(value, axis, low + [(j, i) for i, j in low])  11.7 us
    ppermute x1, waiting for transfers between devices, body(): other_a = lax.ppermute(field_a, 'vert', pair)  8.45 us
    pallas_call x5, Pallas kernels, call(): pl.pallas_call(kernel, out_shape=shapes, in_specs=specs or [LOCAL] * len(...  8.04 us
    ppermute x1, starting transfers between devices, body(): other_b = lax.ppermute(field_b, 'vert', pair)  4.64 us
    ppermute x1, starting transfers between devices, body(): other_a = lax.ppermute(field_a, 'vert', pair)  2.13 us
    transpose x1, local copies, waits for them, and re-layouts, body(): tiles = jnp.transpose(vectors, (1, 2, 0, 3)).reshape(64, 8, 128)  1.12 us
  transfers between devices with their start and end apart: 6, of which 4 were waited for; matrix products, arithmetic and copies ran while one was open for 1% of the time, Pallas kernels for 7%

profile of v3, /device:TPU:377, one launch (start us, length us, event | category | flops | bytes accessed | tf_op | source)
XLA Modules:
  0.0 49.6 jit_solution(16744085945792928846)
XLA Ops:
  0.6 0.0 copy-start
  0.6 0.0 copy-start.1
  0.6 1.1 %copy.6 = f32[8,8,8,128]{3,2,1,0:T(8,128)S(1)} copy(f32[8,8,8,128]{3,1,0,2:T(8,128)} %bitcast.9) | data formatting | bytes 524288 | tf_op jit(solution)/shard_map/transpose | solution.py:505
  1.8 0.0 copy-done
  1.8 0.0 copy-done.1
  1.8 2.4 %collective-permute-start = (f32[37,8,128]{2,1,0:T(8,128)S(1)}, f32[37,8,128]{2,1,0:T(8,128)S(1)}, u32[]{:S(2)}, u32[]{:S(2)}) collective-permute-start(f32[37,8,128]{2,1,0:T(8,128)S(1)} %get-tuple-element.23), channel_id=1, source_target_pairs={{0,2},{4,6},{8,10},{12,14},{2,0},{6,4},{10,8},{14,12},{1,3},{5,7},... | collective-permute-start | bytes 454664 | tf_op jit(solution)/shard_map/ppermute | solution.py:501
  4.2 3.6 %collective-permute-start.1 = (f32[37,8,128]{2,1,0:T(8,128)S(1)}, f32[37,8,128]{2,1,0:T(8,128)S(1)}, u32[]{:S(2)}, u32[]{:S(2)}) collective-permute-start(f32[37,8,128]{2,1,0:T(8,128)S(1)} %get-tuple-element.24), channel_id=1, source_target_pairs={{2,4},{6,8},{10,12},{4,2},{8,6},{12,10},{3,5},{7,9},{11,13},{5,3},... | collective-permute-start | bytes 454664 | tf_op jit(solution)/shard_map/ppermute | solution.py:501
  7.8 0.7 %collective-permute-done.got1 = f32[37,8,128]{2,1,0:T(8,128)S(1)} collective-permute-done((f32[37,8,128]{2,1,0:T(8,128)S(1)}, f32[37,8,128]{2,1,0:T(8,128)S(1)}, u32[]{:S(2)}, u32[]{:S(2)}) %collective-permute-start) | collective-permute-done | bytes 151584 | tf_op jit(solution)/shard_map/ppermute | solution.py:501
  8.6 4.2 %collective-permute-done.1.got2 = f32[37,8,128]{2,1,0:T(8,128)S(1)} collective-permute-done((f32[37,8,128]{2,1,0:T(8,128)S(1)}, f32[37,8,128]{2,1,0:T(8,128)S(1)}, u32[]{:S(2)}, u32[]{:S(2)}) %collective-permute-start.1) | collective-permute-done | bytes 151584 | tf_op jit(solution)/shard_map/ppermute | solution.py:501
  12.8 0.1 shard_map.51
  12.8 3.7 %collective-permute-start.2 = (f32[74,8,128]{2,1,0:T(8,128)S(1)}, f32[74,8,128]{2,1,0:T(8,128)S(1)}, u32[]{:S(2)}, u32[]{:S(2)}) collective-permute-start(f32[74,8,128]{2,1,0:T(8,128)S(1)} %get-tuple-element.25), channel_id=1, source_target_pairs={{0,16},{32,48},{64,80},{96,112},{128,144},{160,176},{192,208},{224... | collective-permute-start | bytes 909320 | tf_op jit(solution)/shard_map/ppermute | solution.py:501
  16.5 2.5 %collective-permute-start.3 = (f32[74,8,128]{2,1,0:T(8,128)S(1)}, f32[74,8,128]{2,1,0:T(8,128)S(1)}, u32[]{:S(2)}, u32[]{:S(2)}) collective-permute-start(f32[74,8,128]{2,1,0:T(8,128)S(1)} %get-tuple-element.26), channel_id=1, source_target_pairs={{16,32},{48,64},{80,96},{112,128},{144,160},{176,192},{208,224},{2... | collective-permute-start | bytes 909320 | tf_op jit(solution)/shard_map/ppermute | solution.py:501
  19.1 0.0 collective-permute-done.2.cross1
  19.1 6.8 %collective-permute-done.3.cross2 = f32[74,8,128]{2,1,0:T(8,128)S(1)} collective-permute-done((f32[74,8,128]{2,1,0:T(8,128)S(1)}, f32[74,8,128]{2,1,0:T(8,128)S(1)}, u32[]{:S(2)}, u32[]{:S(2)}) %collective-permute-start.3) | collective-permute-done | bytes 303136 | tf_op jit(solution)/shard_map/ppermute | solution.py:501
  25.9 1.2 %shard_map.52 = (f32[64,8,128]{2,1,0:T(8,128)S(1)}, f32[36,8,128]{2,1,0:T(8,128)S(1)}, f32[104,128]{1,0:T(8,128)S(1)}, f32[104,128]{1,0:T(8,128)S(1)}, f32[104,128]{1,0:T(8,128)S(1)}) custom-call(f32[64,8,128]{2,1,0:T(8,128)S(1)} %bitcast.7, f32[8,8,128]{2,1,0:T(8,128)S(1)} %copy-done, f32[64,128]{1,0:T(8,128)S(1)} %get-tuple-element.22.padded, ...), custom_call_target="tpu_custom_call" | custom-call | bytes 1806336 | tf_op jit(solution)/shard_map/pallas_call | solution.py:487
  27.2 0.1 eq.15
  27.2 4.6 %collective-permute-start.4 = (f32[36,8,128]{2,1,0:T(8,128)S(1)}, f32[36,8,128]{2,1,0:T(8,128)S(1)}, u32[]{:S(2)}, u32[]{:S(2)}) collective-permute-start(f32[36,8,128]{2,1,0:T(8,128)S(1)} %get-tuple-element.27.refs_0_), channel_id=1, source_target_pairs={{0,1},{1,0},{2,3},{3,2},{4,5},{5,4},{6,7},{7,6},{8,9},{9,8},{10,11... | collective-permute-start | bytes 442376 | tf_op jit(solution)/shard_map/ppermute | solution.py:530
  31.9 2.1 %collective-permute-start.5 = (f32[64,8,128]{2,1,0:T(8,128)S(1)}, f32[64,8,128]{2,1,0:T(8,128)S(1)}, u32[]{:S(2)}, u32[]{:S(2)}) collective-permute-start(f32[64,8,128]{2,1,0:T(8,128)S(1)} %get-tuple-element.31.refs_0_), channel_id=1, source_target_pairs={{0,1},{1,0},{2,3},{3,2},{4,5},{5,4},{6,7},{7,6},{8,9},{9,8},{10,11... | collective-permute-start | bytes 786440 | tf_op jit(solution)/shard_map/ppermute | solution.py:529
  34.0 0.3 fusion.refs_4_
  34.3 0.1 reshape.20
  34.4 8.4 %collective-permute-done.5.refs_1_ = f32[64,8,128]{2,1,0:T(8,128)S(1)} collective-permute-done((f32[64,8,128]{2,1,0:T(8,128)S(1)}, f32[64,8,128]{2,1,0:T(8,128)S(1)}, u32[]{:S(2)}, u32[]{:S(2)}) %collective-permute-start.5) | collective-permute-done | bytes 262176 | tf_op jit(solution)/shard_map/ppermute | solution.py:529
  42.9 3.3 %shard_map.53 = (f32[1024,128]{1,0:T(8,128)S(1)}, f32[5,9,8,256]{3,2,1,0:T(8,128)S(1)}, bf16[224,128]{1,0:T(8,128)(2,1)S(1)}, bf16[224,128]{1,0:T(8,128)(2,1)S(1...) custom-call(f32[64,8,128]{2,1,0:T(8,128)S(1)} %get-tuple-element.31., ...), custom_call_target="tpu_custom_call" | custom-call | bytes 3072000 | tf_op jit(solution)/shard_map/pallas_call | solution.py:487
  46.1 0.0 collective-permute-done.4.refs_1_
  46.1 3.4 %shard_map.54 = (f32[1024,128]{1,0:T(8,128)}, f32[8,9,8,256]{3,2,1,0:T(8,128)}) custom-call(f32[36,8,128]{2,1,0:T(8,128)S(1)} %get-tuple-element.27.refs_0_, f32[36,8,128]{2,1,0:T(8,128)S(1)} %collective-permute-done.4.refs_1_, f32[104,128]{1,0:T(8,128)S(1)} %get-tuple-element.28.refs_2_, f32[104,128]{1,0:T(8,128)S(1)} %get-tuple-element.29.refs_3_, ...), custom_call_target="tpu_custom_call" | custom-call | bytes 3956736 | tf_op jit(solution)/shard_map/pallas_call | solution.py:487
  (3 shorter events, 0.1 us)
Async XLA Ops:
  0.6 1.1 %copy-start = (f32[8,8,128]{2,1,0:T(8,128)S(1)}, f32[8,8,128]{2,1,0:T(8,128)}, u32[]{:S(2)}) copy-start(f32[8,8,128]{2,1,0:T(8,128)} %cond.5) | copy-start | bytes 98308
  0.6 1.1 %copy-start.1 = (s32[8,8,16]{2,1,0:T(8,128)S(1)}, s32[8,8,16]{2,1,0:T(8,128)}, u32[]{:S(2)}) copy-start(s32[8,8,16]{2,1,0:T(8,128)} %param.5) | copy-start | bytes 12292
  1.8 6.7 %collective-permute-start = (f32[37,8,128]{2,1,0:T(8,128)S(1)}, f32[37,8,128]{2,1,0:T(8,128)S(1)}, u32[]{:S(2)}, u32[]{:S(2)}) collective-permute-start(f32[37,8,128]{2,1,0:T(8,128)S(1)} %get-tuple-element.23), channel_id=1, source_target_pairs={{0,2},{4,6},{8,10},{12,14},{2,0},{6,4},{10,8},{14,12},{1,3},{5,7},... | collective-permute-start | bytes 454664 | tf_op jit(solution)/shard_map/ppermute | solution.py:501
  4.2 8.5 %collective-permute-start.1 = (f32[37,8,128]{2,1,0:T(8,128)S(1)}, f32[37,8,128]{2,1,0:T(8,128)S(1)}, u32[]{:S(2)}, u32[]{:S(2)}) collective-permute-start(f32[37,8,128]{2,1,0:T(8,128)S(1)} %get-tuple-element.24), channel_id=1, source_target_pairs={{2,4},{6,8},{10,12},{4,2},{8,6},{12,10},{3,5},{7,9},{11,13},{5,3},... | collective-permute-start | bytes 454664 | tf_op jit(solution)/shard_map/ppermute | solution.py:501
  12.8 6.3 %collective-permute-start.2 = (f32[74,8,128]{2,1,0:T(8,128)S(1)}, f32[74,8,128]{2,1,0:T(8,128)S(1)}, u32[]{:S(2)}, u32[]{:S(2)}) collective-permute-start(f32[74,8,128]{2,1,0:T(8,128)S(1)} %get-tuple-element.25), channel_id=1, source_target_pairs={{0,16},{32,48},{64,80},{96,112},{128,144},{160,176},{192,208},{224... | collective-permute-start | bytes 909320 | tf_op jit(solution)/shard_map/ppermute | solution.py:501
  16.5 9.3 %collective-permute-start.3 = (f32[74,8,128]{2,1,0:T(8,128)S(1)}, f32[74,8,128]{2,1,0:T(8,128)S(1)}, u32[]{:S(2)}, u32[]{:S(2)}) collective-permute-start(f32[74,8,128]{2,1,0:T(8,128)S(1)} %get-tuple-element.26), channel_id=1, source_target_pairs={{16,32},{48,64},{80,96},{112,128},{144,160},{176,192},{208,224},{2... | collective-permute-start | bytes 909320 | tf_op jit(solution)/shard_map/ppermute | solution.py:501
  27.2 18.9 %collective-permute-start.4 = (f32[36,8,128]{2,1,0:T(8,128)S(1)}, f32[36,8,128]{2,1,0:T(8,128)S(1)}, u32[]{:S(2)}, u32[]{:S(2)}) collective-permute-start(f32[36,8,128]{2,1,0:T(8,128)S(1)} %get-tuple-element.27.refs_0_), channel_id=1, source_target_pairs={{0,1},{1,0},{2,3},{3,2},{4,5},{5,4},{6,7},{7,6},{8,9},{9,8},{10,11... | collective-permute-start | bytes 442376 | tf_op jit(solution)/shard_map/ppermute | solution.py:530
  31.9 11.0 %collective-permute-start.5 = (f32[64,8,128]{2,1,0:T(8,128)S(1)}, f32[64,8,128]{2,1,0:T(8,128)S(1)}, u32[]{:S(2)}, u32[]{:S(2)}) collective-permute-start(f32[64,8,128]{2,1,0:T(8,128)S(1)} %get-tuple-element.31.refs_0_), channel_id=1, source_target_pairs={{0,1},{1,0},{2,3},{3,2},{4,5},{5,4},{6,7},{7,6},{8,9},{9,8},{10,11... | collective-permute-start | bytes 786440 | tf_op jit(solution)/shard_map/ppermute | solution.py:529

commit v4 on v3

--- a/solution.py
+++ b/solution.py
@@ -34,7 +34,7 @@
     return jnp.where(lane == 0, 0.0, WZ), jnp.where(lane == 127, 0.0, WZ)
 
 
-def pack_kernel(tiles, cond, points, padded, first, second):
+def pack_kernel(tiles, cond, points, padded, first, second, beside):
     even = 1 - lax.axis_index("gy") % 2
     padded[...] = jnp.full((64, 128), -1.0, F32)
     padded[:, 0:16] = points[...].astype(F32)
@@ -46,10 +46,23 @@
                 out[x * 4 + y] = tiles[x * 8 + y + 4 * up]
         ends = padded[pl.ds(0, 8, stride=8), :], padded[pl.ds(7, 8, stride=8), :]
         out[36] = jnp.where(up == 1, ends[1], ends[0])
-
-
-def cross_kernel(tiles, cond, padded, got1, got2, first, second):
-    y_even, x_even = lax.axis_index("gy") % 2 == 0, 1 - lax.axis_index("gx") % 2
+    own_part(beside, 0, lax.axis_index("gx") % 2, tiles, cond, padded)
+
+
+def own_part(out, start, up, tiles, cond, padded):
+    for x in range(4):
+        for y in range(8):
+            out[start + x * 8 + y] = tiles[(x + 4 * up) * 8 + y]
+        out[start + 32 + x] = cond[x + 4 * up]
+    out[start + 36] = jnp.where(up == 1, padded[56:64, :], padded[0:8, :])
+
+
+def middle_kernel(tiles, cond, padded, first):
+    own_part(first, 0, 1 - lax.axis_index("gx") % 2, tiles, cond, padded)
+
+
+def cross_kernel(filled, got1, got2, first, second):
+    y_even, up = lax.axis_index("gy") % 2 == 0, lax.axis_index("gx") % 2
 
     def low(*at):
         return jnp.where(y_even, got2[at], got1[at])
@@ -57,30 +70,23 @@
     def high(*at):
         return jnp.where(y_even, got1[at], got2[at])
 
-    for out, up in ((first, x_even), (second, 1 - x_even)):
-        for xx in range(4):
-            x = xx + 4 * up
+    for out, start, up in ((first, 37, 1 - up), (second, 0, up)):
+        for x in range(4):
             for y in range(4):
-                out[xx * 16 + y] = low(x * 4 + y)
-                out[xx * 16 + 12 + y] = high(x * 4 + y)
-            for y in range(8):
-                out[xx * 16 + 4 + y] = tiles[x * 8 + y]
-            rows = slice(xx % 2 * 4, xx % 2 * 4 + 4)
-            k = cond[x]
-            out[64 + 2 * xx, 0:4, :] = low(32 + xx // 2 + 2 * up, rows)
-            out[64 + 2 * xx, 4:8, :] = k[0:4, :]
-            out[65 + 2 * xx, 0:4, :] = k[4:8, :]
-            out[65 + 2 * xx, 4:8, :] = high(32 + xx // 2 + 2 * up, rows)
-        top = up == 1
-        out[73] = jnp.zeros((8, 128), F32)
-        out[72, 0:1, :] = jnp.where(top, low(36, slice(7, 8)), low(36, slice(0, 1)))
-        out[72, 1:8, :] = jnp.where(top, padded[56:63, :], padded[0:7, :])
-        out[73, 0:1, :] = jnp.where(top, padded[63:64, :], padded[7:8, :])
-        out[73, 1:2, :] = jnp.where(top, high(36, slice(7, 8)), high(36, slice(0, 1)))
+                out[start + x * 8 + y] = low((x + 4 * up) * 4 + y)
+                out[start + x * 8 + 4 + y] = high((x + 4 * up) * 4 + y)
+            rows = slice(x % 2 * 4, x % 2 * 4 + 4)
+            out[start + 32 + x, 0:4, :] = low(32 + x // 2 + 2 * up, rows)
+            out[start + 32 + x, 4:8, :] = high(32 + x // 2 + 2 * up, rows)
+        out[start + 36] = jnp.zeros((8, 128), F32)
+        for row, source in ((0, low), (1, high)):
+            out[start + 36, row : row + 1, :] = jnp.where(
+                up == 1, source(36, slice(7, 8)), source(36, slice(0, 1))
+            )
 
 
 def sweep_kernel(
-    tiles, cond, padded, got1, got2, cross1, cross2,
+    tiles, cond, padded, got1, got2, near, far_own, far_corner,
     field_a, field_b, k_out, e_out, c_out,
     u0, u1, kk, kz, hh, h4, rk, ee,
 ):
@@ -92,11 +98,13 @@
     def yhigh(*at):
         return jnp.where(y_even, got1[at], got2[at])
 
-    def xlow(*at):
-        return jnp.where(x_even, cross2[at], cross1[at])
-
-    def xhigh(*at):
-        return jnp.where(x_even, cross1[at], cross2[at])
+    def own(is_low, *at):
+        a, b = far_own[at], near[at]
+        return jnp.where(x_even, a, b) if is_low else jnp.where(x_even, b, a)
+
+    def corner(is_low, n, *at):
+        a, b = far_corner[(n, *at)], near[(n + 37, *at)]
+        return jnp.where(x_even, a, b) if is_low else jnp.where(x_even, b, a)
 
     for x in range(16):
         if 4 <= x < 12:
@@ -105,9 +113,10 @@
             kk[x, 4:12, :] = cond[x - 4]
             kk[x, 12:16, :] = yhigh(32 + (x - 4) // 2, rows)
         else:
-            source, xx = (xlow, x) if x < 4 else (xhigh, x - 12)
-            kk[x, 0:8, :] = source(64 + 2 * xx)
-            kk[x, 8:16, :] = source(65 + 2 * xx)
+            n = 32 + x % 4
+            kk[x, 0:4, :] = corner(x < 4, n, slice(0, 4))
+            kk[x, 4:12, :] = own(x < 4, n)
+            kk[x, 12:16, :] = corner(x < 4, n, slice(4, 8))
 
     low16, high16 = z_weights(16)
     for x in range(16):
@@ -125,10 +134,11 @@
 
     for x in range(16):
         for y in range(16):
-            if x < 4:
-                t = xlow(x * 16 + y)
-            elif x >= 12:
-                t = xhigh((x - 12) * 16 + y)
+            if not 4 <= x < 12:
+                if 4 <= y < 12:
+                    t = own(x < 4, x % 4 * 8 + y - 4)
+                else:
+                    t = corner(x < 4, x % 4 * 8 + (y if y < 4 else y - 8))
             elif y < 4:
                 t = ylow((x - 4) * 4 + y)
             elif y >= 12:
@@ -211,9 +221,9 @@
             c_out[row + 1 : row + 9, :] = padded[(x - 1) * 8 : (x - 1) * 8 + 8, :]
             c_out[row + 9 : row + 10, :] = yhigh(36, slice(x - 1, x))
         else:
-            source = xlow if x == 0 else xhigh
-            c_out[row : row + 8, :] = source(72)
-            c_out[row + 8 : row + 10, :] = source(73, slice(0, 2))
+            c_out[row : row + 1, :] = corner(x == 0, 36, slice(0, 1))
+            c_out[row + 1 : row + 9, :] = own(x == 0, 36)
+            c_out[row + 9 : row + 10, :] = corner(x == 0, 36, slice(1, 2))
     k_out[100:104, :] = jnp.zeros((4, 128), F32)
     e_out[100:104, :] = jnp.zeros((4, 128), F32)
     c_out[100:104, :] = jnp.full((4, 128), -1.0, F32)
@@ -481,7 +491,7 @@
         copy.wait()
 
 
-def call(kernel, outs, scratch=(), specs=None, args=(), flops=0, outs_at=None):
+def call(kernel, outs, scratch=(), specs=None, args=(), flops=0, outs_at=None, aliases=None):
     shapes = [jax.ShapeDtypeStruct(*o) for o in outs]
     moved = sum(a.size * 4 for a in args) + sum(4 * s.size for s in shapes)
     return pl.pallas_call(
@@ -490,6 +500,7 @@
         in_specs=specs or [LOCAL] * len(args),
         out_specs=outs_at or [LOCAL] * len(outs),
         scratch_shapes=list(scratch),
+        input_output_aliases=aliases or {},
         compiler_params=pltpu.CompilerParams(vmem_limit_bytes=48 << 20),
         cost_estimate=pl.CostEstimate(flops=flops, bytes_accessed=moved, transcendentals=0),
     )(*args)
@@ -503,27 +514,27 @@
 
 def body(vectors, conductivity, c_points):
     tiles = jnp.transpose(vectors, (1, 2, 0, 3)).reshape(64, 8, 128)
-    padded, send1, send2 = call(
+    cond = conductivity
+    padded, send1, send2, beside = call(
         pack_kernel,
-        [((64, 128), F32), (SLAB, F32), (SLAB, F32)],
-        args=(tiles, conductivity, c_points.reshape(64, 16)),
-    )
-    cond = conductivity
+        [((64, 128), F32), (SLAB, F32), (SLAB, F32), (SLAB, F32)],
+        args=(tiles, cond, c_points.reshape(64, 16)),
+    )
     got2 = swapped(send2, "gy", 1)
     got1 = swapped(send1, "gy", 0)
+    far_own = swapped(beside, "gx", 1)
+    (filled,) = call(middle_kernel, [(CROSS, F32)], args=(tiles, cond, padded))
     send1, send2 = call(
-        cross_kernel,
-        [(CROSS, F32)] * 2,
-        args=(tiles, cond, padded, got1, got2),
-    )
-    cross2 = swapped(send2, "gx", 1)
-    cross1 = swapped(send1, "gx", 0)
+        cross_kernel, [(CROSS, F32), (SLAB, F32)], args=(filled, got1, got2), aliases={0: 0}
+    )
+    far_corner = swapped(send2, "gx", 1)
+    near = swapped(send1, "gx", 0)
     rows = ((104, 128), F32)
     field_a, field_b, k10, e10, c10 = call(
         sweep_kernel,
         [((64, 8, 128), F32), ((36, 8, 128), F32), rows, rows, rows],
         [VMEM((16, 16, 8, 128), F32)] * 2 + [VMEM((16, 16, 128), F32)] * 6,
-        args=(tiles, cond, padded, got1, got2, cross1, cross2),
+        args=(tiles, cond, padded, got1, got2, near, far_own, far_corner),
     )
     pair = [(0, 1), (1, 0)]
     other_a = lax.ppermute(field_a, "vert", pair)

time: 49.8 us -> 51.5 us (1.034)
  starting transfers between devices: 19 us -> 23.3 us
  waiting for transfers between devices: 20.2 us -> 17.6 us
    ppermute x4 -> x5, starting transfers between devices: 12.2 us -> 16.5 us  [swapped(): return lax.ppermute(value, axis, low + [(j, i) for i, j in low])]
    ppermute x4 -> x5, waiting for transfers between devices: 11.7 us -> 8.37 us  [swapped(): return lax.ppermute(value, axis, low + [(j, i) for i, j in low])]
    ppermute x1, waiting for transfers between devices: 8.45 us -> 9.18 us  [body(): other_a = lax.ppermute(field_a, 'vert', pair)]
    pallas_call x5 -> x6, Pallas kernels: 8.04 us -> 8.03 us  [call(): pl.pallas_call(kernel, out_shape=shapes, in_specs=specs or [LOCAL] * len(...]
  transfers between devices with their start and end apart: 6 -> 7, of which waited for: 4 -> 5; matrix products, arithmetic and copies ran while one was open for 1% -> 1% of each run, Pallas kernels for 7% -> 6%
where the time goes in v4:
time: 51.5 us; the launch traced here: 51.2 us
  starting transfers between devices  23.3 us (45%)
  waiting for transfers between devices  17.6 us (34%)
  Pallas kernels  8.03 us (16%)
  local copies, waits for them, and re-layouts  1.3 us (3%)
  between operations  0.77 us (1%)
    ppermute x5, starting transfers between devices, swapped(): return lax.ppermute(value, axis, low + [(j, i) for i, j in low])  16.5 us
    ppermute x1, waiting for transfers between devices, body(): other_a = lax.ppermute(field_a, 'vert', pair)  9.18 us
    ppermute x5, waiting for transfers between devices, swapped(): return lax.ppermute(value, axis, low + [(j, i) for i, j in low])  8.37 us
    pallas_call x6, Pallas kernels, call(): pl.pallas_call(kernel, out_shape=shapes, in_specs=specs or [LOCAL] * len(...  8.03 us
    ppermute x1, starting transfers between devices, body(): other_b = lax.ppermute(field_b, 'vert', pair)  4.64 us
    ppermute x1, starting transfers between devices, body(): other_a = lax.ppermute(field_a, 'vert', pair)  2.13 us
    transpose x1, local copies, waits for them, and re-layouts, body(): tiles = jnp.transpose(vectors, (1, 2, 0, 3)).reshape(64, 8, 128)  1.12 us
  transfers between devices with their start and end apart: 7, of which 5 were waited for; matrix products, arithmetic and copies ran while one was open for 1% of the time, Pallas kernels for 6%

profile of v4, /device:TPU:377, one launch (start us, length us, event | category | flops | bytes accessed | tf_op | source)
XLA Modules:
  0.0 51.2 jit_solution(13057369163505658225)
XLA Ops:
  0.6 0.0 copy-start
  0.6 0.0 copy-start.1
  0.6 1.1 %copy.7 = f32[8,8,8,128]{3,2,1,0:T(8,128)S(1)} copy(f32[8,8,8,128]{3,1,0,2:T(8,128)} %bitcast.9) | data formatting | bytes 524288 | tf_op jit(solution)/shard_map/transpose | solution.py:516
  1.8 0.0 copy-done
  1.8 0.0 copy-done.1
  1.8 0.1 shard_map.50
  1.8 2.4 %collective-permute-start = (f32[37,8,128]{2,1,0:T(8,128)S(1)}, f32[37,8,128]{2,1,0:T(8,128)S(1)}, u32[]{:S(2)}, u32[]{:S(2)}) collective-permute-start(f32[37,8,128]{2,1,0:T(8,128)S(1)} %get-tuple-element.24), channel_id=1, source_target_pairs={{0,2},{4,6},{8,10},{12,14},{2,0},{6,4},{10,8},{14,12},{1,3},{5,7},... | collective-permute-start | bytes 454664 | tf_op jit(solution)/shard_map/ppermute | solution.py:512
  4.2 3.6 %collective-permute-start.1 = (f32[37,8,128]{2,1,0:T(8,128)S(1)}, f32[37,8,128]{2,1,0:T(8,128)S(1)}, u32[]{:S(2)}, u32[]{:S(2)}) collective-permute-start(f32[37,8,128]{2,1,0:T(8,128)S(1)} %get-tuple-element.25), channel_id=1, source_target_pairs={{2,4},{6,8},{10,12},{4,2},{8,6},{12,10},{3,5},{7,9},{11,13},{5,3},... | collective-permute-start | bytes 454664 | tf_op jit(solution)/shard_map/ppermute | solution.py:512
  7.9 0.7 %collective-permute-done.got1 = f32[37,8,128]{2,1,0:T(8,128)S(1)} collective-permute-done((f32[37,8,128]{2,1,0:T(8,128)S(1)}, f32[37,8,128]{2,1,0:T(8,128)S(1)}, u32[]{:S(2)}, u32[]{:S(2)}) %collective-permute-start) | collective-permute-done | bytes 151584 | tf_op jit(solution)/shard_map/ppermute | solution.py:512
  8.6 4.2 %collective-permute-done.1.got2 = f32[37,8,128]{2,1,0:T(8,128)S(1)} collective-permute-done((f32[37,8,128]{2,1,0:T(8,128)S(1)}, f32[37,8,128]{2,1,0:T(8,128)S(1)}, u32[]{:S(2)}, u32[]{:S(2)}) %collective-permute-start.1) | collective-permute-done | bytes 151584 | tf_op jit(solution)/shard_map/ppermute | solution.py:512
  12.8 3.7 %collective-permute-start.2 = (f32[74,8,128]{2,1,0:T(8,128)S(1)}, f32[74,8,128]{2,1,0:T(8,128)S(1)}, u32[]{:S(2)}, u32[]{:S(2)}) collective-permute-start(f32[74,8,128]{2,1,0:T(8,128)S(1)} %get-tuple-element.26), channel_id=1, source_target_pairs={{0,16},{32,48},{64,80},{96,112},{128,144},{160,176},{192,208},{224... | collective-permute-start | bytes 909320 | tf_op jit(solution)/shard_map/ppermute | solution.py:512
  16.5 2.5 %collective-permute-start.3 = (f32[37,8,128]{2,1,0:T(8,128)S(1)}, f32[37,8,128]{2,1,0:T(8,128)S(1)}, u32[]{:S(2)}, u32[]{:S(2)}) collective-permute-start(f32[37,8,128]{2,1,0:T(8,128)S(1)} %get-tuple-element.27), channel_id=1, source_target_pairs={{16,32},{48,64},{80,96},{112,128},{144,160},{176,192},{208,224},{2... | collective-permute-start | bytes 454664 | tf_op jit(solution)/shard_map/ppermute | solution.py:512
  19.1 4.2 %collective-permute-start.4 = (f32[37,8,128]{2,1,0:T(8,128)S(1)}, f32[37,8,128]{2,1,0:T(8,128)S(1)}, u32[]{:S(2)}, u32[]{:S(2)}) collective-permute-start(f32[37,8,128]{2,1,0:T(8,128)S(1)} %get-tuple-element.28), channel_id=1, source_target_pairs={{16,32},{48,64},{80,96},{112,128},{144,160},{176,192},{208,224},{2... | collective-permute-start | bytes 454664 | tf_op jit(solution)/shard_map/ppermute | solution.py:512
  23.3 0.9 %collective-permute-done.3.far_own = f32[37,8,128]{2,1,0:T(8,128)S(1)} collective-permute-done((f32[37,8,128]{2,1,0:T(8,128)S(1)}, f32[37,8,128]{2,1,0:T(8,128)S(1)}, u32[]{:S(2)}, u32[]{:S(2)}) %collective-permute-start.3) | collective-permute-done | bytes 151584 | tf_op jit(solution)/shard_map/ppermute | solution.py:512
  24.2 2.6 %collective-permute-done.4.far_corner = f32[37,8,128]{2,1,0:T(8,128)S(1)} collective-permute-done((f32[37,8,128]{2,1,0:T(8,128)S(1)}, f32[37,8,128]{2,1,0:T(8,128)S(1)}, u32[]{:S(2)}, u32[]{:S(2)}) %collective-permute-start.4) | collective-permute-done | bytes 151584 | tf_op jit(solution)/shard_map/ppermute | solution.py:512
  26.8 0.0 collective-permute-done.2.near
  26.8 1.2 %shard_map.53 = (f32[64,8,128]{2,1,0:T(8,128)S(1)}, f32[36,8,128]{2,1,0:T(8,128)S(1)}, f32[104,128]{1,0:T(8,128)S(1)}, f32[104,128]{1,0:T(8,128)S(1)}, f32[104,128]{1,0:T(8,128)S(1)}) custom-call(f32[64,8,128]{2,1,0:T(8,128)S(1)} %bitcast.7, f32[8,8,128]{2,1,0:T(8,128)S(1)} %copy-done, f32[64,128]{1,0:T(8,128)S(1)} %get-tuple-element.23.padded, ...), custom_call_target="tpu_custom_call" | custom-call | bytes 1806336 | tf_op jit(solution)/shard_map/pallas_call | solution.py:497
  28.1 0.1 eq.15
  28.1 4.6 %collective-permute-start.5 = (f32[36,8,128]{2,1,0:T(8,128)S(1)}, f32[36,8,128]{2,1,0:T(8,128)S(1)}, u32[]{:S(2)}, u32[]{:S(2)}) collective-permute-start(f32[36,8,128]{2,1,0:T(8,128)S(1)} %get-tuple-element.29.refs_0_), channel_id=1, source_target_pairs={{0,1},{1,0},{2,3},{3,2},{4,5},{5,4},{6,7},{7,6},{8,9},{9,8},{10,11... | collective-permute-start | bytes 442376 | tf_op jit(solution)/shard_map/ppermute | solution.py:541
  32.8 2.1 %collective-permute-start.6 = (f32[64,8,128]{2,1,0:T(8,128)S(1)}, f32[64,8,128]{2,1,0:T(8,128)S(1)}, u32[]{:S(2)}, u32[]{:S(2)}) collective-permute-start(f32[64,8,128]{2,1,0:T(8,128)S(1)} %get-tuple-element.33.refs_0_), channel_id=1, source_target_pairs={{0,1},{1,0},{2,3},{3,2},{4,5},{5,4},{6,7},{7,6},{8,9},{9,8},{10,11... | collective-permute-start | bytes 786440 | tf_op jit(solution)/shard_map/ppermute | solution.py:540
  34.9 0.3 fusion.refs_4_
  35.2 0.1 reshape.20
  35.3 9.2 %collective-permute-done.6.refs_1_ = f32[64,8,128]{2,1,0:T(8,128)S(1)} collective-permute-done((f32[64,8,128]{2,1,0:T(8,128)S(1)}, f32[64,8,128]{2,1,0:T(8,128)S(1)}, u32[]{:S(2)}, u32[]{:S(2)}) %collective-permute-start.6) | collective-permute-done | bytes 262176 | tf_op jit(solution)/shard_map/ppermute | solution.py:540
  44.5 3.3 %shard_map.54 = (f32[1024,128]{1,0:T(8,128)S(1)}, f32[5,9,8,256]{3,2,1,0:T(8,128)S(1)}, bf16[224,128]{1,0:T(8,128)(2,1)S(1)}, bf16[224,128]{1,0:T(8,128)(2,1)S(1...) custom-call(f32[64,8,128]{2,1,0:T(8,128)S(1)} %get-tuple-element.33., ...), custom_call_target="tpu_custom_call" | custom-call | bytes 3072000 | tf_op jit(solution)/shard_map/pallas_call | solution.py:497
  47.7 0.0 collective-permute-done.5.refs_1_
  47.8 3.4 %shard_map.55 = (f32[1024,128]{1,0:T(8,128)}, f32[8,9,8,256]{3,2,1,0:T(8,128)}) custom-call(f32[36,8,128]{2,1,0:T(8,128)S(1)} %get-tuple-element.29.refs_0_, f32[36,8,128]{2,1,0:T(8,128)S(1)} %collective-permute-done.5.refs_1_, f32[104,128]{1,0:T(8,128)S(1)} %get-tuple-element.30.refs_2_, f32[104,128]{1,0:T(8,128)S(1)} %get-tuple-element.31.refs_3_, ...), custom_call_target="tpu_custom_call" | custom-call | bytes 3956736 | tf_op jit(solution)/shard_map/pallas_call | solution.py:497
  (4 shorter events, 0.1 us)
Async XLA Ops:
  0.6 1.1 %copy-start = (f32[8,8,128]{2,1,0:T(8,128)S(1)}, f32[8,8,128]{2,1,0:T(8,128)}, u32[]{:S(2)}) copy-start(f32[8,8,128]{2,1,0:T(8,128)} %cond.5) | copy-start | bytes 98308
  0.6 1.1 %copy-start.1 = (s32[8,8,16]{2,1,0:T(8,128)S(1)}, s32[8,8,16]{2,1,0:T(8,128)}, u32[]{:S(2)}) copy-start(s32[8,8,16]{2,1,0:T(8,128)} %param.5) | copy-start | bytes 12292
  1.8 6.7 %collective-permute-start = (f32[37,8,128]{2,1,0:T(8,128)S(1)}, f32[37,8,128]{2,1,0:T(8,128)S(1)}, u32[]{:S(2)}, u32[]{:S(2)}) collective-permute-start(f32[37,8,128]{2,1,0:T(8,128)S(1)} %get-tuple-element.24), channel_id=1, source_target_pairs={{0,2},{4,6},{8,10},{12,14},{2,0},{6,4},{10,8},{14,12},{1,3},{5,7},... | collective-permute-start | bytes 454664 | tf_op jit(solution)/shard_map/ppermute | solution.py:512
  4.2 8.5 %collective-permute-start.1 = (f32[37,8,128]{2,1,0:T(8,128)S(1)}, f32[37,8,128]{2,1,0:T(8,128)S(1)}, u32[]{:S(2)}, u32[]{:S(2)}) collective-permute-start(f32[37,8,128]{2,1,0:T(8,128)S(1)} %get-tuple-element.25), channel_id=1, source_target_pairs={{2,4},{6,8},{10,12},{4,2},{8,6},{12,10},{3,5},{7,9},{11,13},{5,3},... | collective-permute-start | bytes 454664 | tf_op jit(solution)/shard_map/ppermute | solution.py:512
  12.8 14.0 %collective-permute-start.2 = (f32[74,8,128]{2,1,0:T(8,128)S(1)}, f32[74,8,128]{2,1,0:T(8,128)S(1)}, u32[]{:S(2)}, u32[]{:S(2)}) collective-permute-start(f32[74,8,128]{2,1,0:T(8,128)S(1)} %get-tuple-element.26), channel_id=1, source_target_pairs={{0,16},{32,48},{64,80},{96,112},{128,144},{160,176},{192,208},{224... | collective-permute-start | bytes 909320 | tf_op jit(solution)/shard_map/ppermute | solution.py:512
  16.5 7.7 %collective-permute-start.3 = (f32[37,8,128]{2,1,0:T(8,128)S(1)}, f32[37,8,128]{2,1,0:T(8,128)S(1)}, u32[]{:S(2)}, u32[]{:S(2)}) collective-permute-start(f32[37,8,128]{2,1,0:T(8,128)S(1)} %get-tuple-element.27), channel_id=1, source_target_pairs={{16,32},{48,64},{80,96},{112,128},{144,160},{176,192},{208,224},{2... | collective-permute-start | bytes 454664 | tf_op jit(solution)/shard_map/ppermute | solution.py:512
  19.1 7.7 %collective-permute-start.4 = (f32[37,8,128]{2,1,0:T(8,128)S(1)}, f32[37,8,128]{2,1,0:T(8,128)S(1)}, u32[]{:S(2)}, u32[]{:S(2)}) collective-permute-start(f32[37,8,128]{2,1,0:T(8,128)S(1)} %get-tuple-element.28), channel_id=1, source_target_pairs={{16,32},{48,64},{80,96},{112,128},{144,160},{176,192},{208,224},{2... | collective-permute-start | bytes 454664 | tf_op jit(solution)/shard_map/ppermute | solution.py:512
  28.1 19.6 %collective-permute-start.5 = (f32[36,8,128]{2,1,0:T(8,128)S(1)}, f32[36,8,128]{2,1,0:T(8,128)S(1)}, u32[]{:S(2)}, u32[]{:S(2)}) collective-permute-start(f32[36,8,128]{2,1,0:T(8,128)S(1)} %get-tuple-element.29.refs_0_), channel_id=1, source_target_pairs={{0,1},{1,0},{2,3},{3,2},{4,5},{5,4},{6,7},{7,6},{8,9},{9,8},{10,11... | collective-permute-start | bytes 442376 | tf_op jit(solution)/shard_map/ppermute | solution.py:541
  32.8 11.7 %collective-permute-start.6 = (f32[64,8,128]{2,1,0:T(8,128)S(1)}, f32[64,8,128]{2,1,0:T(8,128)S(1)}, u32[]{:S(2)}, u32[]{:S(2)}) collective-permute-start(f32[64,8,128]{2,1,0:T(8,128)S(1)} %get-tuple-element.33.refs_0_), channel_id=1, source_target_pairs={{0,1},{1,0},{2,3},{3,2},{4,5},{5,4},{6,7},{7,6},{8,9},{9,8},{10,11... | collective-permute-start | bytes 786440 | tf_op jit(solution)/shard_map/ppermute | solution.py:540

commit v5 on v4

--- a/solution.py
+++ b/solution.py
@@ -14,10 +14,14 @@
 F32 = jnp.float32
 BF16 = jnp.bfloat16
 VMEM = pltpu.VMEM
+GROUPS = 7
+COLUMNS = 8 * GROUPS
+FULL = COLUMNS // 10
+KEPT = slice(160 * (FULL - 1), 16 * COLUMNS)
+SIZE = KEPT.stop - KEPT.start
 SLAB = (37, 8, 128)
 CROSS = (74, 8, 128)
 LOCAL = pl.BlockSpec(memory_space=VMEM)
-BATCHES = (((0, 1, 2, 3), (4, 5, 6, 7)), ((8, 9, 10), (11, 12)))
 FAR = pl.BlockSpec(memory_space=pltpu.HBM)
 
 
@@ -188,29 +192,16 @@
             r = jnp.broadcast_to(rx[y : y + 1, :], (8, 128))
             write(j, (a * u0[x, y] + b * w) * r)
 
-    def low_rows(x, carry):
-        def write(j, value):
-            field_a[(x - 3) * 10 + j] = value
-
-        last(x, write)
-        return carry
-
-    def high_rows(x, carry):
-        def write(j, value):
-            field_b[(x - 3) * 10 + j - 64] = value
-
-        last(x, write)
-        return carry
-
-    def middle(j, value):
-        if j < 4:
-            field_a[60 + j] = value
-        else:
-            field_b[j - 4] = value
-
-    lax.fori_loop(3, 9, low_rows, 0, unroll=6)
-    last(9, middle)
-    lax.fori_loop(10, 13, high_rows, 0, unroll=3)
+    for x in range(10):
+
+        def write(j, value, x=x):
+            column = x * 10 + j
+            if column < COLUMNS:
+                field_a[column] = value
+            else:
+                field_b[column - COLUMNS] = value
+
+        last(x + 3, write)
 
     for x in range(10):
         k_out[x * 10 : x * 10 + 10, :] = kk[x + 3, 3:13, :]
@@ -246,9 +237,6 @@
     return jnp.take_along_axis(t, index, axis=1)
 
 
-KEPT = slice(800, 1024)
-
-
 def early_kernel(*refs):
     galerkin(0, refs[:6], (), refs[6:8], refs[8:14], refs[14:])
 
@@ -279,11 +267,12 @@
 
     copies = []
     if part == 1:
-        copies += [interp_copy(x, early_ps) for x in range(1, 6)]
-        copies += [coarse_copy(x, early_cs) for x in range(1, 5)]
+        copies += [interp_copy(x, early_ps) for x in range(1, FULL)]
+        copies += [coarse_copy(x, early_cs) for x in range(1, FULL - 1)]
         for copy in copies:
             copy.start()
-    groups = range(8) if part == 0 else range(8, 13)
+    groups = range(GROUPS) if part == 0 else range(GROUPS, 13)
+    batches = [groups[n : n + 4] for n in range(0, len(groups), 4)]
     first = lax.axis_index("vert") == 0
     lane16 = iota((16, 128), 1)
     sub16 = iota((16, 128), 0)
@@ -342,7 +331,7 @@
         return [system[0:8, :], system[8:16, :]]
 
     systems = {}
-    for batch in BATCHES[part]:
+    for batch in batches:
         pairs = [fields(g) for g in batch]
         spots = [values(g, pair) for g, pair in zip(batch, pairs)]
         found = [rights(pair, spot) for pair, spot in zip(pairs, spots)]
@@ -399,7 +388,7 @@
         r1s[rows_of(g), :], r2s[rows_of(g), :] = halves(image)
         e1s[rows_of(g), :], e2s[rows_of(g), :] = halves(spread(e10, g) * p - image)
 
-    for batch in BATCHES[part]:
+    for batch in batches:
         found = [weights(g) for g in batch]
         for g, pair in zip(batch, found):
             finish(g, *pair)
@@ -413,14 +402,14 @@
         for source, (ref, at) in zip(given[2:], pieces):
             ref[at, :] = source[...]
         ps[KEPT, :] = early_ps[KEPT, :]
-        cs[4, 0:6] = early_cs[4, 0:6]
-        late_copies = [interp_copy(x, ps) for x in range(6, 9)]
+        cs[FULL - 2, 0:6] = early_cs[FULL - 2, 0:6]
+        late_copies = [interp_copy(x, ps) for x in range(FULL, 9)]
         for copy in late_copies:
             copy.start()
         copies += late_copies
 
     def wanted(x, source):
-        return 1 <= x <= 8 and (max(x, source) <= 5) == (part == 0)
+        return 1 <= x <= 8 and (max(x, source) < FULL) == (part == 0)
 
     def multiply(x, slot):
         base = x * 160
@@ -478,13 +467,13 @@
                     merged = pltpu.roll(merged, 16 * last_turn, 1, stride=16, stride_axis=0)
                     cs[x - ox - 1, 3 * (ox + 1) + o, :, half * 128 : half * 128 + 128] = scale * merged
 
-    order = range(6) if part == 0 else range(5, 10)
+    order = range(FULL) if part == 0 else range(FULL - 1, 10)
     multiply(order[0], 0)
     for n, x in enumerate(order):
         if n + 1 < len(order):
             multiply(x + 1, (n + 1) % 2)
         arrange(x, n % 2)
-        if part == 1 and x > 5:
+        if part == 1 and x >= FULL:
             copies.append(coarse_copy(x - 1, cs))
             copies[-1].start()
     for copy in copies:
@@ -532,7 +521,7 @@
     rows = ((104, 128), F32)
     field_a, field_b, k10, e10, c10 = call(
         sweep_kernel,
-        [((64, 8, 128), F32), ((36, 8, 128), F32), rows, rows, rows],
+        [((COLUMNS, 8, 128), F32), ((100 - COLUMNS, 8, 128), F32), rows, rows, rows],
         [VMEM((16, 16, 8, 128), F32)] * 2 + [VMEM((16, 16, 128), F32)] * 6,
         args=(tiles, cond, padded, got1, got2, near, far_own, far_corner),
     )
@@ -549,7 +538,7 @@
     late_scratch = [
         VMEM((1664, 128), F32), VMEM((8, 9, 8, 256), F32), pltpu.SemaphoreType.DMA((16,)),
     ]
-    kept = [((1024, 128), F32), ((5, 9, 8, 256), F32)] + [((224, 128), BF16)] * 6
+    kept = [((16 * COLUMNS, 128), F32), ((FULL - 1, 9, 8, 256), F32)] + [((SIZE, 128), BF16)] * 6
     kept = call(
         early_kernel, kept, scratch, args=(field_a, other_a, k10, e10, onehot, index)
     )

time: 51.5 us -> 50.7 us (0.984)
  waiting for transfers between devices: 17.6 us -> 16.9 us
    ppermute x1, waiting for transfers between devices: 9.18 us -> 8.48 us  [body(): other_a = lax.ppermute(field_a, 'vert', pair)]
where the time goes in v5:
time: 50.7 us; the launch traced here: 50.5 us
  starting transfers between devices  23.3 us (46%)
  waiting for transfers between devices  16.9 us (33%)
  Pallas kernels  8 us (16%)
  local copies, waits for them, and re-layouts  1.3 us (3%)
  between operations  0.77 us (2%)
    ppermute x5, starting transfers between devices, swapped(): return lax.ppermute(value, axis, low + [(j, i) for i, j in low])  16.5 us
    ppermute x1, waiting for transfers between devices, body(): other_a = lax.ppermute(field_a, 'vert', pair)  8.48 us
    ppermute x5, waiting for transfers between devices, swapped(): return lax.ppermute(value, axis, low + [(j, i) for i, j in low])  8.37 us
    pallas_call x6, Pallas kernels, call(): pl.pallas_call(kernel, out_shape=shapes, in_specs=specs or [LOCAL] * len(...  8 us
    ppermute x1, starting transfers between devices, body(): other_b = lax.ppermute(field_b, 'vert', pair)  4.64 us
    ppermute x1, starting transfers between devices, body(): other_a = lax.ppermute(field_a, 'vert', pair)  2.13 us
    transpose x1, local copies, waits for them, and re-layouts, body(): tiles = jnp.transpose(vectors, (1, 2, 0, 3)).reshape(64, 8, 128)  1.12 us
  transfers between devices with their start and end apart: 7, of which 5 were waited for; matrix products, arithmetic and copies ran while one was open for 1% of the time, Pallas kernels for 6%

profile of v5, /device:TPU:377, one launch (start us, length us, event | category | flops | bytes accessed | tf_op | source)
XLA Modules:
  0.0 50.5 jit_solution(13672078314615593175)
XLA Ops:
  0.6 0.0 copy-start
  0.6 0.0 copy-start.1
  0.6 1.1 %copy.7 = f32[8,8,8,128]{3,2,1,0:T(8,128)S(1)} copy(f32[8,8,8,128]{3,1,0,2:T(8,128)} %bitcast.9) | data formatting | bytes 524288 | tf_op jit(solution)/shard_map/transpose | solution.py:505
  1.8 0.0 copy-done
  1.8 0.0 copy-done.1
  1.8 0.1 shard_map.50
  1.8 2.4 %collective-permute-start = (f32[37,8,128]{2,1,0:T(8,128)S(1)}, f32[37,8,128]{2,1,0:T(8,128)S(1)}, u32[]{:S(2)}, u32[]{:S(2)}) collective-permute-start(f32[37,8,128]{2,1,0:T(8,128)S(1)} %get-tuple-element.24), channel_id=1, source_target_pairs={{0,2},{4,6},{8,10},{12,14},{2,0},{6,4},{10,8},{14,12},{1,3},{5,7},... | collective-permute-start | bytes 454664 | tf_op jit(solution)/shard_map/ppermute | solution.py:501
  4.2 3.6 %collective-permute-start.1 = (f32[37,8,128]{2,1,0:T(8,128)S(1)}, f32[37,8,128]{2,1,0:T(8,128)S(1)}, u32[]{:S(2)}, u32[]{:S(2)}) collective-permute-start(f32[37,8,128]{2,1,0:T(8,128)S(1)} %get-tuple-element.25), channel_id=1, source_target_pairs={{2,4},{6,8},{10,12},{4,2},{8,6},{12,10},{3,5},{7,9},{11,13},{5,3},... | collective-permute-start | bytes 454664 | tf_op jit(solution)/shard_map/ppermute | solution.py:501
  7.9 0.7 %collective-permute-done.got1 = f32[37,8,128]{2,1,0:T(8,128)S(1)} collective-permute-done((f32[37,8,128]{2,1,0:T(8,128)S(1)}, f32[37,8,128]{2,1,0:T(8,128)S(1)}, u32[]{:S(2)}, u32[]{:S(2)}) %collective-permute-start) | collective-permute-done | bytes 151584 | tf_op jit(solution)/shard_map/ppermute | solution.py:501
  8.6 4.2 %collective-permute-done.1.got2 = f32[37,8,128]{2,1,0:T(8,128)S(1)} collective-permute-done((f32[37,8,128]{2,1,0:T(8,128)S(1)}, f32[37,8,128]{2,1,0:T(8,128)S(1)}, u32[]{:S(2)}, u32[]{:S(2)}) %collective-permute-start.1) | collective-permute-done | bytes 151584 | tf_op jit(solution)/shard_map/ppermute | solution.py:501
  12.8 3.7 %collective-permute-start.2 = (f32[74,8,128]{2,1,0:T(8,128)S(1)}, f32[74,8,128]{2,1,0:T(8,128)S(1)}, u32[]{:S(2)}, u32[]{:S(2)}) collective-permute-start(f32[74,8,128]{2,1,0:T(8,128)S(1)} %get-tuple-element.26), channel_id=1, source_target_pairs={{0,16},{32,48},{64,80},{96,112},{128,144},{160,176},{192,208},{224... | collective-permute-start | bytes 909320 | tf_op jit(solution)/shard_map/ppermute | solution.py:501
  16.5 2.5 %collective-permute-start.3 = (f32[37,8,128]{2,1,0:T(8,128)S(1)}, f32[37,8,128]{2,1,0:T(8,128)S(1)}, u32[]{:S(2)}, u32[]{:S(2)}) collective-permute-start(f32[37,8,128]{2,1,0:T(8,128)S(1)} %get-tuple-element.27), channel_id=1, source_target_pairs={{16,32},{48,64},{80,96},{112,128},{144,160},{176,192},{208,224},{2... | collective-permute-start | bytes 454664 | tf_op jit(solution)/shard_map/ppermute | solution.py:501
  19.1 4.2 %collective-permute-start.4 = (f32[37,8,128]{2,1,0:T(8,128)S(1)}, f32[37,8,128]{2,1,0:T(8,128)S(1)}, u32[]{:S(2)}, u32[]{:S(2)}) collective-permute-start(f32[37,8,128]{2,1,0:T(8,128)S(1)} %get-tuple-element.28), channel_id=1, source_target_pairs={{16,32},{48,64},{80,96},{112,128},{144,160},{176,192},{208,224},{2... | collective-permute-start | bytes 454664 | tf_op jit(solution)/shard_map/ppermute | solution.py:501
  23.3 0.9 %collective-permute-done.3.far_own = f32[37,8,128]{2,1,0:T(8,128)S(1)} collective-permute-done((f32[37,8,128]{2,1,0:T(8,128)S(1)}, f32[37,8,128]{2,1,0:T(8,128)S(1)}, u32[]{:S(2)}, u32[]{:S(2)}) %collective-permute-start.3) | collective-permute-done | bytes 151584 | tf_op jit(solution)/shard_map/ppermute | solution.py:501
  24.2 2.6 %collective-permute-done.4.far_corner = f32[37,8,128]{2,1,0:T(8,128)S(1)} collective-permute-done((f32[37,8,128]{2,1,0:T(8,128)S(1)}, f32[37,8,128]{2,1,0:T(8,128)S(1)}, u32[]{:S(2)}, u32[]{:S(2)}) %collective-permute-start.4) | collective-permute-done | bytes 151584 | tf_op jit(solution)/shard_map/ppermute | solution.py:501
  26.8 0.0 collective-permute-done.2.near
  26.8 1.2 %shard_map.53 = (f32[56,8,128]{2,1,0:T(8,128)S(1)}, f32[44,8,128]{2,1,0:T(8,128)S(1)}, f32[104,128]{1,0:T(8,128)S(1)}, f32[104,128]{1,0:T(8,128)S(1)}, f32[104,128]{1,0:T(8,128)S(1)}) custom-call(f32[64,8,128]{2,1,0:T(8,128)S(1)} %bitcast.7, f32[8,8,128]{2,1,0:T(8,128)S(1)} %copy-done, f32[64,128]{1,0:T(8,128)S(1)} %get-tuple-element.23.padded, ...), custom_call_target="tpu_custom_call" | custom-call | bytes 1806336 | tf_op jit(solution)/shard_map/pallas_call | solution.py:486
  28.1 0.1 eq.15
  28.1 4.6 %collective-permute-start.5 = (f32[44,8,128]{2,1,0:T(8,128)S(1)}, f32[44,8,128]{2,1,0:T(8,128)S(1)}, u32[]{:S(2)}, u32[]{:S(2)}) collective-permute-start(f32[44,8,128]{2,1,0:T(8,128)S(1)} %get-tuple-element.29.refs_0_), channel_id=1, source_target_pairs={{0,1},{1,0},{2,3},{3,2},{4,5},{5,4},{6,7},{7,6},{8,9},{9,8},{10,11... | collective-permute-start | bytes 540680 | tf_op jit(solution)/shard_map/ppermute | solution.py:530
  32.8 2.1 %collective-permute-start.6 = (f32[56,8,128]{2,1,0:T(8,128)S(1)}, f32[56,8,128]{2,1,0:T(8,128)S(1)}, u32[]{:S(2)}, u32[]{:S(2)}) collective-permute-start(f32[56,8,128]{2,1,0:T(8,128)S(1)} %get-tuple-element.33.refs_0_), channel_id=1, source_target_pairs={{0,1},{1,0},{2,3},{3,2},{4,5},{5,4},{6,7},{7,6},{8,9},{9,8},{10,11... | collective-permute-start | bytes 688136 | tf_op jit(solution)/shard_map/ppermute | solution.py:529
  34.9 0.3 fusion.refs_4_
  35.2 0.1 reshape.20
  35.3 8.5 %collective-permute-done.6.refs_1_ = f32[56,8,128]{2,1,0:T(8,128)S(1)} collective-permute-done((f32[56,8,128]{2,1,0:T(8,128)S(1)}, f32[56,8,128]{2,1,0:T(8,128)S(1)}, u32[]{:S(2)}, u32[]{:S(2)}) %collective-permute-start.6) | collective-permute-done | bytes 229408 | tf_op jit(solution)/shard_map/ppermute | solution.py:529
  43.8 3.0 %shard_map.54 = (f32[896,128]{1,0:T(8,128)S(1)}, f32[4,9,8,256]{3,2,1,0:T(8,128)S(1)}, bf16[256,128]{1,0:T(8,128)(2,1)S(1)}, bf16[256,128]{1,0:T(8,128)(2,1)S(1)...) custom-call(f32[56,8,128]{2,1,0:T(8,128)S(1)} %get-tuple-element.33., ...), custom_call_target="tpu_custom_call" | custom-call | bytes 2965504 | tf_op jit(solution)/shard_map/pallas_call | solution.py:486
  46.8 0.0 collective-permute-done.5.refs_1_
  46.8 3.7 %shard_map.55 = (f32[1024,128]{1,0:T(8,128)}, f32[8,9,8,256]{3,2,1,0:T(8,128)}) custom-call(f32[44,8,128]{2,1,0:T(8,128)S(1)} %get-tuple-element.29.refs_0_, f32[44,8,128]{2,1,0:T(8,128)S(1)} %collective-permute-done.5.refs_1_, f32[104,128]{1,0:T(8,128)S(1)} %get-tuple-element.30.refs_2_, f32[104,128]{1,0:T(8,128)S(1)} %get-tuple-element.31.refs_3_, ...), custom_call_target="tpu_custom_call" | custom-call | bytes 3981312 | tf_op jit(solution)/shard_map/pallas_call | solution.py:486
  (4 shorter events, 0.1 us)
Async XLA Ops:
  0.6 1.1 %copy-start = (f32[8,8,128]{2,1,0:T(8,128)S(1)}, f32[8,8,128]{2,1,0:T(8,128)}, u32[]{:S(2)}) copy-start(f32[8,8,128]{2,1,0:T(8,128)} %cond.5) | copy-start | bytes 98308
  0.6 1.1 %copy-start.1 = (s32[8,8,16]{2,1,0:T(8,128)S(1)}, s32[8,8,16]{2,1,0:T(8,128)}, u32[]{:S(2)}) copy-start(s32[8,8,16]{2,1,0:T(8,128)} %param.5) | copy-start | bytes 12292
  1.8 6.7 %collective-permute-start = (f32[37,8,128]{2,1,0:T(8,128)S(1)}, f32[37,8,128]{2,1,0:T(8,128)S(1)}, u32[]{:S(2)}, u32[]{:S(2)}) collective-permute-start(f32[37,8,128]{2,1,0:T(8,128)S(1)} %get-tuple-element.24), channel_id=1, source_target_pairs={{0,2},{4,6},{8,10},{12,14},{2,0},{6,4},{10,8},{14,12},{1,3},{5,7},... | collective-permute-start | bytes 454664 | tf_op jit(solution)/shard_map/ppermute | solution.py:501
  4.2 8.5 %collective-permute-start.1 = (f32[37,8,128]{2,1,0:T(8,128)S(1)}, f32[37,8,128]{2,1,0:T(8,128)S(1)}, u32[]{:S(2)}, u32[]{:S(2)}) collective-permute-start(f32[37,8,128]{2,1,0:T(8,128)S(1)} %get-tuple-element.25), channel_id=1, source_target_pairs={{2,4},{6,8},{10,12},{4,2},{8,6},{12,10},{3,5},{7,9},{11,13},{5,3},... | collective-permute-start | bytes 454664 | tf_op jit(solution)/shard_map/ppermute | solution.py:501
  12.8 14.0 %collective-permute-start.2 = (f32[74,8,128]{2,1,0:T(8,128)S(1)}, f32[74,8,128]{2,1,0:T(8,128)S(1)}, u32[]{:S(2)}, u32[]{:S(2)}) collective-permute-start(f32[74,8,128]{2,1,0:T(8,128)S(1)} %get-tuple-element.26), channel_id=1, source_target_pairs={{0,16},{32,48},{64,80},{96,112},{128,144},{160,176},{192,208},{224... | collective-permute-start | bytes 909320 | tf_op jit(solution)/shard_map/ppermute | solution.py:501
  16.5 7.7 %collective-permute-start.3 = (f32[37,8,128]{2,1,0:T(8,128)S(1)}, f32[37,8,128]{2,1,0:T(8,128)S(1)}, u32[]{:S(2)}, u32[]{:S(2)}) collective-permute-start(f32[37,8,128]{2,1,0:T(8,128)S(1)} %get-tuple-element.27), channel_id=1, source_target_pairs={{16,32},{48,64},{80,96},{112,128},{144,160},{176,192},{208,224},{2... | collective-permute-start | bytes 454664 | tf_op jit(solution)/shard_map/ppermute | solution.py:501
  19.1 7.7 %collective-permute-start.4 = (f32[37,8,128]{2,1,0:T(8,128)S(1)}, f32[37,8,128]{2,1,0:T(8,128)S(1)}, u32[]{:S(2)}, u32[]{:S(2)}) collective-permute-start(f32[37,8,128]{2,1,0:T(8,128)S(1)} %get-tuple-element.28), channel_id=1, source_target_pairs={{16,32},{48,64},{80,96},{112,128},{144,160},{176,192},{208,224},{2... | collective-permute-start | bytes 454664 | tf_op jit(solution)/shard_map/ppermute | solution.py:501
  28.1 18.7 %collective-permute-start.5 = (f32[44,8,128]{2,1,0:T(8,128)S(1)}, f32[44,8,128]{2,1,0:T(8,128)S(1)}, u32[]{:S(2)}, u32[]{:S(2)}) collective-permute-start(f32[44,8,128]{2,1,0:T(8,128)S(1)} %get-tuple-element.29.refs_0_), channel_id=1, source_target_pairs={{0,1},{1,0},{2,3},{3,2},{4,5},{5,4},{6,7},{7,6},{8,9},{9,8},{10,11... | collective-permute-start | bytes 540680 | tf_op jit(solution)/shard_map/ppermute | solution.py:530
  32.8 11.0 %collective-permute-start.6 = (f32[56,8,128]{2,1,0:T(8,128)S(1)}, f32[56,8,128]{2,1,0:T(8,128)S(1)}, u32[]{:S(2)}, u32[]{:S(2)}) collective-permute-start(f32[56,8,128]{2,1,0:T(8,128)S(1)} %get-tuple-element.33.refs_0_), channel_id=1, source_target_pairs={{0,1},{1,0},{2,3},{3,2},{4,5},{5,4},{6,7},{7,6},{8,9},{9,8},{10,11... | collective-permute-start | bytes 688136 | tf_op jit(solution)/shard_map/ppermute | solution.py:529
